TPU v7x, 256 devices: a whole 4x4x8 slice. The times are simulated.
256 devices in a mesh: gx: 32 (over z_hi, x, y), gy: 8 (over z_lo, core).
Axes of the slice: x: 4, y: 4, z: 8 (z_hi: 2, z_lo: 4; z = z_hi * 4 + z_lo), core: 2. Of those that a mesh axis runs over, the one named last changes fastest.
Arguments:
- stress: float32 [6, 16, 2048, 1024], P(None, None, 'gx', 'gy'), may hold values from -6 to 6
- velocity: float32 [3, 16, 2048, 1024], P(None, None, 'gx', 'gy'), may hold values from -6 to 6
- material: int32 [16, 2048, 1024], P(None, 'gx', 'gy'), may hold values from 0 to 2
- layer_kind: int32 [16], replicated, may hold values from 0 to 2
- buoyancy: float32 [3], replicated, may hold values from 0.05 to 0.3
- lame_first: float32 [3], replicated, may hold values from 0.05 to 0.3
- shear_modulus: float32 [3], replicated, may hold values from 0.05 to 0.2
- piezo: float32 [3], replicated, may hold values from 0.5 to 2
- permit_lateral: float32 [3], replicated, may hold values from 0.5 to 4
- permit_normal: float32 [3], replicated, may hold values from 0.5 to 4
Outputs:
- stress_next: float32 [6, 16, 2048, 1024], P(None, None, 'gx', 'gy')
- velocity_next: float32 [3, 16, 2048, 1024], P(None, None, 'gx', 'gy')
- potential_modes: float32 [2, 16, 1024, 2048], P(None, None, ('gx', 'gy'))
Inputs may be any that keep to these rules, and one draw needn't show every extreme that they name: `layer_kind`: material codes of the layers, as for cells.
All inputs are finite; a program needn't handle non-finite values.
Results may differ from a plain program's by a relative error of at most 0.000076.
Values sent between devices are 32-bit elements; how exact they have to be, the bound alone decides.
No kernel may reach another device: no remote copies, remote signals or barrier semaphores. Data moves between devices by JAX's collectives and lax.ppermute only.
A program may use at most 192 MiB of HBM per device.

v0:
```python
import math

import jax
import jax.numpy as jnp
from jax import lax
from jax.sharding import PartitionSpec as P


def extended(block, sides, width):
    for axis, dim in sides:
        count = lax.axis_size(axis)
        forward = [(i, i + 1) for i in range(count - 1)]
        backward = [(target, source) for source, target in forward]
        low = lax.ppermute(
            lax.slice_in_dim(block, block.shape[dim] - width, None, axis=dim), axis, forward
        )
        high = lax.ppermute(lax.slice_in_dim(block, 0, width, axis=dim), axis, backward)
        block = jnp.concatenate([low, block, high], axis=dim)
    return block


def lookup(codes, table):
    result = jnp.zeros(codes.shape, jnp.float32)
    for material_no in range(3):
        result = result + jnp.where(codes == material_no, table[material_no], 0.0)
    return result


def centre(padded):
    return padded[..., 1:-1, 1:-1]


def x_plus(padded):
    return padded[..., 2:, 1:-1] - padded[..., 1:-1, 1:-1]


def x_minus(padded):
    return padded[..., 1:-1, 1:-1] - padded[..., :-2, 1:-1]


def y_plus(padded):
    return padded[..., 1:-1, 2:] - padded[..., 1:-1, 1:-1]


def y_minus(padded):
    return padded[..., 1:-1, 1:-1] - padded[..., 1:-1, :-2]


def z_plus(inner):
    upper = jnp.concatenate([inner[1:], jnp.zeros_like(inner[:1])], axis=0)
    return upper - inner


def z_minus(inner):
    lower = jnp.concatenate([jnp.zeros_like(inner[:1]), inner[:-1]], axis=0)
    return inner - lower


def advance_velocity(stress_pad, veloc, buoy_field):
    new_x = veloc[0] + buoy_field * (
        x_plus(stress_pad[0]) + y_minus(stress_pad[3]) + z_minus(centre(stress_pad[4]))
    )
    new_y = veloc[1] + buoy_field * (
        x_minus(stress_pad[3]) + y_plus(stress_pad[1]) + z_minus(centre(stress_pad[5]))
    )
    new_z = veloc[2] + buoy_field * (
        x_minus(stress_pad[4]) + y_minus(stress_pad[5]) + z_plus(centre(stress_pad[2]))
    )
    return jnp.stack([new_x, new_y, new_z])


def advance_stress(stress, veloc_pad, lame_field, shear_field):
    strain_x = x_minus(veloc_pad[0])
    strain_y = y_minus(veloc_pad[1])
    strain_z = z_minus(centre(veloc_pad[2]))
    diverge = strain_x + strain_y + strain_z
    new_xx = stress[0] + lame_field * diverge + 2.0 * shear_field * strain_x
    new_yy = stress[1] + lame_field * diverge + 2.0 * shear_field * strain_y
    new_zz = stress[2] + lame_field * diverge + 2.0 * shear_field * strain_z
    new_xy = stress[3] + shear_field * (y_plus(veloc_pad[0]) + x_plus(veloc_pad[1]))
    new_xz = stress[4] + shear_field * (z_plus(centre(veloc_pad[0])) + x_plus(veloc_pad[2]))
    new_yz = stress[5] + shear_field * (z_plus(centre(veloc_pad[1])) + y_plus(veloc_pad[2]))
    return jnp.stack([new_xx, new_yy, new_zz, new_xy, new_xz, new_yz])


def couplings(layer_kind, permit_lateral, permit_normal):
    lateral = lookup(layer_kind, permit_lateral)
    normal = lookup(layer_kind, permit_normal)
    couple = jnp.concatenate([normal[:1], 0.5 * (normal[:-1] + normal[1:]), normal[-1:]])
    return (lateral, couple)


def solve_layers(rhs, wave, lateral, couple):
    layers = rhs.shape[1]
    factors = []
    carries = []
    for layer_no in range(layers):
        pivot = couple[layer_no] + couple[layer_no + 1] + wave * lateral[layer_no]
        if layer_no > 0:
            pivot = pivot - couple[layer_no] * factors[-1]
            carry = (rhs[:, layer_no] + couple[layer_no] * carries[-1]) / pivot
        else:
            carry = rhs[:, layer_no] / pivot
        factors.append(couple[layer_no + 1] / pivot)
        carries.append(carry)
    solved = [carries[-1]]
    for layer_no in range(layers - 2, -1, -1):
        solved.append(carries[layer_no] + factors[layer_no] * solved[-1])
    return jnp.stack(solved[::-1], axis=1)


def phase_table(first, second, length):
    product = first[:, None] * second[None, :] % length
    angle = product.astype(jnp.float32) * (2.0 * math.pi / length)
    scale = 1.0 / math.sqrt(length)
    return (jnp.cos(angle) * scale, jnp.sin(angle) * scale)


def per_device(
    stress,
    velocity,
    material,
    layer_kind,
    buoyancy,
    lame_first,
    shear_modulus,
    piezo,
    permit_lateral,
    permit_normal,
):
    buoy_field = lookup(material, buoyancy)
    lame_field = lookup(material, lame_first)
    shear_field = lookup(material, shear_modulus)
    stress_pad = extended(stress, (("gx", 2), ("gy", 3)), 1)
    velocity_next = advance_velocity(stress_pad, velocity, buoy_field)
    veloc_pad = extended(velocity_next, (("gx", 2), ("gy", 3)), 1)
    stress_next = advance_stress(stress, veloc_pad, lame_field, shear_field)
    charge = lookup(material, piezo) * (stress_next[4] + stress_next[5])
    count_x = lax.axis_size("gx")
    count_y = lax.axis_size("gy")
    cells_x = charge.shape[1]
    total_x = cells_x * count_x
    total_y = charge.shape[2] * count_y
    piece = cells_x // count_y
    block_y = total_y // (count_x * count_y)
    places_x = jnp.arange(total_x, dtype=jnp.int32)
    places_y = jnp.arange(total_y, dtype=jnp.int32)
    columns = lax.all_to_all(charge, "gy", split_axis=1, concat_axis=2, tiled=True)
    true_x = (
        places_x // piece % count_x * cells_x
        + places_x // (count_x * piece) * piece
        + places_x % piece
    )
    cos_y, sin_y = phase_table(places_y, places_y, total_y)
    real_y = jnp.einsum("zxy,yk->zxk", columns, cos_y, precision=lax.Precision.HIGHEST)
    imag_y = -jnp.einsum("zxy,yk->zxk", columns, sin_y, precision=lax.Precision.HIGHEST)
    partial_value = jnp.stack([real_y, imag_y])
    lines = lax.all_to_all(
        lax.all_to_all(partial_value, "gx", split_axis=3, concat_axis=2, tiled=True),
        "gy",
        split_axis=3,
        concat_axis=2,
        tiled=True,
    )
    cos_x, sin_x = phase_table(true_x, places_x, total_x)
    with_cos = jnp.einsum("czxk,xm->czkm", lines, cos_x, precision=lax.Precision.HIGHEST)
    with_sin = jnp.einsum("czxk,xm->czkm", lines, sin_x, precision=lax.Precision.HIGHEST)
    rhs = jnp.stack([with_cos[0] + with_sin[1], with_cos[1] - with_sin[0]])
    first_y = lax.axis_index(("gx", "gy")) * block_y
    mode_y = (first_y + jnp.arange(block_y, dtype=jnp.int32)).astype(jnp.float32)
    wave_x = 2.0 * jnp.sin(math.pi * places_x.astype(jnp.float32) / total_x)
    wave_y = 2.0 * jnp.sin(math.pi * mode_y / total_y)
    wave = wave_y[:, None] * wave_y[:, None] + wave_x[None, :] * wave_x[None, :]
    lateral, couple = couplings(layer_kind, permit_lateral, permit_normal)
    potential_modes = solve_layers(rhs, wave, lateral, couple)
    return (stress_next, velocity_next, potential_modes)


def solution(mesh):
    in_specs = (
        P(None, None, "gx", "gy"),
        P(None, None, "gx", "gy"),
        P(None, "gx", "gy"),
        P(),
        P(),
        P(),
        P(),
        P(),
        P(),
        P(),
    )
    out_specs = (
        P(None, None, "gx", "gy"),
        P(None, None, "gx", "gy"),
        P(None, None, ("gx", "gy"), None),
    )
    return jax.shard_map(
        per_device, mesh=mesh, in_specs=in_specs, out_specs=out_specs, check_vma=False
    )
```

profile of v0, /device:TPU:1, one launch (start us, length us, event | category | flops | bytes accessed | tf_op | source)
XLA Modules:
  0.0 732.8 jit_solution(10278458157353485769)
XLA Ops:
  43.1 9.6 %broadcast_divide_fusion.8 = f32[4,2048]{1,0:T(4,128)} fusion(f32[]{:T(128)} %bitcast.76, f32[]{:T(128)} %bitcast.65, f32[]{:T(128)S(6)} %add.1733, f32[]{:T(128)} %bitcast.61, f32[]{:T(128)} %bitcast.67, f32[]{:T(128)S(6)} %add.1745, f32[]{:T(128)} %bitcast.66, f32[]{:T(128)} %bitcast.69, f32[]{:T(128)S(6)} %add.1749, f32[]{:T(128)} %bitcast.68, ...), kind=kLoop, calls=%fused_computation.291 | loop fusion | flops 278528 | bytes 41060 | tf_op jit(solution)/shard_map/div | solution.py:104
  54.1 10.3 %fusion.147 = f32[4,2048]{1,0:T(4,128)} fusion(f32[]{:T(128)} %bitcast.79, f32[]{:T(128)S(6)} %add.1769, f32[]{:T(128)} %bitcast.76, f32[2048]{0:T(1024)S(1)} %multiply_multiply_fusion, f32[4]{0:T(128)S(1)} %multiply_multiply_fusion.1, f32[]{:T(128)} %bitcast.65, f32[]{:T(128)S(6)} %add.1733, f32[]{:T(128)} %bitcast.61, f32[]{:T(128)} %bitcast.67, ...), kind=kLoop, calls=%fused_computation.252 | loop fusion | flops 311296 | bytes 41068 | tf_op jit(solution)/shard_map/sub | solution.py:100
  64.4 11.0 %broadcast_divide_fusion.7 = f32[4,2048]{1,0:T(4,128)} fusion(f32[]{:T(128)} %bitcast.78, f32[]{:T(128)} %bitcast.65, f32[]{:T(128)S(6)} %add.1733, f32[]{:T(128)} %bitcast.61, f32[]{:T(128)} %bitcast.67, f32[]{:T(128)S(6)} %add.1745, f32[]{:T(128)} %bitcast.66, f32[]{:T(128)} %bitcast.69, f32[]{:T(128)S(6)} %add.1749, f32[]{:T(128)} %bitcast.68, ...), kind=kLoop, calls=%fused_computation.290 | loop fusion | flops 319488 | bytes 41072 | tf_op jit(solution)/shard_map/div | solution.py:104
  76.7 11.6 %fusion.149 = f32[4,2048]{1,0:T(4,128)} fusion(f32[]{:T(128)} %bitcast.81, f32[]{:T(128)S(6)} %add.1773, f32[]{:T(128)} %bitcast.78, f32[2048]{0:T(1024)S(1)} %multiply_multiply_fusion, f32[4]{0:T(128)S(1)} %multiply_multiply_fusion.1, f32[]{:T(128)} %bitcast.65, f32[]{:T(128)S(6)} %add.1733, f32[]{:T(128)} %bitcast.61, f32[]{:T(128)} %bitcast.67, ...), kind=kLoop, calls=%fused_computation.254 | loop fusion | flops 352256 | bytes 41080 | tf_op jit(solution)/shard_map/sub | solution.py:100
  88.4 12.3 %broadcast_divide_fusion.6 = f32[4,2048]{1,0:T(4,128)} fusion(f32[]{:T(128)} %bitcast.80, f32[]{:T(128)} %bitcast.65, f32[]{:T(128)S(6)} %add.1733, f32[]{:T(128)} %bitcast.61, f32[]{:T(128)} %bitcast.67, f32[]{:T(128)S(6)} %add.1745, f32[]{:T(128)} %bitcast.66, f32[]{:T(128)} %bitcast.69, f32[]{:T(128)S(6)} %add.1749, f32[]{:T(128)} %bitcast.68, ...), kind=kLoop, calls=%fused_computation.289 | loop fusion | flops 360448 | bytes 41084 | tf_op jit(solution)/shard_map/div | solution.py:104
  101.9 13.0 %fusion.151 = f32[4,2048]{1,0:T(4,128)} fusion(f32[]{:T(128)} %bitcast.83, f32[]{:T(128)S(6)} %add.1777, f32[]{:T(128)} %bitcast.80, f32[2048]{0:T(1024)S(1)} %multiply_multiply_fusion, f32[4]{0:T(128)S(1)} %multiply_multiply_fusion.1, f32[]{:T(128)} %bitcast.65, f32[]{:T(128)S(6)} %add.1733, f32[]{:T(128)} %bitcast.61, f32[]{:T(128)} %bitcast.67, ...), kind=kLoop, calls=%fused_computation.256 | loop fusion | flops 393216 | bytes 41092 | tf_op jit(solution)/shard_map/sub | solution.py:100
  114.9 13.6 %broadcast_divide_fusion.5 = f32[4,2048]{1,0:T(4,128)} fusion(f32[]{:T(128)} %bitcast.82, f32[]{:T(128)} %bitcast.65, f32[]{:T(128)S(6)} %add.1733, f32[]{:T(128)} %bitcast.61, f32[]{:T(128)} %bitcast.67, f32[]{:T(128)S(6)} %add.1745, f32[]{:T(128)} %bitcast.66, f32[]{:T(128)} %bitcast.69, f32[]{:T(128)S(6)} %add.1749, f32[]{:T(128)} %bitcast.68, ...), kind=kLoop, calls=%fused_computation.288 | loop fusion | flops 401408 | bytes 41096 | tf_op jit(solution)/shard_map/div | solution.py:104
  129.8 14.2 %fusion.153 = f32[4,2048]{1,0:T(4,128)} fusion(f32[]{:T(128)} %bitcast.85, f32[]{:T(128)S(6)} %add.1781, f32[]{:T(128)} %bitcast.82, f32[2048]{0:T(1024)S(1)} %multiply_multiply_fusion, f32[4]{0:T(128)S(1)} %multiply_multiply_fusion.1, f32[]{:T(128)} %bitcast.65, f32[]{:T(128)S(6)} %add.1733, f32[]{:T(128)} %bitcast.61, f32[]{:T(128)} %bitcast.67, ...), kind=kLoop, calls=%fused_computation.258 | loop fusion | flops 434176 | bytes 41104 | tf_op jit(solution)/shard_map/sub | solution.py:100
  144.0 14.9 %broadcast_divide_fusion.4 = f32[4,2048]{1,0:T(4,128)} fusion(f32[]{:T(128)} %bitcast.84, f32[]{:T(128)} %bitcast.65, f32[]{:T(128)S(6)} %add.1733, f32[]{:T(128)} %bitcast.61, f32[]{:T(128)} %bitcast.67, f32[]{:T(128)S(6)} %add.1745, f32[]{:T(128)} %bitcast.66, f32[]{:T(128)} %bitcast.69, f32[]{:T(128)S(6)} %add.1749, f32[]{:T(128)} %bitcast.68, ...), kind=kLoop, calls=%fused_computation.287 | loop fusion | flops 442368 | bytes 41108 | tf_op jit(solution)/shard_map/div | solution.py:104
  160.1 15.6 %fusion.155 = f32[4,2048]{1,0:T(4,128)} fusion(f32[]{:T(128)} %bitcast.87, f32[]{:T(128)S(6)} %add.1785, f32[]{:T(128)} %bitcast.84, f32[2048]{0:T(1024)S(1)} %multiply_multiply_fusion, f32[4]{0:T(128)S(1)} %multiply_multiply_fusion.1, f32[]{:T(128)} %bitcast.65, f32[]{:T(128)S(6)} %add.1733, f32[]{:T(128)} %bitcast.61, f32[]{:T(128)} %bitcast.67, ...), kind=kLoop, calls=%fused_computation.260 | loop fusion | flops 475136 | bytes 41116 | tf_op jit(solution)/shard_map/sub | solution.py:100
  175.7 16.2 %broadcast_divide_fusion.3 = f32[4,2048]{1,0:T(4,128)} fusion(f32[]{:T(128)} %bitcast.86, f32[]{:T(128)} %bitcast.65, f32[]{:T(128)S(6)} %add.1733, f32[]{:T(128)} %bitcast.61, f32[]{:T(128)} %bitcast.67, f32[]{:T(128)S(6)} %add.1745, f32[]{:T(128)} %bitcast.66, f32[]{:T(128)} %bitcast.69, f32[]{:T(128)S(6)} %add.1749, f32[]{:T(128)} %bitcast.68, ...), kind=kLoop, calls=%fused_computation.286 | loop fusion | flops 483328 | bytes 41120 | tf_op jit(solution)/shard_map/div | solution.py:104
  286.8 16.8 %fusion.157 = f32[4,2048]{1,0:T(4,128)} fusion(f32[]{:T(128)} %bitcast.89, f32[]{:T(128)S(6)} %add.1789, f32[]{:T(128)} %bitcast.86, f32[2048]{0:T(1024)S(1)} %multiply_multiply_fusion, f32[4]{0:T(128)S(1)} %multiply_multiply_fusion.1, f32[]{:T(128)} %bitcast.65, f32[]{:T(128)S(6)} %add.1733, f32[]{:T(128)} %bitcast.61, f32[]{:T(128)} %bitcast.67, ...), kind=kLoop, calls=%fused_computation.262 | loop fusion | flops 516096 | bytes 41128 | tf_op jit(solution)/shard_map/sub | solution.py:100
  304.8 17.3 %broadcast_divide_fusion.2 = f32[4,2048]{1,0:T(4,128)} fusion(f32[]{:T(128)} %bitcast.88, f32[]{:T(128)} %bitcast.65, f32[]{:T(128)S(6)} %add.1733, f32[]{:T(128)} %bitcast.61, f32[]{:T(128)} %bitcast.67, f32[]{:T(128)S(6)} %add.1745, f32[]{:T(128)} %bitcast.66, f32[]{:T(128)} %bitcast.69, f32[]{:T(128)S(6)} %add.1749, f32[]{:T(128)} %bitcast.68, ...), kind=kLoop, calls=%fused_computation.285 | loop fusion | flops 524288 | bytes 41132 | tf_op jit(solution)/shard_map/div | solution.py:104
  322.2 17.9 %fusion.159 = f32[4,2048]{1,0:T(4,128)} fusion(f32[]{:T(128)} %bitcast.91, f32[]{:T(128)S(6)} %add.1793, f32[]{:T(128)} %bitcast.88, f32[2048]{0:T(1024)S(1)} %multiply_multiply_fusion, f32[4]{0:T(128)S(1)} %multiply_multiply_fusion.1, f32[]{:T(128)} %bitcast.65, f32[]{:T(128)S(6)} %add.1733, f32[]{:T(128)} %bitcast.61, f32[]{:T(128)} %bitcast.67, ...), kind=kLoop, calls=%fused_computation.264 | loop fusion | flops 557056 | bytes 41140 | tf_op jit(solution)/shard_map/sub | solution.py:100
  340.1 18.5 %fusion.42 = f32[1,16,8,1024]{3,2,1,0:T(8,128)S(1)} fusion(f32[16,8,8,128]{3,0,2,1:T(8,128)S(1)} %bitcast.207), kind=kOutput, calls=%fused_computation.73 | convolution fusion | flops 1626472448 | bytes 1048576 | tf_op jit(solution)/shard_map/zxy,yk->zxk/dot_general | solution.py:156
  358.6 18.5 %fusion.36 = f32[1,16,8,1024]{3,2,1,0:T(8,128)S(1)} fusion(f32[16,8,8,128]{3,0,2,1:T(8,128)S(1)} %bitcast.208), kind=kOutput, calls=%fused_computation.71 | convolution fusion | flops 1626341376 | bytes 1048576 | tf_op jit(solution)/shard_map/zxy,yk->zxk/dot_general | solution.py:155
  392.4 27.6 %all-to-all-start.1 = ((f32[32,1,8192]{2,1,0:T(1,128)}), f32[32,1,8192]{2,1,0:T(1,128)}, u32[]{:S(2)}, u32[]{:S(2)}) async-start(f32[32,1,8192]{2,1,0:T(1,128)} %reshape.956), calls=%async_computation.1 | async-start | bytes 2097152 | tf_op jit(solution)/shard_map/all_to_all | solution.py:159
  420.0 18.6 %broadcast_divide_fusion.1 = f32[4,2048]{1,0:T(4,128)} fusion(f32[]{:T(128)} %bitcast.90, f32[]{:T(128)} %bitcast.65, f32[]{:T(128)S(6)} %add.1733, f32[]{:T(128)} %bitcast.61, f32[]{:T(128)} %bitcast.67, f32[]{:T(128)S(6)} %add.1745, f32[]{:T(128)} %bitcast.66, f32[]{:T(128)} %bitcast.69, f32[]{:T(128)S(6)} %add.1749, f32[]{:T(128)} %bitcast.68, ...), kind=kLoop, calls=%fused_computation.284 | loop fusion | flops 565248 | bytes 41144 | tf_op jit(solution)/shard_map/div | solution.py:104
  441.9 19.2 %fusion.161 = f32[4,2048]{1,0:T(4,128)} fusion(f32[]{:T(128)} %bitcast.93, f32[]{:T(128)S(6)} %add.1797, f32[]{:T(128)} %bitcast.90, f32[2048]{0:T(1024)S(1)} %multiply_multiply_fusion, f32[4]{0:T(128)S(1)} %multiply_multiply_fusion.1, f32[]{:T(128)} %bitcast.65, f32[]{:T(128)S(6)} %add.1733, f32[]{:T(128)} %bitcast.61, f32[]{:T(128)} %bitcast.67, ...), kind=kLoop, calls=%fused_computation.266 | loop fusion | flops 598016 | bytes 41152 | tf_op jit(solution)/shard_map/sub | solution.py:100
  461.1 19.8 %broadcast_divide_fusion = f32[4,2048]{1,0:T(4,128)} fusion(f32[]{:T(128)} %bitcast.92, f32[]{:T(128)} %bitcast.65, f32[]{:T(128)S(6)} %add.1733, f32[]{:T(128)} %bitcast.61, f32[]{:T(128)} %bitcast.67, f32[]{:T(128)S(6)} %add.1745, f32[]{:T(128)} %bitcast.66, f32[]{:T(128)} %bitcast.69, f32[]{:T(128)S(6)} %add.1749, f32[]{:T(128)} %bitcast.68, ...), kind=kLoop, calls=%fused_computation.283 | loop fusion | flops 606208 | bytes 41156 | tf_op jit(solution)/shard_map/div | solution.py:104
  481.0 20.4 %fusion.163 = f32[4,2048]{1,0:T(4,128)} fusion(f32[]{:T(128)} %bitcast.95, f32[]{:T(128)S(6)} %add.1801, f32[]{:T(128)} %bitcast.92, f32[2048]{0:T(1024)S(1)} %multiply_multiply_fusion, f32[4]{0:T(128)S(1)} %multiply_multiply_fusion.1, f32[]{:T(128)} %bitcast.65, f32[]{:T(128)S(6)} %add.1733, f32[]{:T(128)} %bitcast.61, f32[]{:T(128)} %bitcast.67, ...), kind=kLoop, calls=%fused_computation.268 | loop fusion | flops 638976 | bytes 41164 | tf_op jit(solution)/shard_map/sub | solution.py:100
  571.8 72.7 %fusion.3 = f32[2,16,4,2048]{3,1,2,0:T(8,128)S(1)} fusion(f32[2,16,2048,4]{2,1,3,0:T(8,128)S(1)} %all_to_all.50, s32[2048]{0:T(1024)S(1)} %fusion.173), kind=kOutput, calls=%fused_computation.6 | convolution fusion | flops 6505365504 | bytes 2105344 | tf_op jit(solution)/shard_map/czxk,xm->czkm/dot_general | solution.py:167
  644.6 72.0 %fusion.5 = f32[2,16,4,2048]{3,1,2,0:T(8,128)S(1)} fusion(f32[2,16,2048,4]{2,1,3,0:T(8,128)S(1)} %all_to_all.50, s32[2048]{0:T(1024)S(1)} %fusion.173), kind=kOutput, calls=%fused_computation.8 | convolution fusion | flops 6505365504 | bytes 2105344 | tf_op jit(solution)/shard_map/czxk,xm->czkm/dot_general | solution.py:166
  717.0 10.5 %fusion.118 = (f32[2,1,4,2048]{3,1,2,0:T(1,128)S(1)}, f32[2,1,4,2048]{3,1,2,0:T(1,128)S(1)}, f32[2,1,4,2048]{3,1,2,0:T(1,128)S(1)}, f32[2,1,4,2048]{3,1,2,0:T(1,...) fusion(f32[1,16,4,2048]{3,1,2,0:T(8,128)S(1)} %get-tuple-elemen, ...), kind=kLoop, calls=%fused_computation.220 | loop fusion | flops 950272 | bytes 2523192 | tf_op jit(solution)/shard_map/div | solution.py:101
  (208 shorter events, 218.2 us)
Async XLA Ops:
  0.6 193.8 %copy-start.19 = (f32[6,16,64,128]{3,2,1,0:T(8,128)S(1)}, f32[6,16,64,128]{3,2,1,0:T(8,128)}, u32[]{:S(2)}) copy-start(f32[6,16,64,128]{3,2,1,0:T(8,128)} %param.10) | copy-start | bytes 9437188
  2.0 196.7 %collective-permute-start.1 = (f32[6,16,1,128]{3,1,2,0:T(8,128)S(1)}, f32[6,16,1,128]{3,1,2,0:T(8,128)S(1)}, u32[]{:S(2)}, u32[]{:S(2)}) collective-permute-start(f32[6,16,1,128]{3,1,2,0:T(8,128)S(1)} %bitcast.210), channel_id=1, source_target_pairs={{8,0},{16,8},{24,16},{32,24},{40,32},{48,40},{56,48},{64,56},{72,6... | collective-permute-start | bytes 147464 | tf_op jit(solution)/shard_map/ppermute | solution.py:17
  3.3 199.6 %collective-permute-start = (f32[6,16,1,128]{3,1,2,0:T(8,128)S(1)}, f32[6,16,1,128]{3,1,2,0:T(8,128)S(1)}, u32[]{:S(2)}, u32[]{:S(2)}) collective-permute-start(f32[6,16,1,128]{3,1,2,0:T(8,128)S(1)} %bitcast.209), channel_id=1, source_target_pairs={{0,8},{8,16},{16,24},{24,32},{32,40},{40,48},{48,56},{56,64},{64,7... | collective-permute-start | bytes 147464 | tf_op jit(solution)/shard_map/ppermute | solution.py:14
  208.2 11.7 %collective-permute-start.3 = (f32[6,16,66,1]{2,1,3,0:T(8,128)S(1)}, f32[6,16,66,1]{2,1,3,0:T(8,128)S(1)}, u32[]{:S(2)}, u32[]{:S(2)}) collective-permute-start(f32[6,16,66,1]{2,1,3,0:T(8,128)S(1)} %get-tuple-element.56), channel_id=1, source_target_pairs={{1,0},{2,1},{3,2},{4,3},{5,4},{6,5},{7,6},{9,8},{10,9},{11,10},{12... | collective-permute-start | bytes 76040 | tf_op jit(solution)/shard_map/ppermute | solution.py:17
  213.4 6.6 collective-permute-start.2
  246.0 7.1 collective-permute-start.5
  248.5 5.9 collective-permute-start.4
  257.5 7.8 %collective-permute-start.7 = (f32[3,16,66,1]{2,1,3,0:T(8,128)S(1)}, f32[3,16,66,1]{2,1,3,0:T(8,128)S(1)}, u32[]{:S(2)}, u32[]{:S(2)}) collective-permute-start(f32[3,16,66,1]{2,1,3,0:T(8,128)S(1)} %get-tuple-element.58), channel_id=1, source_target_pairs={{1,0},{2,1},{3,2},{4,3},{5,4},{6,5},{7,6},{9,8},{10,9},{11,10},{12... | collective-permute-start | bytes 38024 | tf_op jit(solution)/shard_map/ppermute | solution.py:17
  260.4 4.8 collective-permute-start.6
  269.8 242.5 %copy-start.2 = (f32[16,66,130]{1,0,2:T(8,128)}, f32[16,66,130]{1,0,2:T(8,128)S(1)}, u32[]{:S(2)}) copy-start(f32[16,66,130]{1,0,2:T(8,128)S(1)} %get-tuple-element.66) | copy-start | bytes 1647364
  281.6 58.5 %all-to-all-start = ((f32[16,64,128]{2,0,1:T(8,128)}), f32[16,64,128]{2,0,1:T(8,128)S(1)}, u32[]{:S(2)}, u32[]{:S(2)}) async-start(f32[16,64,128]{2,0,1:T(8,128)} %copy.64), calls=%async_computation | async-start | bytes 1048576 | tf_op jit(solution)/shard_map/all_to_all | solution.py:148
  392.4 121.2 %all-to-all-start.1 = ((f32[32,1,8192]{2,1,0:T(1,128)}), f32[32,1,8192]{2,1,0:T(1,128)}, u32[]{:S(2)}, u32[]{:S(2)}) async-start(f32[32,1,8192]{2,1,0:T(1,128)} %reshape.956), calls=%async_computation.1 | async-start | bytes 2097152 | tf_op jit(solution)/shard_map/all_to_all | solution.py:159
  535.2 34.6 %all-to-all-start.2 = ((f32[2,16,256,32]{2,1,0,3:T(8,128)}), f32[2,16,256,32]{2,1,0,3:T(8,128)}, u32[]{:S(2)}, u32[]{:S(2)}) async-start(f32[2,16,256,32]{2,1,0,3:T(8,128)} %copy.68), calls=%async_computation.2 | async-start | bytes 2097152 | tf_op jit(solution)/shard_map/all_to_all | solution.py:158
  644.5 72.4 %copy-start.26 = (f32[4,2048]{1,0:T(4,128)S(1)}, f32[4,2048]{1,0:T(4,128)}, u32[]{:S(2)}) copy-start(f32[4,2048]{1,0:T(4,128)} %get-tuple-element.78) | copy-start | bytes 98308
  644.5 72.4 %copy-start.27 = (f32[4,2048]{1,0:T(4,128)S(1)}, f32[4,2048]{1,0:T(4,128)}, u32[]{:S(2)}) copy-start(f32[4,2048]{1,0:T(4,128)} %get-tuple-element.80) | copy-start | bytes 98308
  644.5 72.4 %copy-start.28 = (f32[4,2048]{1,0:T(4,128)S(1)}, f32[4,2048]{1,0:T(4,128)}, u32[]{:S(2)}) copy-start(f32[4,2048]{1,0:T(4,128)} %get-tuple-element.82) | copy-start | bytes 98308
  644.5 72.4 %copy-start.29 = (f32[4,2048]{1,0:T(4,128)S(1)}, f32[4,2048]{1,0:T(4,128)}, u32[]{:S(2)}) copy-start(f32[4,2048]{1,0:T(4,128)} %get-tuple-element.84) | copy-start | bytes 98308
  644.5 72.4 %copy-start.30 = (f32[4,2048]{1,0:T(4,128)S(1)}, f32[4,2048]{1,0:T(4,128)}, u32[]{:S(2)}) copy-start(f32[4,2048]{1,0:T(4,128)} %get-tuple-element.86) | copy-start | bytes 98308
  644.5 72.4 %copy-start.31 = (f32[4,2048]{1,0:T(4,128)S(1)}, f32[4,2048]{1,0:T(4,128)}, u32[]{:S(2)}) copy-start(f32[4,2048]{1,0:T(4,128)} %get-tuple-element.87) | copy-start | bytes 98308
  644.5 72.4 %copy-start.35 = (f32[4,2048]{1,0:T(4,128)S(1)}, f32[4,2048]{1,0:T(4,128)}, u32[]{:S(2)}) copy-start(f32[4,2048]{1,0:T(4,128)} %fusion.151) | copy-start | bytes 98308
  644.5 72.4 %copy-start.36 = (f32[4,2048]{1,0:T(4,128)S(1)}, f32[4,2048]{1,0:T(4,128)}, u32[]{:S(2)}) copy-start(f32[4,2048]{1,0:T(4,128)} %fusion.153) | copy-start | bytes 98308
  644.5 72.4 %copy-start.41 = (f32[4,2048]{1,0:T(4,128)S(1)}, f32[4,2048]{1,0:T(4,128)}, u32[]{:S(2)}) copy-start(f32[4,2048]{1,0:T(4,128)} %fusion.145) | copy-start | bytes 98308
  644.5 72.4 %copy-start.42 = (f32[4,2048]{1,0:T(4,128)S(1)}, f32[4,2048]{1,0:T(4,128)}, u32[]{:S(2)}) copy-start(f32[4,2048]{1,0:T(4,128)} %fusion.147) | copy-start | bytes 98308
  644.6 72.4 %copy-start.43 = (f32[4,2048]{1,0:T(4,128)S(1)}, f32[4,2048]{1,0:T(4,128)}, u32[]{:S(2)}) copy-start(f32[4,2048]{1,0:T(4,128)} %fusion.149) | copy-start | bytes 98308
  (45 other events, 645.0 us)
where the time goes:
time: 744 us; the launch traced here: 733 us
  other arithmetic  373 us (50%)
  matrix products  182 us (24%)
  local copies, waits for them, and re-layouts  93.2 us (13%)
  starting transfers between devices  62.6 us (8%)
  between operations  22.4 us (3%)
    div x11, other arithmetic, solve_layers(): factors.append(couple[layer_no + 1] / pivot)  149 us
    sub x10, other arithmetic, solve_layers(): pivot = pivot - couple[layer_no] * factors[-1]  148 us
    dot_general x1, matrix products, per_device(): jnp.einsum('czxk,xm->czkm', lines, sin_x, precision=lax.Precision.HIGHEST)  72.7 us
    dot_general x1, matrix products, per_device(): jnp.einsum('czxk,xm->czkm', lines, cos_x, precision=lax.Precision.HIGHEST)  72 us
    unnamed x127, local copies, waits for them, and re-layouts  34.2 us
    all_to_all x1, starting transfers between devices, per_device(): lax.all_to_all(partial_value, 'gx', split_axis=3, concat_axis=2, tiled=True)  27.6 us
    unnamed x5, other arithmetic  20.7 us
    dot_general x1, matrix products, per_device(): jnp.einsum('zxy,yk->zxk', columns, sin_y, precision=lax.Precision.HIGHEST)  18.5 us
  transfers between devices with their start and end apart: 11, of which 0 were waited for; matrix products, arithmetic and copies ran while one was open for 49% of the time, Pallas kernels for 0%

commit v1 on v0

v1 whole, which is shorter than its diff:
```python
import functools
import math

import jax
import jax.numpy as jnp
import ml_dtypes
import numpy as np
from jax import lax
from jax.experimental import pallas as pl
from jax.experimental.pallas import tpu as pltpu
from jax.sharding import PartitionSpec as P

NZ = 16
NX = 2048
NY = 1024
DX = 32
DY = 8
BX = NX // DX
BY = NY // DY
VMEM_LIMIT = 56 * 1024 * 1024


def halves(values):
    high = values.astype(ml_dtypes.bfloat16)
    low = (values - high.astype(np.float64)).astype(ml_dtypes.bfloat16)
    return high, low


def split(values):
    high = values.astype(jnp.bfloat16)
    low = (values - high.astype(jnp.float32)).astype(jnp.bfloat16)
    return high, low


def tables_y():
    j = np.arange(128)
    a = np.arange(8)
    angle = 2.0 * np.pi * (np.outer(j, j) % 128) / 128
    cos, sin = np.cos(angle) / 32.0, np.sin(angle) / 32.0
    weights = np.block([[cos, sin], [-sin, cos]])
    turn = 2.0 * np.pi * np.outer(a, j) / NY
    twiddle = np.stack([np.cos(turn), np.sin(turn)], axis=1).reshape(16, 128)
    return *halves(weights), twiddle.astype(np.float32)


def tables_x():
    n1 = np.arange(128)
    angle = 2.0 * np.pi * (np.outer(n1, n1) % 128) / 128
    scale = 1.0 / math.sqrt(NX)
    cos, sin = np.cos(angle) * scale, np.sin(angle) * scale
    real_rows = np.concatenate([cos, -sin], axis=1).reshape(DX, 1, 4, 256)
    imag_rows = np.concatenate([sin, cos], axis=1).reshape(DX, 1, 4, 256)
    weights = np.concatenate([real_rows, imag_rows], axis=1).reshape(256, 256)
    turn = 2.0 * np.pi * np.outer(np.arange(16), n1) / NX
    twiddle = np.stack([np.cos(turn), np.sin(turn)], axis=1).reshape(32, 128)
    return *halves(weights), twiddle.astype(np.float32)


def table_wave():
    wave = 2.0 * np.sin(np.pi * np.arange(NX) / NX)
    return (wave * wave).astype(np.float32).reshape(1, NX)


def dot3(a, b, dims):
    (a_high, a_low), (b_high, b_low) = a, b
    dot = functools.partial(
        lax.dot_general, dimension_numbers=(dims, ((), ())), preferred_element_type=jnp.float32
    )
    return dot(a_high, b_high) + (dot(a_low, b_high) + dot(a_high, b_low))


def pick(codes, table_ref):
    first, second, third = table_ref[0], table_ref[1], table_ref[2]
    return jnp.where(codes == 0, first, jnp.where(codes == 1, second, third))


def lanes(values):
    return lax.broadcasted_iota(jnp.int32, values.shape, values.ndim - 1)


def rows(values):
    return lax.broadcasted_iota(jnp.int32, values.shape, values.ndim - 2)


def next_lane(values):
    moved = pltpu.roll(values, values.shape[-1] - 1, values.ndim - 1)
    return jnp.where(lanes(values) == values.shape[-1] - 1, 0.0, moved)


def last_lane(values):
    moved = pltpu.roll(values, 1, values.ndim - 1)
    return jnp.where(lanes(values) == 0, 0.0, moved)


def next_row(values, edge):
    size = values.shape[0]
    moved = pltpu.roll(values, size - 1, 0)
    tail = moved[size - 8 :]
    tail = jnp.where(rows(tail) == 7, edge, tail)
    return jnp.concatenate([moved[: size - 8], tail], axis=0)


def last_row(values, edge):
    moved = pltpu.roll(values, 1, 0)
    head = jnp.where(rows(moved[:8]) == 0, edge, moved[:8])
    return jnp.concatenate([head, moved[8:]], axis=0)


def next_layer(values):
    size = values.shape[0]
    moved = pltpu.roll(values, size - 1, 0)
    return jnp.where(rows(values) == size - 1, 0.0, moved)


def last_layer(values):
    moved = pltpu.roll(values, 1, 0)
    return jnp.where(rows(values) == 0, 0.0, moved)


def edge_rows(buoy, stress_first, stress_end, veloc_first, veloc_end, mat_first, mat_end, down_ref, up_ref):
    sxx, sxy, sxz = (stress_end[c, :, 7, :] for c in (0, 3, 4))
    b = pick(mat_end[:, 7, :], buoy)
    down_ref[0] = veloc_end[0, :, 7, :] + b * ((sxy - last_lane(sxy)) + (sxz - last_layer(sxz)) - sxx)
    down_ref[1] = b
    down_ref[2] = sxy
    down_ref[3] = sxz
    sxx, syy, szz, sxy, sxz, syz = (stress_first[c, :, 0, :] for c in range(6))
    b = pick(mat_first[:, 0, :], buoy)
    up_ref[0] = veloc_first[1, :, 0, :] + b * (sxy + (next_lane(syy) - syy) + (syz - last_layer(syz)))
    up_ref[1] = veloc_first[2, :, 0, :] + b * (sxz + (syz - last_lane(syz)) + (next_layer(szz) - szz))
    up_ref[2] = b
    up_ref[3] = sxx
    up_ref[4] = syy
    up_ref[5] = syz


def advance_velocity(buoy, stress, veloc, material, low, high, new, right_ref, left_ref):
    column = lax.broadcasted_iota(jnp.int32, (BX, BY), 1)
    right = jnp.zeros((BX, BY), jnp.float32)
    left = jnp.zeros((BX, BY), jnp.float32)
    for z in range(NZ):
        sxx, syy, szz, sxy, sxz, syz = (stress[c, z] for c in range(6))
        b = pick(material[z], buoy)
        dz_sxz = sxz - stress[4, z - 1] if z else sxz
        dz_syz = syz - stress[5, z - 1] if z else syz
        dz_szz = stress[2, z + 1] - szz if z < NZ - 1 else -szz
        ux = veloc[0, z] + b * (
            (next_row(sxx, high[3, z : z + 1]) - sxx) + (sxy - last_lane(sxy)) + dz_sxz
        )
        uy = veloc[1, z] + b * (
            (sxy - last_row(sxy, low[2, z : z + 1])) + (next_lane(syy) - syy) + dz_syz
        )
        uz = veloc[2, z] + b * (
            (sxz - last_row(sxz, low[3, z : z + 1])) + (syz - last_lane(syz)) + dz_szz
        )
        new[0, z] = ux
        new[1, z] = uy
        new[2, z] = uz
        for part, value in enumerate((uy, b, sxy, syz)):
            spot = part * NZ + z
            moved = pltpu.roll(value, (spot + 1) % BY, 1)
            right = jnp.where(column == spot, moved, right)
        for part, value in enumerate((ux, uz, b, syy)):
            spot = part * NZ + z
            moved = pltpu.roll(value, spot, 1) if spot else value
            left = jnp.where(column == spot, moved, left)
    right_ref[:BX] = right
    left_ref[:BX] = left
    corner = column[:NZ]
    right_ref[BX:] = jnp.where(
        corner == 0, pltpu.roll(low[2], 1, 1), jnp.where(corner == 1, pltpu.roll(high[5], 2, 1), 0.0)
    )
    left_ref[BX:] = jnp.where(corner == 0, high[4], 0.0)


def advance_stress(
    buoy, lame, shear, piezo, stress, part, material, low, high,
    own_right, own_left, from_left, from_right, new_stress, new_veloc, charge,
):
    lane = lax.broadcasted_iota(jnp.int32, (BX, BY), 1)
    corner_lane = lane[:NZ]
    west, east = from_left[:BX], from_right[:BX]
    mine_east, mine_west = own_right[:BX], own_left[:BX]

    def shifted(values, by):
        return pltpu.roll(values, (-by * NZ) % BY, 1)

    uy_west = west + shifted(west, 1) * shifted(mine_west, 3)
    ux_east = east - shifted(east, 2) * shifted(mine_east, 2)
    uz_east = shifted(east, 1) - shifted(east, 2) * shifted(mine_east, 3)
    west_corner, east_corner = from_left[BX:], from_right[BX:]
    ux_low = low[0] - jnp.where(corner_lane == 0, low[1] * west_corner[:, 0:1], 0.0)
    uy_high = high[0] + jnp.where(corner_lane == BY - 1, high[2] * east_corner[:, 0:1], 0.0)
    uz_high = high[1] - jnp.where(corner_lane == 0, high[2] * west_corner[:, 1:2], 0.0)

    def beside(values, spot):
        return jnp.broadcast_to(values[:, spot : spot + 1], (BX, BY))

    for z in range(NZ):
        b = pick(material[z], buoy)
        new_veloc[0, z] = part[0, z] - jnp.where(lane == 0, b * beside(west, 2 * NZ + z), 0.0)
        new_veloc[1, z] = part[1, z] + jnp.where(lane == BY - 1, b * beside(east, 3 * NZ + z), 0.0)
        new_veloc[2, z] = part[2, z] - jnp.where(lane == 0, b * beside(west, 3 * NZ + z), 0.0)
    for z in range(NZ):
        sxx, syy, szz, sxy, sxz, syz = (stress[c, z] for c in range(6))
        ux, uy, uz = (new_veloc[c, z] for c in range(3))
        codes = material[z]
        lam, mu, e = pick(codes, lame), pick(codes, shear), pick(codes, piezo)
        row = slice(z, z + 1)
        ex = ux - last_row(ux, ux_low[row] + low[1, row] * sxx[0:1])
        ey = uy - jnp.where(lane == 0, beside(uy_west, z), pltpu.roll(uy, 1, 1))
        ez = uz - new_veloc[2, z - 1] if z else uz
        lam_div = lam * (ex + ey + ez)
        mu2 = 2.0 * mu
        new_stress[0, z] = sxx + lam_div + mu2 * ex
        new_stress[1, z] = syy + lam_div + mu2 * ey
        new_stress[2, z] = szz + lam_div + mu2 * ez
        b_high = high[2, row]
        dx_uy = next_row(uy, uy_high[row] - b_high * sxy[BX - 1 : BX]) - uy
        dx_uz = next_row(uz, uz_high[row] - b_high * sxz[BX - 1 : BX]) - uz
        last = lane == BY - 1
        dy_ux = jnp.where(last, beside(ux_east, z), pltpu.roll(ux, BY - 1, 1)) - ux
        dy_uz = jnp.where(last, beside(uz_east, z), pltpu.roll(uz, BY - 1, 1)) - uz
        dz_ux = new_veloc[0, z + 1] - ux if z < NZ - 1 else -ux
        dz_uy = new_veloc[1, z + 1] - uy if z < NZ - 1 else -uy
        new_sxz = sxz + mu * (dz_ux + dx_uz)
        new_syz = syz + mu * (dz_uy + dy_uz)
        new_stress[3, z] = sxy + mu * (dy_ux + dx_uy)
        new_stress[4, z] = new_sxz
        new_stress[5, z] = new_syz
        charge[z] = e * (new_sxz + new_syz)


ROOT = math.sqrt(0.5)


def real_dft8(c):
    s = [c[i] + c[i + 4] for i in range(4)]
    d = [c[i] - c[i + 4] for i in range(4)]
    even, odd = s[0] + s[2], s[1] + s[3]
    near, far = ROOT * (d[1] - d[3]), ROOT * (d[1] + d[3])
    re1, re3 = d[0] + near, d[0] - near
    im1, im3 = -(d[2] + far), d[2] - far
    re2, im2 = s[0] - s[2], s[3] - s[1]
    zero = None
    return [
        (even + odd, zero), (re1, im1), (re2, im2), (re3, im3),
        (even - odd, zero), (re3, -im3), (re2, -im2), (re1, -im1),
    ]


def transform_y(charge, w_high, w_low, twiddle, out, real_lines, imag_lines):
    for z in range(2):
        for ihi in range(4):
            at = slice(16 * ihi, 16 * ihi + 16)
            modes = real_dft8([charge[g, z, at, :] for g in range(8)])
            for a, (re, im) in enumerate(modes):
                cos, sin = twiddle[2 * a : 2 * a + 1, :], twiddle[2 * a + 1 : 2 * a + 2, :]
                if a == 0:
                    new_re, new_im = re, jnp.zeros_like(re)
                elif im is None:
                    new_re, new_im = re * cos, -(re * sin)
                else:
                    new_re, new_im = re * cos + im * sin, im * cos - re * sin
                base = (ihi * 2 + a // 4) * 128 + z * 4 + a % 4
                real_lines[pl.ds(base, 16, stride=8), :] = new_re
                imag_lines[pl.ds(base, 16, stride=8), :] = new_im
    weights = (w_high[...], w_low[...])
    for ihi in range(4):
        for ahi in range(2):
            block = slice((ihi * 2 + ahi) * 128, (ihi * 2 + ahi + 1) * 128)
            lines = jnp.concatenate([real_lines[block, :], imag_lines[block, :]], axis=1)
            modes = dot3(weights, split(lines), ((1,), (1,)))
            for part in range(2):
                start = ahi * 8 + part * 4 + ihi
                out[pl.ds(start, 128, stride=16), :] = modes[part * 128 : (part + 1) * 128]


def butterfly4(x):
    (ar, ai), (br, bi) = (
        (x[0][0] + x[2][0], x[0][1] + x[2][1]),
        (x[0][0] - x[2][0], x[0][1] - x[2][1]),
    )
    (cr, ci), (dr, di) = (
        (x[1][0] + x[3][0], x[1][1] + x[3][1]),
        (x[1][0] - x[3][0], x[1][1] - x[3][1]),
    )
    return [(ar + cr, ai + ci), (br + di, bi - dr), (ar - cr, ai - ci), (br - di, bi + dr)]


def turned(value, step):
    re, im = value
    step %= 16
    if step == 0:
        return value
    if step == 4:
        return im, -re
    if step == 2:
        return ROOT * (re + im), ROOT * (im - re)
    if step == 6:
        return ROOT * (im - re), -ROOT * (re + im)
    cos, sin = math.cos(2 * math.pi * step / 16), math.sin(2 * math.pi * step / 16)
    return re * cos + im * sin, im * cos - re * sin


def dft16(x):
    inner = [butterfly4([x[4 * na + nb] for na in range(4)]) for nb in range(4)]
    result = [None] * 16
    for ka in range(4):
        outer = butterfly4([turned(inner[nb][ka], nb * ka) for nb in range(4)])
        for kb in range(4):
            result[ka + 4 * kb] = outer[kb]
    return result


def coupling_scalars(layer_kind, lateral, normal):
    def at(table, kind):
        return jnp.where(kind == 0, table[0], jnp.where(kind == 1, table[1], table[2]))

    el = [at(lateral, layer_kind[z]) for z in range(NZ)]
    en = [at(normal, layer_kind[z]) for z in range(NZ)]
    g = [en[0]] + [0.5 * (en[z - 1] + en[z]) for z in range(1, NZ)] + [en[-1]]
    return el, g


def pivots(layer_kind, lateral, normal, wave_x, inverse):
    el, g = coupling_scalars(layer_kind, lateral, normal)
    first = (lax.axis_index("gx") * DY + lax.axis_index("gy")) * 4
    ky = first + rows(jnp.zeros((8, 128), jnp.float32)) % 4
    wave_y = 2.0 * jnp.sin(math.pi * ky.astype(jnp.float32) / NY)
    wave_y = wave_y * wave_y
    for k in range(NX // 512):
        at = slice(512 * k, 512 * k + 512)
        wave = jnp.concatenate([wave_y] * 4, axis=1) + wave_x[:, at]
        factor = None
        for z in range(NZ):
            pivot = g[z] + g[z + 1] + wave * el[z]
            if z:
                pivot = pivot - g[z] * factor
            inv = 1.0 / pivot
            inverse[z, :, at] = inv
            factor = g[z + 1] * inv


def solve(layer_kind, lateral, normal, lines, w_high, w_low, twiddle, inverse, out, rhs):
    weights = (w_high[...], w_low[...])
    upper = rows(jnp.zeros((8, 128), jnp.float32)) < 4
    for gy in range(DY):
        block = lines[:, gy].reshape(256, 128)
        modes = dot3(split(block.T), weights, ((1,), (0,)))
        turned_modes = []
        for n2 in range(16):
            re, im = modes[8 * n2 : 8 * n2 + 8, :128], modes[8 * n2 : 8 * n2 + 8, 128:]
            if n2:
                cos, sin = twiddle[2 * n2 : 2 * n2 + 1, :], twiddle[2 * n2 + 1 : 2 * n2 + 2, :]
                re, im = re * cos + im * sin, im * cos - re * sin
            turned_modes.append((re, im))
        for k2, (re, im) in enumerate(dft16(turned_modes)):
            at = slice(128 * k2, 128 * k2 + 128)
            rhs[2 * gy, :, at] = jnp.where(upper, re, pltpu.roll(im, 4, 0))
            rhs[2 * gy + 1, :, at] = jnp.where(upper, pltpu.roll(re, 4, 0), im)
    _, g = coupling_scalars(layer_kind, lateral, normal)
    for k in range(NX // 256):
        at = slice(256 * k, 256 * k + 256)
        sums = []
        for z in range(NZ):
            value = rhs[z, :, at]
            if z:
                value = value + g[z] * (sums[-1] * inverse[z - 1, :, at])
            sums.append(value)
        above = None
        for z in range(NZ - 1, -1, -1):
            value = sums[z]
            if above is not None:
                value = value + g[z + 1] * above
            above = value * inverse[z, :, at]
            out[0, z, :, at] = above[:4]
            out[1, z, :, at] = above[4:]


SMEM = pl.BlockSpec(memory_space=pltpu.SMEM)
VMEM = pl.BlockSpec(memory_space=pltpu.VMEM)


def call(body, name, outs, in_specs, args, scratch=(), flops=1_000_000, grid_spec=None):
    shapes = [jax.ShapeDtypeStruct(shape, jnp.float32) for shape in outs]
    moved = sum(4 * math.prod(shape) for shape in outs) + sum(4 * v.size for v in args)
    return pl.pallas_call(
        body,
        name=name,
        out_shape=shapes,
        in_specs=in_specs,
        out_specs=[VMEM] * len(outs),
        scratch_shapes=list(scratch),
        compiler_params=pltpu.CompilerParams(vmem_limit_bytes=VMEM_LIMIT),
        cost_estimate=pl.CostEstimate(flops=flops, bytes_accessed=moved, transcendentals=0),
    )(*args)


def edge_call(buoyancy, stress, velocity, material):
    end = BX // 8 - 1
    block4 = lambda count, at: pl.BlockSpec((count, NZ, 8, BY), lambda i: (0, 0, at, 0))
    block3 = lambda at: pl.BlockSpec((NZ, 8, BY), lambda i: (0, at, 0))
    whole = lambda count: pl.BlockSpec((count, NZ, BY), lambda i: (0, 0, 0))
    return pl.pallas_call(
        edge_rows,
        name="edge_rows",
        grid=(1,),
        out_shape=[jax.ShapeDtypeStruct((count, NZ, BY), jnp.float32) for count in (4, 6)],
        in_specs=[SMEM, block4(6, 0), block4(6, end), block4(3, 0), block4(3, end), block3(0), block3(end)],
        out_specs=[whole(4), whole(6)],
        compiler_params=pltpu.CompilerParams(vmem_limit_bytes=VMEM_LIMIT),
    )(buoyancy, stress, stress, velocity, velocity, material, material)


def per_device(
    stress, velocity, material, layer_kind, buoyancy, lame_first, shear_modulus, piezo, permit_lateral, permit_normal
):
    def chain(count):
        forward = [(i, i + 1) for i in range(count - 1)]
        return forward, [(target, source) for source, target in forward]

    down, up = chain(DX)
    right, left = chain(DY)
    to_next, to_previous = edge_call(buoyancy, stress, velocity, material)
    low = lax.ppermute(to_next, "gx", down)
    high = lax.ppermute(to_previous, "gx", up)
    part, own_right, own_left = call(
        advance_velocity,
        "advance_velocity",
        [(3, NZ, BX, BY), (BX + NZ, BY), (BX + NZ, BY)],
        [SMEM] + [VMEM] * 5,
        (buoyancy, stress, velocity, material, low, high),
    )
    from_left = lax.ppermute(own_right, "gy", right)
    from_right = lax.ppermute(own_left, "gy", left)
    stress_next, velocity_next, charge = call(
        advance_stress,
        "advance_stress",
        [(6, NZ, BX, BY), (3, NZ, BX, BY), (NZ, BX, BY)],
        [SMEM] * 4 + [VMEM] * 9,
        (
            buoyancy, lame_first, shear_modulus, piezo, stress, part, material, low, high,
            own_right, own_left, from_left, from_right,
        ),
    )
    charge = lax.all_to_all(charge, "gy", 0, 0, tiled=True).reshape(DY, 2, BX, BY)
    modes, = call(
        transform_y,
        "transform_y",
        [(NY * 2, 128)],
        [VMEM] * 4,
        (charge, *(jnp.asarray(t) for t in tables_y())),
        [pltpu.VMEM((1024, 128), jnp.float32)] * 2,
    )
    lines = lax.all_to_all(modes.reshape(DX * DY, 8, 128), ("gx", "gy"), 0, 0, tiled=True)
    scalars = (layer_kind, permit_lateral, permit_normal)
    inverse, = call(
        pivots, "pivots", [(NZ, 8, NX)], [SMEM] * 3 + [VMEM], (*scalars, jnp.asarray(table_wave()))
    )
    potential_modes, = call(
        solve,
        "solve",
        [(2, NZ, 4, NX)],
        [SMEM] * 3 + [VMEM] * 5,
        (*scalars, lines.reshape(DX, DY, 8, 128), *(jnp.asarray(t) for t in tables_x()), inverse),
        [pltpu.VMEM((NZ, 8, NX), jnp.float32)],
    )
    return (stress_next, velocity_next, potential_modes)


def solution(mesh):
    field = P(None, None, "gx", "gy")
    return jax.shard_map(
        per_device,
        mesh=mesh,
        in_specs=(field, field, P(None, "gx", "gy")) + (P(),) * 7,
        out_specs=(field, field, P(None, None, ("gx", "gy"), None)),
        check_vma=False,
    )
```

time: 744 us -> 116 us (0.16); the launches traced: 733 us -> 115 us
  other arithmetic: 373 us -> 0 us
  matrix products: 182 us -> 0 us
  local copies, waits for them, and re-layouts: 93.2 us -> 2.82 us
  waiting for transfers between devices: 0.03 us -> 33.8 us
  starting transfers between devices: 62.6 us -> 35 us
  Pallas kernels: 0 us -> 23.7 us
  between operations: 22.4 us -> 0.69 us
  blocking collectives: 0 us -> 19.2 us
    dot_general x4 -> x0, matrix products: 182 us -> none  [the longest x1 72.7 us: per_device(): jnp.einsum('czxk,xm->czkm', lines, sin_x, precision=lax.Precision.HIGHEST)]
    div x12 -> x0, other arithmetic: 160 us -> none  [the longest x11 149 us: solve_layers(): factors.append(couple[layer_no + 1] / pivot)]
    sub x10 -> x0, other arithmetic: 148 us -> none  [solve_layers(): pivot = pivot - couple[layer_no] * factors[-1]]
    unnamed x127 -> x10, local copies, waits for them, and re-layouts: 34.2 us -> 2.82 us
    all_to_all x3 -> x1, waiting for transfers between devices: 0.01 us -> 28.9 us  [per_device(): lax.all_to_all(modes.reshape(DX * DY, 8, 128), ('gx', 'gy'), 0, 0, tiled=...]
    pallas_call x0 -> x6, Pallas kernels: none -> 23.7 us  [the longest x5 21.6 us: call(): pl.pallas_call(body, name=name, out_shape=shapes, in_specs=in_specs, out_...]
    unnamed x5 -> x0, other arithmetic: 20.7 us -> none
    slice x19 -> x0, local copies, waits for them, and re-layouts: 20 us -> none  [the longest x6 5.4 us: lookup(): result = result + jnp.where(codes == material_no, table[material_no], 0.0)]
  transfers between devices with their start and end apart: 11 -> 5, of which waited for: 0 -> 3; matrix products, arithmetic and copies ran while one was open for 49% -> 0% of each run, Pallas kernels for 0% -> 2%
where the time goes in v1:
time: 116 us; the launch traced here: 115 us
  starting transfers between devices  35 us (30%)
  waiting for transfers between devices  33.8 us (29%)
  Pallas kernels  23.7 us (20%)
  blocking collectives  19.2 us (17%)
  local copies, waits for them, and re-layouts  2.82 us (2%)
    all_to_all x1, waiting for transfers between devices, per_device(): lax.all_to_all(modes.reshape(DX * DY, 8, 128), ('gx', 'gy'), 0, 0, tiled=...  28.9 us
    all_to_all x1, starting transfers between devices, per_device(): lax.all_to_all(modes.reshape(DX * DY, 8, 128), ('gx', 'gy'), 0, 0, tiled=...  21.8 us
    pallas_call x5, Pallas kernels, call(): pl.pallas_call(body, name=name, out_shape=shapes, in_specs=in_specs, out_...  21.6 us
    all_to_all x1, blocking collectives, per_device(): lax.all_to_all(charge, 'gy', 0, 0, tiled=True).reshape(DY, 2, BX, BY)  19.2 us
    ppermute x1, starting transfers between devices, per_device(): from_left = lax.ppermute(own_right, 'gy', right)  5.38 us
    ppermute x1, starting transfers between devices, per_device(): low = lax.ppermute(to_next, 'gx', down)  4.66 us
    ppermute x1, waiting for transfers between devices, per_device(): from_right = lax.ppermute(own_left, 'gy', left)  3.58 us
    unnamed x10, local copies, waits for them, and re-layouts  2.82 us
  transfers between devices with their start and end apart: 5, of which 3 were waited for; matrix products, arithmetic and copies ran while one was open for 0% of the time, Pallas kernels for 2%

profile of v1, /device:TPU:1, one launch (start us, length us, event | category | flops | bytes accessed | tf_op | source)
XLA Modules:
  0.0 115.2 jit_solution(18167994385211601283)
XLA Ops:
  0.6 2.0 %edge_rows.1 = (f32[4,16,128]{2,1,0:T(8,128)}, f32[6,16,128]{2,1,0:T(8,128)}) custom-call(f32[3]{0:T(128)} %buoy.5, f32[6,16,64,128]{3,2,1,0:T(8,128)} %stress.3, f32[6,16,64,128]{3,2,1,0:T(8,128)} %stress.3, f32[3,16,64,128]{3,2,1,0:T(8,128)} %veloc.1, f32[3,16,64,128]{3,2,1,0:T(8,128)} %veloc.1, s32[16,64,128]{2,1,0:T(8,128)} %material.3, ...), custom_call_target="tpu_custom_call" | custom-call | tf_op jit(solution)/shard_map/edge_rows/pallas_call | solution.py:405
  2.7 1.3 %collective-permute-start.1 = (f32[6,16,128]{2,1,0:T(8,128)}, f32[6,16,128]{2,1,0:T(8,128)S(1)}, u32[]{:S(2)}, u32[]{:S(2)}) collective-permute-start(f32[6,16,128]{2,1,0:T(8,128)} %get-tuple-element.12), channel_id=1, source_target_pairs={{8,0},{16,8},{24,16},{32,24},{40,32},{48,40},{56,48},{64,56},{72,6... | collective-permute-start | bytes 147464 | tf_op jit(solution)/shard_map/ppermute | solution.py:427
  3.9 4.7 %collective-permute-start = (f32[4,16,128]{2,1,0:T(8,128)}, f32[4,16,128]{2,1,0:T(8,128)S(1)}, u32[]{:S(2)}, u32[]{:S(2)}) collective-permute-start(f32[4,16,128]{2,1,0:T(8,128)} %get-tuple-element.11), channel_id=1, source_target_pairs={{0,8},{8,16},{16,24},{24,32},{32,40},{40,48},{48,56},{56,64},{64,7... | collective-permute-start | bytes 98312 | tf_op jit(solution)/shard_map/ppermute | solution.py:426
  8.6 1.3 %collective-permute-done.low = f32[4,16,128]{2,1,0:T(8,128)S(1)} collective-permute-done((f32[4,16,128]{2,1,0:T(8,128)}, f32[4,16,128]{2,1,0:T(8,128)S(1)}, u32[]{:S(2)}, u32[]{:S(2)}) %collective-permute-start) | collective-permute-done | bytes 32800 | tf_op jit(solution)/shard_map/ppermute | solution.py:426
  9.9 0.0 copy-start.2
  9.9 0.0 collective-permute-done.1.high
  9.9 0.6 copy-done.2
  10.5 0.6 copy-done.1
  11.2 6.2 %advance_velocity.1 = (f32[3,16,64,128]{3,2,1,0:T(8,128)}, f32[80,128]{1,0:T(8,128)}, f32[80,128]{1,0:T(8,128)}) custom-call(f32[3]{0:T(128)} %buoy.5, f32[6,16,64,128]{3,2,1,0:T(8,128)} %stress.3, f32[3,16,64,128]{3,2,1,0:T(8,128)} %veloc.1, s32[16,64,128]{2,1,0:T(8,128)} %material.3, f32[4,16,128]{2,1,0:T(8,128)} %copy-done.2, f32[6,16,128]{2,1,0:T(8,128)} %copy-done.1), custom_call_target="tpu_custom_call" | custom-call | flops 1000000 | bytes 6979596 | tf_op jit(solution)/shard_map/advance_velocity/pallas_call | solution.py:388
  17.3 5.4 %collective-permute-start.2 = (f32[80,128]{1,0:T(8,128)}, f32[80,128]{1,0:T(8,128)S(1)}, u32[]{:S(2)}, u32[]{:S(2)}) collective-permute-start(f32[80,128]{1,0:T(8,128)} %get-tuple-element.14.own_right), channel_id=1, source_target_pairs={{0,1},{1,2},{2,3},{3,4},{4,5},{5,6},{6,7},{8,9},{9,10},{10,11},{11... | collective-permute-start | bytes 122888 | tf_op jit(solution)/shard_map/ppermute | solution.py:435
  22.7 1.9 %collective-permute-start.3 = (f32[80,128]{1,0:T(8,128)}, f32[80,128]{1,0:T(8,128)S(1)}, u32[]{:S(2)}, u32[]{:S(2)}) collective-permute-start(f32[80,128]{1,0:T(8,128)} %get-tuple-element.15.own_left), channel_id=1, source_target_pairs={{1,0},{2,1},{3,2},{4,3},{5,4},{6,5},{7,6},{9,8},{10,9},{11,10},{12... | collective-permute-start | bytes 122888 | tf_op jit(solution)/shard_map/ppermute | solution.py:436
  24.6 0.0 collective-permute-done.2.from_left
  24.6 0.0 copy-start.3
  24.7 3.6 %collective-permute-done.3.from_right = f32[80,128]{1,0:T(8,128)S(1)} collective-permute-done((f32[80,128]{1,0:T(8,128)}, f32[80,128]{1,0:T(8,128)S(1)}, u32[]{:S(2)}, u32[]{:S(2)}) %collective-permute-start.3) | collective-permute-done | bytes 40992 | tf_op jit(solution)/shard_map/ppermute | solution.py:436
  28.2 0.0 copy-done.3
  28.2 0.6 copy-done.4
  28.9 6.4 %advance_stress.1 = (f32[6,16,64,128]{3,2,1,0:T(8,128)}, f32[3,16,64,128]{3,2,1,0:T(8,128)}, f32[16,64,128]{2,1,0:T(8,128)}) custom-call(f32[3]{0:T(128)} %buoy.5, f32[3]{0:T(128)} %lame.1, f32[3]{0:T(128)} %shear.1, f32[3]{0:T(128)} %piezo.1, f32[6,16,64,128]{3,2,1,0:T(8,128)} %stress.3, f32[3,16,64,128]{3,2,1,0:T(8,128)} %get-tuple-element.13.part, ...), custom_call_target="tpu_custom_call" | custom-call | flops 1000000 | bytes 10731568 | tf_op jit(solution)/shard_map/advance_stress/pallas_call | solution.py:388
  35.3 19.2 %all_to_all.10 = f32[16,64,128]{2,1,0:T(8,128)} all-to-all(f32[16,64,128]{2,1,0:T(8,128)} %get-tuple-element.18), channel_id=1, replica_groups=mesh['gx'=32,'gy'=8] {'gy'}, dimensions={0} | all-to-all | bytes 1048576 | tf_op jit(solution)/shard_map/all_to_all | solution.py:447
  54.5 3.3 %transform_y.1 = f32[2048,128]{1,0:T(8,128)} custom-call(f32[8,2,64,128]{3,2,1,0:T(8,128)} %bitcast.5, bf16[256,256]{1,0:T(8,128)(2,1)} %constant.14.clone.w_high, bf16[256,256]{1,0:T(8,128)(2,1)} %constant.15.clone.w_low, f32[16,128]{1,0:T(8,128)} %constant.16.clone.twiddle), custom_call_target="tpu_custom_call" | custom-call | flops 1000000 | bytes 2105344 | tf_op jit(solution)/shard_map/transform_y/pallas_call | solution.py:388
  57.8 21.8 %all-to-all-start.1 = ((f32[256,8,128]{2,1,0:T(8,128)}), f32[256,8,128]{2,1,0:T(8,128)S(1)}, u32[]{:S(2)}, u32[]{:S(2)}) async-start(f32[256,8,128]{2,1,0:T(8,128)} %bitcast.3), calls=%async_computation.1 | async-start | bytes 2097152 | tf_op jit(solution)/shard_map/all_to_all | solution.py:456
  79.6 2.0 %pivots.1.inverse = f32[16,8,2048]{2,1,0:T(8,128)} custom-call(s32[16]{0:T(128)} %layer_kind.3, f32[3]{0:T(128)} %lateral.3, f32[3]{0:T(128)} %normal.3, f32[1,2048]{1,0:T(1,128)} %constant.17.clone.wave_x), custom_call_target="tpu_custom_call" | custom-call | flops 1000000 | bytes 1056856 | tf_op jit(solution)/shard_map/pivots/pallas_call | solution.py:388
  81.7 28.9 %all-to-all-done.1 = f32[256,8,128]{2,1,0:T(8,128)S(1)} async-done(((f32[256,8,128]{2,1,0:T(8,128)}), f32[256,8,128]{2,1,0:T(8,128)S(1)}, u32[]{:S(2)}, u32[]{:S(2)}) %all-to-all-start.1) | async-done | bytes 1048608 | tf_op jit(solution)/shard_map/all_to_all | solution.py:456
  110.6 1.0 copy-done
  111.5 3.6 %solve.1 = f32[2,16,4,2048]{3,2,1,0:T(4,128)} custom-call(s32[16]{0:T(128)} %layer_kind.3, f32[3]{0:T(128)} %lateral.3, f32[3]{0:T(128)} %normal.3, f32[32,8,8,128]{3,2,1,0:T(8,128)} %bitcast.4, bf16[256,256]{1,0:T(8,128)(2,1)} %constant.18.clone.w_high, bf16[256,256]{1,0:T(8,128)(2,1)} %constant.19.clone.w_low, f32[32,128]{1,0:T(8,128)} %constant.20.clone.twiddle, ...), custom_call_target="tpu_custom_call" | custom-call | flops 1000000 | bytes 3686488 | tf_op jit(solution)/shard_map/solve/pallas_call | solution.py:388
  (3 shorter events, 0.0 us)
Async XLA Ops:
  2.7 7.3 %collective-permute-start.1 = (f32[6,16,128]{2,1,0:T(8,128)}, f32[6,16,128]{2,1,0:T(8,128)S(1)}, u32[]{:S(2)}, u32[]{:S(2)}) collective-permute-start(f32[6,16,128]{2,1,0:T(8,128)} %get-tuple-element.12), channel_id=1, source_target_pairs={{8,0},{16,8},{24,16},{32,24},{40,32},{48,40},{56,48},{64,56},{72,6... | collective-permute-start | bytes 147464 | tf_op jit(solution)/shard_map/ppermute | solution.py:427
  3.9 6.0 %collective-permute-start = (f32[4,16,128]{2,1,0:T(8,128)}, f32[4,16,128]{2,1,0:T(8,128)S(1)}, u32[]{:S(2)}, u32[]{:S(2)}) collective-permute-start(f32[4,16,128]{2,1,0:T(8,128)} %get-tuple-element.11), channel_id=1, source_target_pairs={{0,8},{8,16},{16,24},{24,32},{32,40},{40,48},{48,56},{56,64},{64,7... | collective-permute-start | bytes 98312 | tf_op jit(solution)/shard_map/ppermute | solution.py:426
  9.9 0.6 copy-start.2
  10.5 0.6 copy-start.1
  17.3 7.3 %collective-permute-start.2 = (f32[80,128]{1,0:T(8,128)}, f32[80,128]{1,0:T(8,128)S(1)}, u32[]{:S(2)}, u32[]{:S(2)}) collective-permute-start(f32[80,128]{1,0:T(8,128)} %get-tuple-element.14.own_right), channel_id=1, source_target_pairs={{0,1},{1,2},{2,3},{3,4},{4,5},{5,6},{6,7},{8,9},{9,10},{10,11},{11... | collective-permute-start | bytes 122888 | tf_op jit(solution)/shard_map/ppermute | solution.py:435
  22.7 5.5 %collective-permute-start.3 = (f32[80,128]{1,0:T(8,128)}, f32[80,128]{1,0:T(8,128)S(1)}, u32[]{:S(2)}, u32[]{:S(2)}) collective-permute-start(f32[80,128]{1,0:T(8,128)} %get-tuple-element.15.own_left), channel_id=1, source_target_pairs={{1,0},{2,1},{3,2},{4,3},{5,4},{6,5},{7,6},{9,8},{10,9},{11,10},{12... | collective-permute-start | bytes 122888 | tf_op jit(solution)/shard_map/ppermute | solution.py:436
  24.6 3.6 %copy-start.3 = (f32[80,128]{1,0:T(8,128)}, f32[80,128]{1,0:T(8,128)S(1)}, u32[]{:S(2)}) copy-start(f32[80,128]{1,0:T(8,128)S(1)} %collective-permute-done.2.from_left) | copy-start | bytes 122884
  28.2 0.6 copy-start.4
  57.8 52.8 %all-to-all-start.1 = ((f32[256,8,128]{2,1,0:T(8,128)}), f32[256,8,128]{2,1,0:T(8,128)S(1)}, u32[]{:S(2)}, u32[]{:S(2)}) async-start(f32[256,8,128]{2,1,0:T(8,128)} %bitcast.3), calls=%async_computation.1 | async-start | bytes 2097152 | tf_op jit(solution)/shard_map/all_to_all | solution.py:456
  110.6 1.0 copy-start

commit v2 on v1

--- a/solution.py
+++ b/solution.py
@@ -117,45 +117,79 @@
     return jnp.where(rows(values) == 0, 0.0, moved)
 
 
-def edge_rows(buoy, stress_first, stress_end, veloc_first, veloc_end, mat_first, mat_end, down_ref, up_ref):
+def odd(axis):
+    return lax.axis_index(axis) % 2 == 1
+
+
+def low_high(axis, first, second):
+    is_odd = odd(axis)
+    low = [jnp.where(is_odd, first[c], second[c]) for c in range(first.shape[0])]
+    high = [jnp.where(is_odd, second[c], first[c]) for c in range(first.shape[0])]
+    return low, high
+
+
+def edge_rows(buoy, stress_first, stress_end, veloc_first, veloc_end, mat_first, mat_end, first, second):
     sxx, sxy, sxz = (stress_end[c, :, 7, :] for c in (0, 3, 4))
     b = pick(mat_end[:, 7, :], buoy)
-    down_ref[0] = veloc_end[0, :, 7, :] + b * ((sxy - last_lane(sxy)) + (sxz - last_layer(sxz)) - sxx)
-    down_ref[1] = b
-    down_ref[2] = sxy
-    down_ref[3] = sxz
+    ux = veloc_end[0, :, 7, :] + b * ((sxy - last_lane(sxy)) + (sxz - last_layer(sxz)) - sxx)
+    down = [ux, b, sxy, sxz, jnp.zeros_like(b), jnp.zeros_like(b)]
     sxx, syy, szz, sxy, sxz, syz = (stress_first[c, :, 0, :] for c in range(6))
     b = pick(mat_first[:, 0, :], buoy)
-    up_ref[0] = veloc_first[1, :, 0, :] + b * (sxy + (next_lane(syy) - syy) + (syz - last_layer(syz)))
-    up_ref[1] = veloc_first[2, :, 0, :] + b * (sxz + (syz - last_lane(syz)) + (next_layer(szz) - szz))
-    up_ref[2] = b
-    up_ref[3] = sxx
-    up_ref[4] = syy
-    up_ref[5] = syz
-
-
-def advance_velocity(buoy, stress, veloc, material, low, high, new, right_ref, left_ref):
+    uy = veloc_first[1, :, 0, :] + b * (sxy + (next_lane(syy) - syy) + (syz - last_layer(syz)))
+    uz = veloc_first[2, :, 0, :] + b * (sxz + (syz - last_lane(syz)) + (next_layer(szz) - szz))
+    up = [uy, uz, b, sxx, syy, syz]
+    is_odd = odd("gx")
+    for c in range(6):
+        first[c] = jnp.where(is_odd, up[c], down[c])
+        second[c] = jnp.where(is_odd, down[c], up[c])
+
+
+CHUNK = 2
+
+
+def copies(pairs, sems):
+    made = []
+    for k in range(NZ // CHUNK):
+        at = pl.ds(k * CHUNK, CHUNK)
+        made.append([])
+        for n, (source, target) in enumerate(pairs):
+            index = (at,) if len(source.shape) == 3 else (slice(None), at)
+            made[-1].append(pltpu.make_async_copy(source.at[index], target.at[index], sems.at[k, n]))
+    return made
+
+
+def advance_velocity(
+    buoy, stress_in, veloc_in, material_in, new_out, right_ref, left_ref,
+    stress, veloc, material, new, in_sems, out_sems,
+):
+    arriving = copies([(stress_in, stress), (veloc_in, veloc), (material_in, material)], in_sems)
+    leaving = copies([(new, new_out)], out_sems)
+    for chunk in arriving:
+        for copy in chunk:
+            copy.start()
     column = lax.broadcasted_iota(jnp.int32, (BX, BY), 1)
     right = jnp.zeros((BX, BY), jnp.float32)
     left = jnp.zeros((BX, BY), jnp.float32)
+    ready = 0
     for z in range(NZ):
+        while ready < min(z + 2, NZ):
+            for copy in arriving[ready // CHUNK]:
+                copy.wait()
+            ready += CHUNK
         sxx, syy, szz, sxy, sxz, syz = (stress[c, z] for c in range(6))
         b = pick(material[z], buoy)
         dz_sxz = sxz - stress[4, z - 1] if z else sxz
         dz_syz = syz - stress[5, z - 1] if z else syz
         dz_szz = stress[2, z + 1] - szz if z < NZ - 1 else -szz
-        ux = veloc[0, z] + b * (
-            (next_row(sxx, high[3, z : z + 1]) - sxx) + (sxy - last_lane(sxy)) + dz_sxz
-        )
-        uy = veloc[1, z] + b * (
-            (sxy - last_row(sxy, low[2, z : z + 1])) + (next_lane(syy) - syy) + dz_syz
-        )
-        uz = veloc[2, z] + b * (
-            (sxz - last_row(sxz, low[3, z : z + 1])) + (syz - last_lane(syz)) + dz_szz
-        )
+        ux = veloc[0, z] + b * ((next_row(sxx, 0.0) - sxx) + (sxy - last_lane(sxy)) + dz_sxz)
+        uy = veloc[1, z] + b * ((sxy - last_row(sxy, 0.0)) + (next_lane(syy) - syy) + dz_syz)
+        uz = veloc[2, z] + b * ((sxz - last_row(sxz, 0.0)) + (syz - last_lane(syz)) + dz_szz)
         new[0, z] = ux
         new[1, z] = uy
         new[2, z] = uz
+        if z % CHUNK == CHUNK - 1:
+            for copy in leaving[z // CHUNK]:
+                copy.start()
         for part, value in enumerate((uy, b, sxy, syz)):
             spot = part * NZ + z
             moved = pltpu.roll(value, (spot + 1) % BY, 1)
@@ -164,23 +198,65 @@
             spot = part * NZ + z
             moved = pltpu.roll(value, spot, 1) if spot else value
             left = jnp.where(column == spot, moved, left)
-    right_ref[:BX] = right
-    left_ref[:BX] = left
-    corner = column[:NZ]
-    right_ref[BX:] = jnp.where(
+    right_ref[...] = right
+    left_ref[...] = left
+    for chunk in leaving:
+        for copy in chunk:
+            copy.wait()
+
+
+def edge_columns(right_ref, left_ref, x_first, x_second, first, second):
+    low, high = low_high("gx", x_first, x_second)
+    corner = lax.broadcasted_iota(jnp.int32, (NZ, BY), 1)
+    layer = lax.broadcasted_iota(jnp.int32, (NZ, BY), 0)
+    row = lax.broadcasted_iota(jnp.int32, (BX, BY), 0)
+    column = lax.broadcasted_iota(jnp.int32, (BX, BY), 1)
+
+    def line(values, spot, at):
+        wide = jnp.broadcast_to(values[:, spot : spot + 1], (NZ, BY))
+        return jnp.sum(jnp.where(corner == layer + at, wide, 0.0), axis=0, keepdims=True)
+
+    def shifted(values, by):
+        return pltpu.roll(values, (-by * NZ) % BY, 1)
+
+    right, left = right_ref[...], left_ref[...]
+    right_b = shifted(right, 1)
+    right = right - jnp.where((row == 0) & (column < NZ), right_b * line(low[2], BY - 1, 0), 0.0)
+    left_b = jnp.where(column < NZ, shifted(left, 2), shifted(left, 1))
+    left = left + jnp.where((row == BX - 1) & (column < NZ), left_b * line(high[3], 0, 0), 0.0)
+    left = left - jnp.where(
+        (row == 0) & (column >= NZ) & (column < 2 * NZ), left_b * line(low[3], 0, NZ), 0.0
+    )
+    right_corner = jnp.where(
         corner == 0, pltpu.roll(low[2], 1, 1), jnp.where(corner == 1, pltpu.roll(high[5], 2, 1), 0.0)
     )
-    left_ref[BX:] = jnp.where(corner == 0, high[4], 0.0)
+    left_corner = jnp.where(corner == 0, high[4], 0.0)
+    is_odd = odd("gy")
+    first[:BX] = jnp.where(is_odd, left, right)
+    first[BX:] = jnp.where(is_odd, left_corner, right_corner)
+    second[:BX] = jnp.where(is_odd, right, left)
+    second[BX:] = jnp.where(is_odd, right_corner, left_corner)
 
 
 def advance_stress(
-    buoy, lame, shear, piezo, stress, part, material, low, high,
-    own_right, own_left, from_left, from_right, new_stress, new_veloc, charge,
+    buoy, lame, shear, piezo, stress_in, part_in, material_in, x_first, x_second,
+    own_right, own_left, y_first, y_second, stress_out, veloc_out, charge_out,
+    stress, part, material, new_stress, new_veloc, charge, in_sems, out_sems,
 ):
+    arriving = copies([(stress_in, stress), (part_in, part), (material_in, material)], in_sems)
+    leaving = copies([(charge, charge_out), (new_stress, stress_out), (new_veloc, veloc_out)], out_sems)
+    for chunk in arriving:
+        for copy in chunk:
+            copy.start()
     lane = lax.broadcasted_iota(jnp.int32, (BX, BY), 1)
     corner_lane = lane[:NZ]
+    row8 = lax.broadcasted_iota(jnp.int32, (8, BY), 0)
+    low, high = low_high("gx", x_first, x_second)
+    y_odd = odd("gy")
+    from_left = jnp.where(y_odd, y_first[...], y_second[...])
+    from_right = jnp.where(y_odd, y_second[...], y_first[...])
     west, east = from_left[:BX], from_right[:BX]
-    mine_east, mine_west = own_right[:BX], own_left[:BX]
+    mine_east, mine_west = own_right[...], own_left[...]
 
     def shifted(values, by):
         return pltpu.roll(values, (-by * NZ) % BY, 1)
@@ -196,18 +272,42 @@
     def beside(values, spot):
         return jnp.broadcast_to(values[:, spot : spot + 1], (BX, BY))
 
-    for z in range(NZ):
+    def at_top(values, added):
+        head = values[:8] + jnp.where(row8 == 0, added, 0.0)
+        return jnp.concatenate([head, values[8:]], axis=0)
+
+    def at_end(values, added):
+        tail = values[BX - 8 :] + jnp.where(row8 == 7, added, 0.0)
+        return jnp.concatenate([values[: BX - 8], tail], axis=0)
+
+    def close_edges(z):
         b = pick(material[z], buoy)
-        new_veloc[0, z] = part[0, z] - jnp.where(lane == 0, b * beside(west, 2 * NZ + z), 0.0)
-        new_veloc[1, z] = part[1, z] + jnp.where(lane == BY - 1, b * beside(east, 3 * NZ + z), 0.0)
-        new_veloc[2, z] = part[2, z] - jnp.where(lane == 0, b * beside(west, 3 * NZ + z), 0.0)
-    for z in range(NZ):
+        row = slice(z, z + 1)
+        head, tail = b[:8], b[BX - 8 :]
+        ux = part[0, z] - jnp.where(lane == 0, b * beside(west, 2 * NZ + z), 0.0)
+        uy = part[1, z] + jnp.where(lane == BY - 1, b * beside(east, 3 * NZ + z), 0.0)
+        uz = part[2, z] - jnp.where(lane == 0, b * beside(west, 3 * NZ + z), 0.0)
+        new_veloc[0, z] = at_end(ux, tail * high[3][row])
+        new_veloc[1, z] = at_top(uy, -(head * low[2][row]))
+        new_veloc[2, z] = at_top(uz, -(head * low[3][row]))
+
+    ready = 0
+    for step in range(NZ + 1):
+        if step < NZ:
+            while ready <= step:
+                for copy in arriving[ready // CHUNK]:
+                    copy.wait()
+                ready += CHUNK
+            close_edges(step)
+        if step == 0:
+            continue
+        z = step - 1
         sxx, syy, szz, sxy, sxz, syz = (stress[c, z] for c in range(6))
         ux, uy, uz = (new_veloc[c, z] for c in range(3))
         codes = material[z]
         lam, mu, e = pick(codes, lame), pick(codes, shear), pick(codes, piezo)
         row = slice(z, z + 1)
-        ex = ux - last_row(ux, ux_low[row] + low[1, row] * sxx[0:1])
+        ex = ux - last_row(ux, ux_low[row] + low[1][row] * sxx[0:1])
         ey = uy - jnp.where(lane == 0, beside(uy_west, z), pltpu.roll(uy, 1, 1))
         ez = uz - new_veloc[2, z - 1] if z else uz
         lam_div = lam * (ex + ey + ez)
@@ -215,7 +315,7 @@
         new_stress[0, z] = sxx + lam_div + mu2 * ex
         new_stress[1, z] = syy + lam_div + mu2 * ey
         new_stress[2, z] = szz + lam_div + mu2 * ez
-        b_high = high[2, row]
+        b_high = high[2][row]
         dx_uy = next_row(uy, uy_high[row] - b_high * sxy[BX - 1 : BX]) - uy
         dx_uz = next_row(uz, uz_high[row] - b_high * sxz[BX - 1 : BX]) - uz
         last = lane == BY - 1
@@ -229,6 +329,12 @@
         new_stress[4, z] = new_sxz
         new_stress[5, z] = new_syz
         charge[z] = e * (new_sxz + new_syz)
+        if z % CHUNK == CHUNK - 1:
+            for copy in leaving[z // CHUNK]:
+                copy.start()
+    for chunk in leaving:
+        for copy in chunk:
+            copy.wait()
 
 
 ROOT = math.sqrt(0.5)
@@ -380,9 +486,10 @@
 
 SMEM = pl.BlockSpec(memory_space=pltpu.SMEM)
 VMEM = pl.BlockSpec(memory_space=pltpu.VMEM)
-
-
-def call(body, name, outs, in_specs, args, scratch=(), flops=1_000_000, grid_spec=None):
+ANY = pl.BlockSpec(memory_space=pl.ANY)
+
+
+def call(body, name, outs, in_specs, args, scratch=(), out_specs=None, flops=1_000_000):
     shapes = [jax.ShapeDtypeStruct(shape, jnp.float32) for shape in outs]
     moved = sum(4 * math.prod(shape) for shape in outs) + sum(4 * v.size for v in args)
     return pl.pallas_call(
@@ -390,7 +497,7 @@
         name=name,
         out_shape=shapes,
         in_specs=in_specs,
-        out_specs=[VMEM] * len(outs),
+        out_specs=out_specs or [VMEM] * len(outs),
         scratch_shapes=list(scratch),
         compiler_params=pltpu.CompilerParams(vmem_limit_bytes=VMEM_LIMIT),
         cost_estimate=pl.CostEstimate(flops=flops, bytes_accessed=moved, transcendentals=0),
@@ -401,48 +508,72 @@
     end = BX // 8 - 1
     block4 = lambda count, at: pl.BlockSpec((count, NZ, 8, BY), lambda i: (0, 0, at, 0))
     block3 = lambda at: pl.BlockSpec((NZ, 8, BY), lambda i: (0, at, 0))
-    whole = lambda count: pl.BlockSpec((count, NZ, BY), lambda i: (0, 0, 0))
+    whole = pl.BlockSpec((6, NZ, BY), lambda i: (0, 0, 0))
     return pl.pallas_call(
         edge_rows,
         name="edge_rows",
         grid=(1,),
-        out_shape=[jax.ShapeDtypeStruct((count, NZ, BY), jnp.float32) for count in (4, 6)],
+        out_shape=[jax.ShapeDtypeStruct((6, NZ, BY), jnp.float32)] * 2,
         in_specs=[SMEM, block4(6, 0), block4(6, end), block4(3, 0), block4(3, end), block3(0), block3(end)],
-        out_specs=[whole(4), whole(6)],
+        out_specs=[whole, whole],
         compiler_params=pltpu.CompilerParams(vmem_limit_bytes=VMEM_LIMIT),
     )(buoyancy, stress, stress, velocity, velocity, material, material)
+
+
+def field(count, dtype=jnp.float32):
+    shape = (NZ, BX, BY)
+    return pltpu.VMEM(shape if count == 1 else (count, *shape), dtype)
+
+
+def swaps(axis, first, second):
+    def pairs(start):
+        both = [(i, i + 1) for i in range(start, lax.axis_size(axis) - 1, 2)]
+        return both + [(b, a) for a, b in both]
+
+    second = lax.ppermute(second, axis, pairs(1))
+    return lax.ppermute(first, axis, pairs(0)), second
 
 
 def per_device(
     stress, velocity, material, layer_kind, buoyancy, lame_first, shear_modulus, piezo, permit_lateral, permit_normal
 ):
-    def chain(count):
-        forward = [(i, i + 1) for i in range(count - 1)]
-        return forward, [(target, source) for source, target in forward]
-
-    down, up = chain(DX)
-    right, left = chain(DY)
-    to_next, to_previous = edge_call(buoyancy, stress, velocity, material)
-    low = lax.ppermute(to_next, "gx", down)
-    high = lax.ppermute(to_previous, "gx", up)
+    chunks = NZ // CHUNK
+    sems = lambda count: pltpu.SemaphoreType.DMA((chunks, count))
+    x_edges = swaps("gx", *edge_call(buoyancy, stress, velocity, material))
     part, own_right, own_left = call(
         advance_velocity,
         "advance_velocity",
-        [(3, NZ, BX, BY), (BX + NZ, BY), (BX + NZ, BY)],
-        [SMEM] + [VMEM] * 5,
-        (buoyancy, stress, velocity, material, low, high),
-    )
-    from_left = lax.ppermute(own_right, "gy", right)
-    from_right = lax.ppermute(own_left, "gy", left)
+        [(3, NZ, BX, BY), (BX, BY), (BX, BY)],
+        [SMEM] + [ANY] * 3,
+        (buoyancy, stress, velocity, material),
+        [field(6), field(3), field(1, jnp.int32), field(3), sems(3), sems(1)],
+        [ANY, VMEM, VMEM],
+    )
+    y_edges = call(
+        edge_columns, "edge_columns", [(BX + NZ, BY)] * 2, [VMEM] * 4, (own_right, own_left, *x_edges)
+    )
+    y_edges = swaps("gy", *y_edges)
+    scalars = (layer_kind, permit_lateral, permit_normal)
+    own_right, layer_kind = lax.optimization_barrier((own_right, layer_kind))
+    inverse, = call(
+        pivots,
+        "pivots",
+        [(NZ, 8, NX)],
+        [SMEM] * 3 + [VMEM],
+        (layer_kind, permit_lateral, permit_normal, jnp.asarray(table_wave())),
+    )
+    own_right, inverse = lax.optimization_barrier((own_right, inverse))
     stress_next, velocity_next, charge = call(
         advance_stress,
         "advance_stress",
         [(6, NZ, BX, BY), (3, NZ, BX, BY), (NZ, BX, BY)],
-        [SMEM] * 4 + [VMEM] * 9,
+        [SMEM] * 4 + [ANY] * 3 + [VMEM] * 6,
         (
-            buoyancy, lame_first, shear_modulus, piezo, stress, part, material, low, high,
-            own_right, own_left, from_left, from_right,
+            buoyancy, lame_first, shear_modulus, piezo, stress, part, material,
+            *x_edges, own_right, own_left, *y_edges,
         ),
+        [field(6), field(3), field(1, jnp.int32), field(6), field(3), field(1), sems(3), sems(3)],
+        [ANY] * 3,
     )
     charge = lax.all_to_all(charge, "gy", 0, 0, tiled=True).reshape(DY, 2, BX, BY)
     modes, = call(
@@ -454,10 +585,6 @@
         [pltpu.VMEM((1024, 128), jnp.float32)] * 2,
     )
     lines = lax.all_to_all(modes.reshape(DX * DY, 8, 128), ("gx", "gy"), 0, 0, tiled=True)
-    scalars = (layer_kind, permit_lateral, permit_normal)
-    inverse, = call(
-        pivots, "pivots", [(NZ, 8, NX)], [SMEM] * 3 + [VMEM], (*scalars, jnp.asarray(table_wave()))
-    )
     potential_modes, = call(
         solve,
         "solve",
@@ -470,11 +597,11 @@
 
 
 def solution(mesh):
-    field = P(None, None, "gx", "gy")
+    spread = P(None, None, "gx", "gy")
     return jax.shard_map(
         per_device,
         mesh=mesh,
-        in_specs=(field, field, P(None, "gx", "gy")) + (P(),) * 7,
-        out_specs=(field, field, P(None, None, ("gx", "gy"), None)),
+        in_specs=(spread, spread, P(None, "gx", "gy")) + (P(),) * 7,
+        out_specs=(spread, spread, P(None, None, ("gx", "gy"), None)),
         check_vma=False,
     )

time: 116 us -> 101 us (0.87)
  blocking collectives: 19.2 us -> 66.9 us
  waiting for transfers between devices: 33.8 us -> 0.24 us
  starting transfers between devices: 35 us -> 7.15 us
  local copies, waits for them, and re-layouts: 2.82 us -> 1.24 us
    all_to_all x0 -> x1, blocking collectives: none -> 46.7 us  [per_device(): lax.all_to_all(modes.reshape(DX * DY, 8, 128), ('gx', 'gy'), 0, 0, tiled=...]
    all_to_all x1 -> x0, waiting for transfers between devices: 28.9 us -> none  [per_device(): lax.all_to_all(modes.reshape(DX * DY, 8, 128), ('gx', 'gy'), 0, 0, tiled=...]
    all_to_all x1 -> x0, starting transfers between devices: 21.8 us -> none  [per_device(): lax.all_to_all(modes.reshape(DX * DY, 8, 128), ('gx', 'gy'), 0, 0, tiled=...]
    ppermute x4, starting transfers between devices: 13.2 us -> 7.15 us  [the longest x2 3.91 us: swaps(): second = lax.ppermute(second, axis, pairs(1))]
    ppermute x4, waiting for transfers between devices: 4.91 us -> 0.24 us  [the longest x2 0.23 us: swaps(): second = lax.ppermute(second, axis, pairs(1))]
    unnamed x10 -> x8, local copies, waits for them, and re-layouts: 2.82 us -> 1.24 us
    pallas_call x5 -> x6, Pallas kernels: 21.6 us -> 21.9 us  [call(): pl.pallas_call(body, name=name, out_shape=shapes, in_specs=in_specs, out_...]
  transfers between devices with their start and end apart: 5 -> 4, of which waited for: 3 -> 1; matrix products, arithmetic and copies ran while one was open for 0% -> 0% of each run, Pallas kernels for 2% -> 8%
where the time goes in v2:
time: 101 us; the launch traced here: 100 us
  blocking collectives  66.9 us (66%)
  Pallas kernels  23.9 us (24%)
  starting transfers between devices  7.15 us (7%)
  local copies, waits for them, and re-layouts  1.24 us (1%)
    all_to_all x1, blocking collectives, per_device(): lax.all_to_all(modes.reshape(DX * DY, 8, 128), ('gx', 'gy'), 0, 0, tiled=...  46.7 us
    pallas_call x6, Pallas kernels, call(): pl.pallas_call(body, name=name, out_shape=shapes, in_specs=in_specs, out_...  21.9 us
    all_to_all x1, blocking collectives, per_device(): lax.all_to_all(charge, 'gy', 0, 0, tiled=True).reshape(DY, 2, BX, BY)  20.2 us
    ppermute x2, starting transfers between devices, swaps(): second = lax.ppermute(second, axis, pairs(1))  3.91 us
    ppermute x2, starting transfers between devices, swaps(): return (lax.ppermute(first, axis, pairs(0)), second)  3.24 us
    pallas_call x1, Pallas kernels, edge_call(): pl.pallas_call(edge_rows, name='edge_rows', grid=(1,), out_shape=[jax.Sha...  2.08 us
  transfers between devices with their start and end apart: 4, of which 1 were waited for; matrix products, arithmetic and copies ran while one was open for 0% of the time, Pallas kernels for 8%

profile of v2, /device:TPU:1, one launch (start us, length us, event | category | flops | bytes accessed | tf_op | source)
XLA Modules:
  0.0 100.1 jit_solution(15337168674806454225)
XLA Ops:
  0.6 2.1 %edge_rows.1 = (f32[6,16,128]{2,1,0:T(8,128)}, f32[6,16,128]{2,1,0:T(8,128)}) custom-call(f32[3]{0:T(128)} %buoy.5, f32[6,16,64,128]{3,2,1,0:T(8,128)} %stress_in.3, f32[6,16,64,128]{3,2,1,0:T(8,128)} %stress_in.3, f32[3,16,64,128]{3,2,1,0:T(8,128)} %veloc_end.1, f32[3,16,64,128]{3,2,1,0:T(8,128)} %veloc_end.1, s32[16,64,128]{2,1,0:T(8,128)} %material_in.3, ...), custom_call_target="tpu_custom_call" | custom-call | tf_op jit(solution)/shard_map/edge_rows/pallas_call | solution.py:512
  2.7 2.1 %collective-permute-start = (f32[6,16,128]{2,1,0:T(8,128)}, f32[6,16,128]{2,1,0:T(8,128)S(1)}, u32[]{:S(2)}, u32[]{:S(2)}) collective-permute-start(f32[6,16,128]{2,1,0:T(8,128)} %get-tuple-element.18), channel_id=1, source_target_pairs={{0,8},{16,24},{32,40},{48,56},{64,72},{80,88},{96,104},{112,120},{... | collective-permute-start | bytes 147464 | tf_op jit(solution)/shard_map/ppermute | solution.py:534
  4.8 0.7 collective-permute-start.1
  5.5 6.0 %advance_velocity.1 = (f32[3,16,64,128]{3,2,1,0:T(8,128)}, f32[64,128]{1,0:T(8,128)}, f32[64,128]{1,0:T(8,128)}) custom-call(f32[3]{0:T(128)} %buoy.5, f32[6,16,64,128]{3,2,1,0:T(8,128)} %stress_in.3, f32[3,16,64,128]{3,2,1,0:T(8,128)} %veloc_end.1, s32[16,64,128]{2,1,0:T(8,128)} %material_in.3), custom_call_target="tpu_custom_call" | custom-call | flops 1000000 | bytes 6881292 | tf_op jit(solution)/shard_map/advance_velocity/pallas_call | solution.py:495
  11.5 0.0 collective-permute-done.x_first
  11.5 0.0 copy-start
  11.5 0.0 collective-permute-done.1.x_second
  11.5 0.0 copy-start.1
  11.5 0.6 copy-done
  12.1 0.0 copy-done.1
  12.1 1.6 %edge_columns.1 = (f32[80,128]{1,0:T(8,128)}, f32[80,128]{1,0:T(8,128)}) custom-call(f32[64,128]{1,0:T(8,128)} %get-tuple-element.23.right_ref.own_right, f32[64,128]{1,0:T(8,128)} %get-tuple-element.24.left_ref.own_left, f32[6,16,128]{2,1,0:T(8,128)} %copy-done, f32[6,16,128]{2,1,0:T(8,128)} %copy-done.1), custom_call_target="tpu_custom_call" | custom-call | flops 1000000 | bytes 245760 | tf_op jit(solution)/shard_map/edge_columns/pallas_call | solution.py:495
  13.7 1.1 %collective-permute-start.2 = (f32[80,128]{1,0:T(8,128)}, f32[80,128]{1,0:T(8,128)S(1)}, u32[]{:S(2)}, u32[]{:S(2)}) collective-permute-start(f32[80,128]{1,0:T(8,128)} %get-tuple-element.25), channel_id=1, source_target_pairs={{0,1},{2,3},{4,5},{6,7},{1,0},{3,2},{5,4},{7,6},{8,9},{10,11},{12,... | collective-permute-start | bytes 122888 | tf_op jit(solution)/shard_map/ppermute | solution.py:534
  14.8 3.3 %collective-permute-start.3 = (f32[80,128]{1,0:T(8,128)}, f32[80,128]{1,0:T(8,128)S(1)}, u32[]{:S(2)}, u32[]{:S(2)}) collective-permute-start(f32[80,128]{1,0:T(8,128)} %get-tuple-element.26), channel_id=1, source_target_pairs={{1,2},{3,4},{5,6},{2,1},{4,3},{6,5},{9,10},{11,12},{13,14},{10,9},... | collective-permute-start | bytes 122888 | tf_op jit(solution)/shard_map/ppermute | solution.py:533
  18.1 2.0 %pivots.1.inverse = f32[16,8,2048]{2,1,0:T(8,128)} custom-call(s32[16]{0:T(128)} %layer_kind.2, f32[3]{0:T(128)} %lateral.3, f32[3]{0:T(128)} %normal.3, f32[1,2048]{1,0:T(1,128)} %constant.14.clone.wave_x), custom_call_target="tpu_custom_call" | custom-call | flops 1000000 | bytes 1056856 | tf_op jit(solution)/shard_map/pivots/pallas_call | solution.py:495
  20.1 0.0 collective-permute-done.2.y_first
  20.1 0.0 copy-start.2
  20.1 0.2 collective-permute-done.3.y_second
  20.4 0.4 copy-done.2
  20.7 0.2 copy-done.3
  21.0 5.3 %advance_stress.1 = (f32[6,16,64,128]{3,2,1,0:T(8,128)}, f32[3,16,64,128]{3,2,1,0:T(8,128)}, f32[16,64,128]{2,1,0:T(8,128)}) custom-call(f32[3]{0:T(128)} %buoy.5, f32[3]{0:T(128)} %lame.1, f32[3]{0:T(128)} %shear.1, f32[3]{0:T(128)} %piezo.1, f32[6,16,64,128]{3,2,1,0:T(8,128)} %stress_in.3, f32[3,16,64,128]{3,2,1,0:T(8,128)} %get-tuple-element.17.part_in, ...), custom_call_target="tpu_custom_call" | custom-call | flops 1000000 | bytes 10731568 | tf_op jit(solution)/shard_map/advance_stress/pallas_call | solution.py:495
  26.3 20.2 %all_to_all.10 = f32[16,64,128]{2,1,0:T(8,128)} all-to-all(f32[16,64,128]{2,1,0:T(8,128)} %get-tuple-element.29), channel_id=1, replica_groups=mesh['gx'=32,'gy'=8] {'gy'}, dimensions={0} | all-to-all | bytes 1048576 | tf_op jit(solution)/shard_map/all_to_all | solution.py:578
  46.5 3.3 %transform_y.1 = f32[2048,128]{1,0:T(8,128)} custom-call(f32[8,2,64,128]{3,2,1,0:T(8,128)} %bitcast.5, bf16[256,256]{1,0:T(8,128)(2,1)} %constant.15.clone.w_high, bf16[256,256]{1,0:T(8,128)(2,1)} %constant.16.clone.w_low, f32[16,128]{1,0:T(8,128)} %constant.17.clone.twiddle), custom_call_target="tpu_custom_call" | custom-call | flops 1000000 | bytes 2105344 | tf_op jit(solution)/shard_map/transform_y/pallas_call | solution.py:495
  49.8 46.7 %all_to_all.11 = f32[256,8,128]{2,1,0:T(8,128)} all-to-all(f32[256,8,128]{2,1,0:T(8,128)} %bitcast.3), channel_id=1, replica_groups=mesh['gx'=32,'gy'=8] {'gx','gy'}, dimensions={0} | all-to-all | bytes 2097152 | tf_op jit(solution)/shard_map/all_to_all | solution.py:587
  96.5 3.6 %solve.1 = f32[2,16,4,2048]{3,2,1,0:T(4,128)} custom-call(s32[16]{0:T(128)} %layer_kind.2, f32[3]{0:T(128)} %lateral.3, f32[3]{0:T(128)} %normal.3, f32[32,8,8,128]{3,2,1,0:T(8,128)} %bitcast.4, bf16[256,256]{1,0:T(8,128)(2,1)} %constant.18.clone.w_high, bf16[256,256]{1,0:T(8,128)(2,1)} %constant.19.clone.w_low, f32[32,128]{1,0:T(8,128)} %constant.20.clone.twiddle, ...), custom_call_target="tpu_custom_call" | custom-call | flops 1000000 | bytes 3686488 | tf_op jit(solution)/shard_map/solve/pallas_call | solution.py:495
  (1 shorter events, 0.0 us)
Async XLA Ops:
  2.7 8.8 %collective-permute-start = (f32[6,16,128]{2,1,0:T(8,128)}, f32[6,16,128]{2,1,0:T(8,128)S(1)}, u32[]{:S(2)}, u32[]{:S(2)}) collective-permute-start(f32[6,16,128]{2,1,0:T(8,128)} %get-tuple-element.18), channel_id=1, source_target_pairs={{0,8},{16,24},{32,40},{48,56},{64,72},{80,88},{96,104},{112,120},{... | collective-permute-start | bytes 147464 | tf_op jit(solution)/shard_map/ppermute | solution.py:534
  4.8 6.6 %collective-permute-start.1 = (f32[6,16,128]{2,1,0:T(8,128)}, f32[6,16,128]{2,1,0:T(8,128)S(1)}, u32[]{:S(2)}, u32[]{:S(2)}) collective-permute-start(f32[6,16,128]{2,1,0:T(8,128)} %get-tuple-element.19), channel_id=1, source_target_pairs={{8,16},{24,32},{40,48},{56,64},{72,80},{88,96},{104,112},{120,128}... | collective-permute-start | bytes 147464 | tf_op jit(solution)/shard_map/ppermute | solution.py:533
  11.5 0.6 copy-start
  11.5 0.6 copy-start.1
  13.7 6.4 %collective-permute-start.2 = (f32[80,128]{1,0:T(8,128)}, f32[80,128]{1,0:T(8,128)S(1)}, u32[]{:S(2)}, u32[]{:S(2)}) collective-permute-start(f32[80,128]{1,0:T(8,128)} %get-tuple-element.25), channel_id=1, source_target_pairs={{0,1},{2,3},{4,5},{6,7},{1,0},{3,2},{5,4},{7,6},{8,9},{10,11},{12,... | collective-permute-start | bytes 122888 | tf_op jit(solution)/shard_map/ppermute | solution.py:534
  14.8 5.5 %collective-permute-start.3 = (f32[80,128]{1,0:T(8,128)}, f32[80,128]{1,0:T(8,128)S(1)}, u32[]{:S(2)}, u32[]{:S(2)}) collective-permute-start(f32[80,128]{1,0:T(8,128)} %get-tuple-element.26), channel_id=1, source_target_pairs={{1,2},{3,4},{5,6},{2,1},{4,3},{6,5},{9,10},{11,12},{13,14},{10,9},... | collective-permute-start | bytes 122888 | tf_op jit(solution)/shard_map/ppermute | solution.py:533
  20.1 0.6 copy-start.2
  20.3 0.6 copy-start.3

commit v3 on v2

--- a/solution.py
+++ b/solution.py
@@ -17,7 +17,7 @@
 DY = 8
 BX = NX // DX
 BY = NY // DY
-VMEM_LIMIT = 56 * 1024 * 1024
+KEPT_LIMIT = 24 * 1024 * 1024
 
 
 def halves(values):
@@ -128,15 +128,29 @@
     return low, high
 
 
-def edge_rows(buoy, stress_first, stress_end, veloc_first, veloc_end, mat_first, mat_end, first, second):
-    sxx, sxy, sxz = (stress_end[c, :, 7, :] for c in (0, 3, 4))
-    b = pick(mat_end[:, 7, :], buoy)
-    ux = veloc_end[0, :, 7, :] + b * ((sxy - last_lane(sxy)) + (sxz - last_layer(sxz)) - sxx)
+def edge_rows(
+    buoy, stress_in, veloc_in, material_in, first, second, stress, veloc, material, sems
+):
+    moves = []
+    for n, row in enumerate((0, BX - 1)):
+        at = pl.ds(row, 1)
+        moves += [
+            pltpu.make_async_copy(stress_in.at[:, :, at], stress.at[n], sems.at[n, 0]),
+            pltpu.make_async_copy(veloc_in.at[:, :, at], veloc.at[n], sems.at[n, 1]),
+            pltpu.make_async_copy(material_in.at[:, at], material.at[n], sems.at[n, 2]),
+        ]
+    for move in moves:
+        move.start()
+    for move in moves:
+        move.wait()
+    sxx, sxy, sxz = (stress[1, c, :, 0, :] for c in (0, 3, 4))
+    b = pick(material[1, :, 0, :], buoy)
+    ux = veloc[1, 0, :, 0, :] + b * ((sxy - last_lane(sxy)) + (sxz - last_layer(sxz)) - sxx)
     down = [ux, b, sxy, sxz, jnp.zeros_like(b), jnp.zeros_like(b)]
-    sxx, syy, szz, sxy, sxz, syz = (stress_first[c, :, 0, :] for c in range(6))
-    b = pick(mat_first[:, 0, :], buoy)
-    uy = veloc_first[1, :, 0, :] + b * (sxy + (next_lane(syy) - syy) + (syz - last_layer(syz)))
-    uz = veloc_first[2, :, 0, :] + b * (sxz + (syz - last_lane(syz)) + (next_layer(szz) - szz))
+    sxx, syy, szz, sxy, sxz, syz = (stress[0, c, :, 0, :] for c in range(6))
+    b = pick(material[0, :, 0, :], buoy)
+    uy = veloc[0, 1, :, 0, :] + b * (sxy + (next_lane(syy) - syy) + (syz - last_layer(syz)))
+    uz = veloc[0, 2, :, 0, :] + b * (sxz + (syz - last_lane(syz)) + (next_layer(szz) - szz))
     up = [uy, uz, b, sxx, syy, syz]
     is_odd = odd("gx")
     for c in range(6):
@@ -144,7 +158,7 @@
         second[c] = jnp.where(is_odd, down[c], up[c])
 
 
-CHUNK = 2
+CHUNK = 4
 
 
 def copies(pairs, sems):
@@ -158,24 +172,11 @@
     return made
 
 
-def advance_velocity(
-    buoy, stress_in, veloc_in, material_in, new_out, right_ref, left_ref,
-    stress, veloc, material, new, in_sems, out_sems,
-):
-    arriving = copies([(stress_in, stress), (veloc_in, veloc), (material_in, material)], in_sems)
-    leaving = copies([(new, new_out)], out_sems)
-    for chunk in arriving:
-        for copy in chunk:
-            copy.start()
+def advance_velocity(buoy, stress, veloc, material, new, right_ref, left_ref):
     column = lax.broadcasted_iota(jnp.int32, (BX, BY), 1)
     right = jnp.zeros((BX, BY), jnp.float32)
     left = jnp.zeros((BX, BY), jnp.float32)
-    ready = 0
     for z in range(NZ):
-        while ready < min(z + 2, NZ):
-            for copy in arriving[ready // CHUNK]:
-                copy.wait()
-            ready += CHUNK
         sxx, syy, szz, sxy, sxz, syz = (stress[c, z] for c in range(6))
         b = pick(material[z], buoy)
         dz_sxz = sxz - stress[4, z - 1] if z else sxz
@@ -187,9 +188,6 @@
         new[0, z] = ux
         new[1, z] = uy
         new[2, z] = uz
-        if z % CHUNK == CHUNK - 1:
-            for copy in leaving[z // CHUNK]:
-                copy.start()
         for part, value in enumerate((uy, b, sxy, syz)):
             spot = part * NZ + z
             moved = pltpu.roll(value, (spot + 1) % BY, 1)
@@ -200,9 +198,6 @@
             left = jnp.where(column == spot, moved, left)
     right_ref[...] = right
     left_ref[...] = left
-    for chunk in leaving:
-        for copy in chunk:
-            copy.wait()
 
 
 def edge_columns(right_ref, left_ref, x_first, x_second, first, second):
@@ -239,15 +234,11 @@
 
 
 def advance_stress(
-    buoy, lame, shear, piezo, stress_in, part_in, material_in, x_first, x_second,
-    own_right, own_left, y_first, y_second, stress_out, veloc_out, charge_out,
-    stress, part, material, new_stress, new_veloc, charge, in_sems, out_sems,
+    buoy, lame, shear, piezo, stress, part, material, x_first, x_second,
+    own_right, own_left, y_first, y_second, stress_out, veloc_out, charge,
+    new_stress, new_veloc, sems,
 ):
-    arriving = copies([(stress_in, stress), (part_in, part), (material_in, material)], in_sems)
-    leaving = copies([(charge, charge_out), (new_stress, stress_out), (new_veloc, veloc_out)], out_sems)
-    for chunk in arriving:
-        for copy in chunk:
-            copy.start()
+    leaving = copies([(new_stress, stress_out), (new_veloc, veloc_out)], sems)
     lane = lax.broadcasted_iota(jnp.int32, (BX, BY), 1)
     corner_lane = lane[:NZ]
     row8 = lax.broadcasted_iota(jnp.int32, (8, BY), 0)
@@ -291,13 +282,8 @@
         new_veloc[1, z] = at_top(uy, -(head * low[2][row]))
         new_veloc[2, z] = at_top(uz, -(head * low[3][row]))
 
-    ready = 0
     for step in range(NZ + 1):
         if step < NZ:
-            while ready <= step:
-                for copy in arriving[ready // CHUNK]:
-                    copy.wait()
-                ready += CHUNK
             close_edges(step)
         if step == 0:
             continue
@@ -448,7 +434,12 @@
             factor = g[z + 1] * inv
 
 
-def solve(layer_kind, lateral, normal, lines, w_high, w_low, twiddle, inverse, out, rhs):
+SPAN = 512
+
+
+def solve(
+    layer_kind, lateral, normal, lines, w_high, w_low, twiddle, inverse, modes_out, rhs, out, sems
+):
     weights = (w_high[...], w_low[...])
     upper = rows(jnp.zeros((8, 128), jnp.float32)) < 4
     for gy in range(DY):
@@ -466,6 +457,7 @@
             rhs[2 * gy, :, at] = jnp.where(upper, re, pltpu.roll(im, 4, 0))
             rhs[2 * gy + 1, :, at] = jnp.where(upper, pltpu.roll(re, 4, 0), im)
     _, g = coupling_scalars(layer_kind, lateral, normal)
+    leaving = []
     for k in range(NX // 256):
         at = slice(256 * k, 256 * k + 256)
         sums = []
@@ -482,6 +474,16 @@
             above = value * inverse[z, :, at]
             out[0, z, :, at] = above[:4]
             out[1, z, :, at] = above[4:]
+        if (k + 1) * 256 % SPAN == 0:
+            done = pl.ds((k + 1) * 256 - SPAN, SPAN)
+            leaving.append(
+                pltpu.make_async_copy(
+                    out.at[:, :, :, done], modes_out.at[:, :, :, done], sems.at[len(leaving)]
+                )
+            )
+            leaving[-1].start()
+    for copy in leaving:
+        copy.wait()
 
 
 SMEM = pl.BlockSpec(memory_space=pltpu.SMEM)
@@ -489,8 +491,15 @@
 ANY = pl.BlockSpec(memory_space=pl.ANY)
 
 
-def call(body, name, outs, in_specs, args, scratch=(), out_specs=None, flops=1_000_000):
-    shapes = [jax.ShapeDtypeStruct(shape, jnp.float32) for shape in outs]
+def near(*values):
+    return tuple(pltpu.with_memory_space_constraint(value, pltpu.VMEM) for value in values)
+
+
+def call(body, name, outs, in_specs, args, scratch=(), out_specs=None, flops=1_000_000, keep=()):
+    shapes = [
+        pltpu.VMEM(shape, jnp.float32) if n in keep else jax.ShapeDtypeStruct(shape, jnp.float32)
+        for n, shape in enumerate(outs)
+    ]
     moved = sum(4 * math.prod(shape) for shape in outs) + sum(4 * v.size for v in args)
     return pl.pallas_call(
         body,
@@ -499,25 +508,9 @@
         in_specs=in_specs,
         out_specs=out_specs or [VMEM] * len(outs),
         scratch_shapes=list(scratch),
-        compiler_params=pltpu.CompilerParams(vmem_limit_bytes=VMEM_LIMIT),
+        compiler_params=pltpu.CompilerParams(vmem_limit_bytes=KEPT_LIMIT),
         cost_estimate=pl.CostEstimate(flops=flops, bytes_accessed=moved, transcendentals=0),
     )(*args)
-
-
-def edge_call(buoyancy, stress, velocity, material):
-    end = BX // 8 - 1
-    block4 = lambda count, at: pl.BlockSpec((count, NZ, 8, BY), lambda i: (0, 0, at, 0))
-    block3 = lambda at: pl.BlockSpec((NZ, 8, BY), lambda i: (0, at, 0))
-    whole = pl.BlockSpec((6, NZ, BY), lambda i: (0, 0, 0))
-    return pl.pallas_call(
-        edge_rows,
-        name="edge_rows",
-        grid=(1,),
-        out_shape=[jax.ShapeDtypeStruct((6, NZ, BY), jnp.float32)] * 2,
-        in_specs=[SMEM, block4(6, 0), block4(6, end), block4(3, 0), block4(3, end), block3(0), block3(end)],
-        out_specs=[whole, whole],
-        compiler_params=pltpu.CompilerParams(vmem_limit_bytes=VMEM_LIMIT),
-    )(buoyancy, stress, stress, velocity, velocity, material, material)
 
 
 def field(count, dtype=jnp.float32):
@@ -537,22 +530,30 @@
 def per_device(
     stress, velocity, material, layer_kind, buoyancy, lame_first, shear_modulus, piezo, permit_lateral, permit_normal
 ):
-    chunks = NZ // CHUNK
-    sems = lambda count: pltpu.SemaphoreType.DMA((chunks, count))
-    x_edges = swaps("gx", *edge_call(buoyancy, stress, velocity, material))
+    x_edges = call(
+        edge_rows,
+        "edge_rows",
+        [(6, NZ, BY)] * 2,
+        [SMEM] + [ANY] * 3,
+        (buoyancy, *(pltpu.with_memory_space_constraint(v, pltpu.HBM) for v in (stress, velocity, material))),
+        [
+            pltpu.VMEM((2, 6, NZ, 1, BY), jnp.float32),
+            pltpu.VMEM((2, 3, NZ, 1, BY), jnp.float32),
+            pltpu.VMEM((2, NZ, 1, BY), jnp.int32),
+            pltpu.SemaphoreType.DMA((2, 3)),
+        ],
+        keep=(0, 1),
+    )
+    x_edges = near(*swaps("gx", *x_edges))
+    stress, velocity, material = near(stress, velocity, material)
     part, own_right, own_left = call(
         advance_velocity,
         "advance_velocity",
         [(3, NZ, BX, BY), (BX, BY), (BX, BY)],
-        [SMEM] + [ANY] * 3,
+        [SMEM] + [VMEM] * 3,
         (buoyancy, stress, velocity, material),
-        [field(6), field(3), field(1, jnp.int32), field(3), sems(3), sems(1)],
-        [ANY, VMEM, VMEM],
-    )
-    y_edges = call(
-        edge_columns, "edge_columns", [(BX + NZ, BY)] * 2, [VMEM] * 4, (own_right, own_left, *x_edges)
-    )
-    y_edges = swaps("gy", *y_edges)
+        keep=(0, 1, 2),
+    )
     scalars = (layer_kind, permit_lateral, permit_normal)
     own_right, layer_kind = lax.optimization_barrier((own_right, layer_kind))
     inverse, = call(
@@ -561,19 +562,31 @@
         [(NZ, 8, NX)],
         [SMEM] * 3 + [VMEM],
         (layer_kind, permit_lateral, permit_normal, jnp.asarray(table_wave())),
+        keep=(0,),
     )
     own_right, inverse = lax.optimization_barrier((own_right, inverse))
+    own_right, inverse = near(own_right, inverse)
+    y_edges = call(
+        edge_columns,
+        "edge_columns",
+        [(BX + NZ, BY)] * 2,
+        [VMEM] * 4,
+        (own_right, own_left, *x_edges),
+        keep=(0, 1),
+    )
+    y_edges = near(*swaps("gy", *y_edges))
     stress_next, velocity_next, charge = call(
         advance_stress,
         "advance_stress",
         [(6, NZ, BX, BY), (3, NZ, BX, BY), (NZ, BX, BY)],
-        [SMEM] * 4 + [ANY] * 3 + [VMEM] * 6,
+        [SMEM] * 4 + [VMEM] * 9,
         (
             buoyancy, lame_first, shear_modulus, piezo, stress, part, material,
             *x_edges, own_right, own_left, *y_edges,
         ),
-        [field(6), field(3), field(1, jnp.int32), field(6), field(3), field(1), sems(3), sems(3)],
-        [ANY] * 3,
+        [field(6), field(3), pltpu.SemaphoreType.DMA((NZ // CHUNK, 2))],
+        [ANY, ANY, VMEM],
+        keep=(2,),
     )
     charge = lax.all_to_all(charge, "gy", 0, 0, tiled=True).reshape(DY, 2, BX, BY)
     modes, = call(
@@ -581,8 +594,9 @@
         "transform_y",
         [(NY * 2, 128)],
         [VMEM] * 4,
-        (charge, *(jnp.asarray(t) for t in tables_y())),
+        (*near(charge), *(jnp.asarray(t) for t in tables_y())),
         [pltpu.VMEM((1024, 128), jnp.float32)] * 2,
+        keep=(0,),
     )
     lines = lax.all_to_all(modes.reshape(DX * DY, 8, 128), ("gx", "gy"), 0, 0, tiled=True)
     potential_modes, = call(
@@ -590,8 +604,13 @@
         "solve",
         [(2, NZ, 4, NX)],
         [SMEM] * 3 + [VMEM] * 5,
-        (*scalars, lines.reshape(DX, DY, 8, 128), *(jnp.asarray(t) for t in tables_x()), inverse),
-        [pltpu.VMEM((NZ, 8, NX), jnp.float32)],
+        (*scalars, *near(lines.reshape(DX, DY, 8, 128)), *(jnp.asarray(t) for t in tables_x()), inverse),
+        [
+            pltpu.VMEM((NZ, 8, NX), jnp.float32),
+            pltpu.VMEM((2, NZ, 4, NX), jnp.float32),
+            pltpu.SemaphoreType.DMA((NX // SPAN,)),
+        ],
+        [ANY],
     )
     return (stress_next, velocity_next, potential_modes)
 

time: 101 us -> 92.6 us (0.917)
  Pallas kernels: 23.9 us -> 13.2 us
  waiting for transfers between devices: 0.24 us -> 2.06 us
    pallas_call x6 -> x7, Pallas kernels: 21.9 us -> 13.2 us  [call(): pl.pallas_call(body, name=name, out_shape=shapes, in_specs=in_specs, out_...]
    pallas_call x1 -> x0, Pallas kernels: 2.08 us -> none  [edge_call(): pl.pallas_call(edge_rows, name='edge_rows', grid=(1,), out_shape=[jax.Sha...]
    ppermute x2, waiting for transfers between devices: 0.23 us -> 2.06 us  [swaps(): second = lax.ppermute(second, axis, pairs(1))]
    all_to_all x1, blocking collectives: 46.7 us -> 48 us  [per_device(): lax.all_to_all(modes.reshape(DX * DY, 8, 128), ('gx', 'gy'), 0, 0, tiled=...]
  transfers between devices with their start and end apart: 4 -> 4, of which waited for: 1 -> 1; matrix products, arithmetic and copies ran while one was open for 0% -> 0% of each run, Pallas kernels for 8% -> 4%
where the time goes in v3:
time: 92.6 us; the launch traced here: 92.4 us
  blocking collectives  67.8 us (73%)
  Pallas kernels  13.2 us (14%)
  starting transfers between devices  7.49 us (8%)
  waiting for transfers between devices  2.06 us (2%)
    all_to_all x1, blocking collectives, per_device(): lax.all_to_all(modes.reshape(DX * DY, 8, 128), ('gx', 'gy'), 0, 0, tiled=...  48 us
    all_to_all x1, blocking collectives, per_device(): lax.all_to_all(charge, 'gy', 0, 0, tiled=True).reshape(DY, 2, BX, BY)  19.8 us
    pallas_call x7, Pallas kernels, call(): pl.pallas_call(body, name=name, out_shape=shapes, in_specs=in_specs, out_...  13.2 us
    ppermute x2, starting transfers between devices, swaps(): second = lax.ppermute(second, axis, pairs(1))  4.03 us
    ppermute x2, starting transfers between devices, swaps(): return (lax.ppermute(first, axis, pairs(0)), second)  3.47 us
    ppermute x2, waiting for transfers between devices, swaps(): second = lax.ppermute(second, axis, pairs(1))  2.06 us
  transfers between devices with their start and end apart: 4, of which 1 were waited for; matrix products, arithmetic and copies ran while one was open for 0% of the time, Pallas kernels for 4%

profile of v3, /device:TPU:1, one launch (start us, length us, event | category | flops | bytes accessed | tf_op | source)
XLA Modules:
  0.0 92.4 jit_solution(15575822067319798292)
XLA Ops:
  0.7 0.0 copy-start.10
  0.7 0.8 copy-done.10
  1.5 1.8 %edge_rows.1 = (f32[6,16,128]{2,1,0:T(8,128)S(1)}, f32[6,16,128]{2,1,0:T(8,128)S(1)}) custom-call(f32[3]{0:T(128)S(1)} %copy-done.10, f32[6,16,64,128]{3,2,1,0:T(8,128)} %stress.3, f32[3,16,64,128]{3,2,1,0:T(8,128)} %veloc_in.1, s32[16,64,128]{2,1,0:T(8,128)} %material.3), custom_call_target="tpu_custom_call" | custom-call | flops 1000000 | bytes 5341196 | tf_op jit(solution)/shard_map/edge_rows/pallas_call | solution.py:504
  3.3 2.2 %collective-permute-start = (f32[6,16,128]{2,1,0:T(8,128)S(1)}, f32[6,16,128]{2,1,0:T(8,128)S(1)}, u32[]{:S(2)}, u32[]{:S(2)}) collective-permute-start(f32[6,16,128]{2,1,0:T(8,128)S(1)} %get-tuple-element.18), channel_id=1, source_target_pairs={{0,8},{16,24},{32,40},{48,56},{64,72},{80,88},{96,104},{112,120},{... | collective-permute-start | bytes 147464 | tf_op jit(solution)/shard_map/ppermute | solution.py:527
  5.5 0.0 copy-start.11
  5.5 0.0 copy-start.17
  5.5 0.8 collective-permute-start.1
  6.4 3.2 %advance_velocity.1 = (f32[3,16,64,128]{3,2,1,0:T(8,128)S(1)}, f32[64,128]{1,0:T(8,128)S(1)}, f32[64,128]{1,0:T(8,128)S(1)}) custom-call(f32[3]{0:T(128)S(1)} %copy-done.10, f32[6,16,64,128]{3,2,1,0:T(8,128)S(1)} %copy-done, f32[3,16,64,128]{3,2,1,0:T(8,128)S(1)} %copy-done.1, s32[16,64,128]{2,1,0:T(8,128)S(1)} %copy-done.2), custom_call_target="tpu_custom_call" | custom-call | flops 1000000 | bytes 6881292 | tf_op jit(solution)/shard_map/advance_velocity/pallas_call | solution.py:504
  9.6 0.9 pivots.1.inverse
  10.5 0.1 edge_columns.1
  10.7 1.3 %collective-permute-start.2 = (f32[80,128]{1,0:T(8,128)S(1)}, f32[80,128]{1,0:T(8,128)S(1)}, u32[]{:S(2)}, u32[]{:S(2)}) collective-permute-start(f32[80,128]{1,0:T(8,128)S(1)} %get-tuple-element.25), channel_id=1, source_target_pairs={{0,1},{2,3},{4,5},{6,7},{1,0},{3,2},{5,4},{7,6},{8,9},{10,11},{12,... | collective-permute-start | bytes 122888 | tf_op jit(solution)/shard_map/ppermute | solution.py:527
  11.9 3.2 %collective-permute-start.3 = (f32[80,128]{1,0:T(8,128)S(1)}, f32[80,128]{1,0:T(8,128)S(1)}, u32[]{:S(2)}, u32[]{:S(2)}) collective-permute-start(f32[80,128]{1,0:T(8,128)S(1)} %get-tuple-element.26), channel_id=1, source_target_pairs={{1,2},{3,4},{5,6},{2,1},{4,3},{6,5},{9,10},{11,12},{13,14},{10,9},... | collective-permute-start | bytes 122888 | tf_op jit(solution)/shard_map/ppermute | solution.py:526
  15.2 2.1 %collective-permute-done.3.y_second = f32[80,128]{1,0:T(8,128)S(1)} collective-permute-done((f32[80,128]{1,0:T(8,128)S(1)}, f32[80,128]{1,0:T(8,128)S(1)}, u32[]{:S(2)}, u32[]{:S(2)}) %collective-permute-start.3) | collective-permute-done | bytes 40992 | tf_op jit(solution)/shard_map/ppermute | solution.py:526
  17.2 0.0 copy-start.3
  17.2 0.0 copy-start.4
  17.3 0.0 copy-start.8
  17.3 3.5 %advance_stress.1 = (f32[6,16,64,128]{3,2,1,0:T(8,128)}, f32[3,16,64,128]{3,2,1,0:T(8,128)}, f32[16,64,128]{2,1,0:T(8,128)S(1)}) custom-call(f32[3]{0:T(128)S(1)} %copy-done.11, f32[3]{0:T(128)S(1)} %copy-done.15, f32[3]{0:T(128)S(1)} %copy-done.16, f32[3]{0:T(128)S(1)} %copy-done.17, f32[6,16,64,128]{3,2,1,0:T(8,128)S(1)} %copy-done, ...), custom_call_target="tpu_custom_call" | custom-call | flops 1000000 | bytes 10731568 | tf_op jit(solution)/shard_map/advance_stress/pallas_call | solution.py:504
  20.8 19.8 %all_to_all.10 = f32[16,64,128]{2,1,0:T(8,128)S(1)} all-to-all(f32[16,64,128]{2,1,0:T(8,128)S(1)} %get-tuple-element.29), channel_id=1, replica_groups=mesh['gx'=32,'gy'=8] {'gy'}, dimensions={0} | all-to-all | bytes 1048576 | tf_op jit(solution)/shard_map/all_to_all | solution.py:591
  40.6 0.0 copy-start.5
  40.6 0.0 copy-start.6
  40.6 0.0 copy-start.7
  40.7 1.2 %transform_y.1 = f32[2048,128]{1,0:T(8,128)S(1)} custom-call(f32[8,2,64,128]{3,2,1,0:T(8,128)S(1)} %bitcast.5, bf16[256,256]{1,0:T(8,128)(2,1)S(1)} %copy-done.4, bf16[256,256]{1,0:T(8,128)(2,1)S(1)} %copy-done.3, f32[16,128]{1,0:T(8,128)S(1)} %copy-done.8), custom_call_target="tpu_custom_call" | custom-call | flops 1000000 | bytes 2105344 | tf_op jit(solution)/shard_map/transform_y/pallas_call | solution.py:504
  41.9 48.0 %all_to_all.11 = f32[256,8,128]{2,1,0:T(8,128)S(1)} all-to-all(f32[256,8,128]{2,1,0:T(8,128)S(1)} %bitcast.3), channel_id=1, replica_groups=mesh['gx'=32,'gy'=8] {'gx','gy'}, dimensions={0} | all-to-all | bytes 2097152 | tf_op jit(solution)/shard_map/all_to_all | solution.py:601
  89.9 2.5 %solve.1 = f32[2,16,4,2048]{3,2,1,0:T(4,128)} custom-call(s32[16]{0:T(128)S(1)} %copy-done.12, f32[3]{0:T(128)S(1)} %copy-done.13, f32[3]{0:T(128)S(1)} %copy-done.14, f32[32,8,8,128]{3,2,1,0:T(8,128)S(1)} %bitcast.4, bf16[256,256]{1,0:T(8,128)(2,1)S(1)} %copy-done.6, bf16[256,256]{1,0:T(8,128)(2,1)S(1)} %copy-done.5, f32[32,128]{1,0:T(8,128)S(1)} %copy-done.7, ...), custom_call_target="tpu_custom_call" | custom-call | flops 1000000 | bytes 3686488 | tf_op jit(solution)/shard_map/solve/pallas_call | solution.py:504
  (29 shorter events, 0.1 us)
Async XLA Ops:
  0.6 5.7 %copy-start.2 = (s32[16,64,128]{2,1,0:T(8,128)S(1)}, s32[16,64,128]{2,1,0:T(8,128)}, u32[]{:S(2)}) copy-start(s32[16,64,128]{2,1,0:T(8,128)} %material.3) | copy-start | bytes 1572868
  0.6 5.7 %copy-start = (f32[6,16,64,128]{3,2,1,0:T(8,128)S(1)}, f32[6,16,64,128]{3,2,1,0:T(8,128)}, u32[]{:S(2)}) copy-start(f32[6,16,64,128]{3,2,1,0:T(8,128)} %stress.3) | copy-start | bytes 9437188
  0.7 5.7 %copy-start.1 = (f32[3,16,64,128]{3,2,1,0:T(8,128)S(1)}, f32[3,16,64,128]{3,2,1,0:T(8,128)}, u32[]{:S(2)}) copy-start(f32[3,16,64,128]{3,2,1,0:T(8,128)} %veloc_in.1) | copy-start | bytes 4718596
  0.7 0.8 copy-start.10
  3.3 7.3 %collective-permute-start = (f32[6,16,128]{2,1,0:T(8,128)S(1)}, f32[6,16,128]{2,1,0:T(8,128)S(1)}, u32[]{:S(2)}, u32[]{:S(2)}) collective-permute-start(f32[6,16,128]{2,1,0:T(8,128)S(1)} %get-tuple-element.18), channel_id=1, source_target_pairs={{0,8},{16,24},{32,40},{48,56},{64,72},{80,88},{96,104},{112,120},{... | collective-permute-start | bytes 147464 | tf_op jit(solution)/shard_map/ppermute | solution.py:527
  5.5 4.1 %copy-start.9 = (f32[1,2048]{1,0:T(1,128)S(1)}, f32[1,2048]{1,0:T(1,128)}, u32[]{:S(2)}) copy-start(f32[1,2048]{1,0:T(1,128)} %constant.14.clone.wave_x) | copy-start | bytes 24580
  5.5 4.1 %copy-start.12 = (s32[16]{0:T(128)S(1)}, s32[16]{0:T(128)}, u32[]{:S(2)}) copy-start(s32[16]{0:T(128)} %layer_kind.2) | copy-start | bytes 196
  5.5 4.1 %copy-start.13 = (f32[3]{0:T(128)S(1)}, f32[3]{0:T(128)}, u32[]{:S(2)}) copy-start(f32[3]{0:T(128)} %lateral.3) | copy-start | bytes 40
  5.5 4.1 %copy-start.14 = (f32[3]{0:T(128)S(1)}, f32[3]{0:T(128)}, u32[]{:S(2)}) copy-start(f32[3]{0:T(128)} %normal.3) | copy-start | bytes 40
  5.5 11.7 %copy-start.11 = (f32[3]{0:T(128)S(1)}, f32[3]{0:T(128)}, u32[]{:S(2)}) copy-start(f32[3]{0:T(128)} %buoy.5) | copy-start | bytes 40
  5.5 11.7 %copy-start.15 = (f32[3]{0:T(128)S(1)}, f32[3]{0:T(128)}, u32[]{:S(2)}) copy-start(f32[3]{0:T(128)} %lame.1) | copy-start | bytes 40
  5.5 11.7 %copy-start.16 = (f32[3]{0:T(128)S(1)}, f32[3]{0:T(128)}, u32[]{:S(2)}) copy-start(f32[3]{0:T(128)} %shear.1) | copy-start | bytes 40
  5.5 11.7 %copy-start.17 = (f32[3]{0:T(128)S(1)}, f32[3]{0:T(128)}, u32[]{:S(2)}) copy-start(f32[3]{0:T(128)} %piezo.1) | copy-start | bytes 40
  5.5 5.0 %collective-permute-start.1 = (f32[6,16,128]{2,1,0:T(8,128)S(1)}, f32[6,16,128]{2,1,0:T(8,128)S(1)}, u32[]{:S(2)}, u32[]{:S(2)}) collective-permute-start(f32[6,16,128]{2,1,0:T(8,128)S(1)} %get-tuple-element.19), channel_id=1, source_target_pairs={{8,16},{24,32},{40,48},{56,64},{72,80},{88,96},{104,112},{120,128}... | collective-permute-start | bytes 147464 | tf_op jit(solution)/shard_map/ppermute | solution.py:526
  10.7 4.5 %collective-permute-start.2 = (f32[80,128]{1,0:T(8,128)S(1)}, f32[80,128]{1,0:T(8,128)S(1)}, u32[]{:S(2)}, u32[]{:S(2)}) collective-permute-start(f32[80,128]{1,0:T(8,128)S(1)} %get-tuple-element.25), channel_id=1, source_target_pairs={{0,1},{2,3},{4,5},{6,7},{1,0},{3,2},{5,4},{7,6},{8,9},{10,11},{12,... | collective-permute-start | bytes 122888 | tf_op jit(solution)/shard_map/ppermute | solution.py:527
  11.9 5.3 %collective-permute-start.3 = (f32[80,128]{1,0:T(8,128)S(1)}, f32[80,128]{1,0:T(8,128)S(1)}, u32[]{:S(2)}, u32[]{:S(2)}) collective-permute-start(f32[80,128]{1,0:T(8,128)S(1)} %get-tuple-element.26), channel_id=1, source_target_pairs={{1,2},{3,4},{5,6},{2,1},{4,3},{6,5},{9,10},{11,12},{13,14},{10,9},... | collective-permute-start | bytes 122888 | tf_op jit(solution)/shard_map/ppermute | solution.py:526
  17.2 23.4 %copy-start.3 = (bf16[256,256]{1,0:T(8,128)(2,1)S(1)}, bf16[256,256]{1,0:T(8,128)(2,1)}, u32[]{:S(2)}) copy-start(bf16[256,256]{1,0:T(8,128)(2,1)} %constant.16.clone.w_low) | copy-start | bytes 393220
  17.2 23.4 %copy-start.4 = (bf16[256,256]{1,0:T(8,128)(2,1)S(1)}, bf16[256,256]{1,0:T(8,128)(2,1)}, u32[]{:S(2)}) copy-start(bf16[256,256]{1,0:T(8,128)(2,1)} %constant.15.clone.w_high) | copy-start | bytes 393220
  17.3 23.3 %copy-start.8 = (f32[16,128]{1,0:T(8,128)S(1)}, f32[16,128]{1,0:T(8,128)}, u32[]{:S(2)}) copy-start(f32[16,128]{1,0:T(8,128)} %constant.17.clone.twiddle) | copy-start | bytes 24580
  40.6 49.3 %copy-start.5 = (bf16[256,256]{1,0:T(8,128)(2,1)S(1)}, bf16[256,256]{1,0:T(8,128)(2,1)}, u32[]{:S(2)}) copy-start(bf16[256,256]{1,0:T(8,128)(2,1)} %constant.19.clone.w_low) | copy-start | bytes 393220
  40.6 49.2 %copy-start.6 = (bf16[256,256]{1,0:T(8,128)(2,1)S(1)}, bf16[256,256]{1,0:T(8,128)(2,1)}, u32[]{:S(2)}) copy-start(bf16[256,256]{1,0:T(8,128)(2,1)} %constant.18.clone.w_high) | copy-start | bytes 393220
  40.6 49.2 %copy-start.7 = (f32[32,128]{1,0:T(8,128)S(1)}, f32[32,128]{1,0:T(8,128)}, u32[]{:S(2)}) copy-start(f32[32,128]{1,0:T(8,128)} %constant.20.clone.twiddle) | copy-start | bytes 49156

commit v4 on v3

--- a/solution.py
+++ b/solution.py
@@ -129,9 +129,9 @@
 
 
 def edge_rows(
-    buoy, stress_in, veloc_in, material_in, first, second, stress, veloc, material, sems
+    buoy_in, stress_in, veloc_in, material_in, second, first, stress, veloc, material, buoy, sems, buoy_sem
 ):
-    moves = []
+    moves = [pltpu.make_async_copy(buoy_in, buoy, buoy_sem)]
     for n, row in enumerate((0, BX - 1)):
         at = pl.ds(row, 1)
         moves += [
@@ -158,7 +158,7 @@
         second[c] = jnp.where(is_odd, down[c], up[c])
 
 
-CHUNK = 4
+CHUNK = 2
 
 
 def copies(pairs, sems):
@@ -200,7 +200,7 @@
     left_ref[...] = left
 
 
-def edge_columns(right_ref, left_ref, x_first, x_second, first, second):
+def edge_columns(right_ref, left_ref, x_second, x_first, second, first):
     low, high = low_high("gx", x_first, x_second)
     corner = lax.broadcasted_iota(jnp.int32, (NZ, BY), 1)
     layer = lax.broadcasted_iota(jnp.int32, (NZ, BY), 0)
@@ -234,8 +234,8 @@
 
 
 def advance_stress(
-    buoy, lame, shear, piezo, stress, part, material, x_first, x_second,
-    own_right, own_left, y_first, y_second, stress_out, veloc_out, charge,
+    buoy, lame, shear, piezo, stress, part, material, x_second, x_first,
+    own_right, own_left, y_second, y_first, stress_out, veloc_out, charge,
     new_stress, new_veloc, sems,
 ):
     leaving = copies([(new_stress, stress_out), (new_veloc, veloc_out)], sems)
@@ -518,13 +518,13 @@
     return pltpu.VMEM(shape if count == 1 else (count, *shape), dtype)
 
 
-def swaps(axis, first, second):
+def swaps(axis, second, first):
     def pairs(start):
         both = [(i, i + 1) for i in range(start, lax.axis_size(axis) - 1, 2)]
         return both + [(b, a) for a, b in both]
 
     second = lax.ppermute(second, axis, pairs(1))
-    return lax.ppermute(first, axis, pairs(0)), second
+    return second, lax.ppermute(first, axis, pairs(0))
 
 
 def per_device(
@@ -534,13 +534,17 @@
         edge_rows,
         "edge_rows",
         [(6, NZ, BY)] * 2,
-        [SMEM] + [ANY] * 3,
-        (buoyancy, *(pltpu.with_memory_space_constraint(v, pltpu.HBM) for v in (stress, velocity, material))),
+        [ANY] * 4,
+        tuple(
+            pltpu.with_memory_space_constraint(v, pltpu.HBM) for v in (buoyancy, stress, velocity, material)
+        ),
         [
             pltpu.VMEM((2, 6, NZ, 1, BY), jnp.float32),
             pltpu.VMEM((2, 3, NZ, 1, BY), jnp.float32),
             pltpu.VMEM((2, NZ, 1, BY), jnp.int32),
+            pltpu.SMEM((3,), jnp.float32),
             pltpu.SemaphoreType.DMA((2, 3)),
+            pltpu.SemaphoreType.DMA,
         ],
         keep=(0, 1),
     )

time: 92.6 us -> 90.1 us (0.973)
  blocking collectives: 67.8 us -> 64.5 us
  starting transfers between devices: 7.49 us -> 10.3 us
    all_to_all x1, blocking collectives: 48 us -> 44.3 us  [per_device(): lax.all_to_all(modes.reshape(DX * DY, 8, 128), ('gx', 'gy'), 0, 0, tiled=...]
    ppermute x2, starting transfers between devices: 4.03 us -> 5.46 us  [swaps(): second = lax.ppermute(second, axis, pairs(1))]
    ppermute x2, starting transfers between devices: 3.47 us -> 4.85 us  [swaps(): return (second, lax.ppermute(first, axis, pairs(0)))]
  transfers between devices with their start and end apart: 4 -> 4, of which waited for: 1 -> 1; matrix products, arithmetic and copies ran while one was open for 0% -> 0% of each run, Pallas kernels for 4% -> 5%
where the time goes in v4:
time: 90.1 us; the launch traced here: 89.9 us
  blocking collectives  64.5 us (72%)
  Pallas kernels  12.5 us (14%)
  starting transfers between devices  10.3 us (11%)
  waiting for transfers between devices  1.58 us (2%)
  between operations  0.91 us (1%)
    all_to_all x1, blocking collectives, per_device(): lax.all_to_all(modes.reshape(DX * DY, 8, 128), ('gx', 'gy'), 0, 0, tiled=...  44.3 us
    all_to_all x1, blocking collectives, per_device(): lax.all_to_all(charge, 'gy', 0, 0, tiled=True).reshape(DY, 2, BX, BY)  20.2 us
    pallas_call x7, Pallas kernels, call(): pl.pallas_call(body, name=name, out_shape=shapes, in_specs=in_specs, out_...  12.5 us
    ppermute x2, starting transfers between devices, swaps(): second = lax.ppermute(second, axis, pairs(1))  5.46 us
    ppermute x2, starting transfers between devices, swaps(): return (second, lax.ppermute(first, axis, pairs(0)))  4.85 us
  transfers between devices with their start and end apart: 4, of which 1 were waited for; matrix products, arithmetic and copies ran while one was open for 0% of the time, Pallas kernels for 5%

profile of v4, /device:TPU:1, one launch (start us, length us, event | category | flops | bytes accessed | tf_op | source)
XLA Modules:
  0.0 89.9 jit_solution(14023376709788724059)
XLA Ops:
  0.7 1.2 %edge_rows.1 = (f32[6,16,128]{2,1,0:T(8,128)S(1)}, f32[6,16,128]{2,1,0:T(8,128)S(1)}) custom-call(f32[3]{0:T(128)} %buoy.3, f32[6,16,64,128]{3,2,1,0:T(8,128)} %stress.3, f32[3,16,64,128]{3,2,1,0:T(8,128)} %veloc_in.1, s32[16,64,128]{2,1,0:T(8,128)} %material.3), custom_call_target="tpu_custom_call" | custom-call | flops 1000000 | bytes 5341196 | tf_op jit(solution)/shard_map/edge_rows/pallas_call | solution.py:504
  1.9 0.8 collective-permute-start
  2.7 0.0 copy-start.9
  2.7 0.0 copy-start.11
  2.7 0.0 copy-start.14
  2.8 0.0 copy-start.15
  2.8 4.8 %collective-permute-start.1 = (f32[6,16,128]{2,1,0:T(8,128)S(1)}, f32[6,16,128]{2,1,0:T(8,128)S(1)}, u32[]{:S(2)}, u32[]{:S(2)}) collective-permute-start(f32[6,16,128]{2,1,0:T(8,128)S(1)} %get-tuple-element.19), channel_id=1, source_target_pairs={{0,8},{16,24},{32,40},{48,56},{64,72},{80,88},{96,104},{112,120},{... | collective-permute-start | bytes 147464 | tf_op jit(solution)/shard_map/ppermute | solution.py:527
  7.5 3.2 %advance_velocity.1 = (f32[3,16,64,128]{3,2,1,0:T(8,128)S(1)}, f32[64,128]{1,0:T(8,128)S(1)}, f32[64,128]{1,0:T(8,128)S(1)}) custom-call(f32[3]{0:T(128)S(1)} %copy-done.10, f32[6,16,64,128]{3,2,1,0:T(8,128)S(1)} %copy-done, f32[3,16,64,128]{3,2,1,0:T(8,128)S(1)} %copy-done.1, s32[16,64,128]{2,1,0:T(8,128)S(1)} %copy-done.2), custom_call_target="tpu_custom_call" | custom-call | flops 1000000 | bytes 6881292 | tf_op jit(solution)/shard_map/advance_velocity/pallas_call | solution.py:504
  10.8 0.9 pivots.1.inverse
  11.7 0.1 edge_columns.1
  11.8 4.7 %collective-permute-start.2 = (f32[80,128]{1,0:T(8,128)S(1)}, f32[80,128]{1,0:T(8,128)S(1)}, u32[]{:S(2)}, u32[]{:S(2)}) collective-permute-start(f32[80,128]{1,0:T(8,128)S(1)} %get-tuple-element.25), channel_id=1, source_target_pairs={{1,2},{3,4},{5,6},{2,1},{4,3},{6,5},{9,10},{11,12},{13,14},{10,9},... | collective-permute-start | bytes 122888 | tf_op jit(solution)/shard_map/ppermute | solution.py:526
  16.5 0.1 collective-permute-start.3
  16.6 1.6 %collective-permute-done.2.y_second = f32[80,128]{1,0:T(8,128)S(1)} collective-permute-done((f32[80,128]{1,0:T(8,128)S(1)}, f32[80,128]{1,0:T(8,128)S(1)}, u32[]{:S(2)}, u32[]{:S(2)}) %collective-permute-start.2) | collective-permute-done | bytes 40992 | tf_op jit(solution)/shard_map/ppermute | solution.py:526
  18.2 0.0 copy-start.3
  18.2 0.0 copy-start.4
  18.2 0.0 copy-start.8
  18.2 3.4 %advance_stress.1 = (f32[6,16,64,128]{3,2,1,0:T(8,128)}, f32[3,16,64,128]{3,2,1,0:T(8,128)}, f32[16,64,128]{2,1,0:T(8,128)S(1)}) custom-call(f32[3]{0:T(128)S(1)} %copy-done.10, f32[3]{0:T(128)S(1)} %copy-done.14, f32[3]{0:T(128)S(1)} %copy-done.15, f32[3]{0:T(128)S(1)} %copy-done.16, f32[6,16,64,128]{3,2,1,0:T(8,128)S(1)} %copy-done, ...), custom_call_target="tpu_custom_call" | custom-call | flops 1000000 | bytes 10731568 | tf_op jit(solution)/shard_map/advance_stress/pallas_call | solution.py:504
  21.6 20.2 %all_to_all.10 = f32[16,64,128]{2,1,0:T(8,128)S(1)} all-to-all(f32[16,64,128]{2,1,0:T(8,128)S(1)} %get-tuple-element.29), channel_id=1, replica_groups=mesh['gx'=32,'gy'=8] {'gy'}, dimensions={0} | all-to-all | bytes 1048576 | tf_op jit(solution)/shard_map/all_to_all | solution.py:595
  41.8 0.0 copy-start.5
  41.8 0.0 copy-start.6
  41.8 0.0 copy-start.7
  41.9 1.2 %transform_y.1 = f32[2048,128]{1,0:T(8,128)S(1)} custom-call(f32[8,2,64,128]{3,2,1,0:T(8,128)S(1)} %bitcast.5, bf16[256,256]{1,0:T(8,128)(2,1)S(1)} %copy-done.4, bf16[256,256]{1,0:T(8,128)(2,1)S(1)} %copy-done.3, f32[16,128]{1,0:T(8,128)S(1)} %copy-done.8), custom_call_target="tpu_custom_call" | custom-call | flops 1000000 | bytes 2105344 | tf_op jit(solution)/shard_map/transform_y/pallas_call | solution.py:504
  43.1 44.3 %all_to_all.11 = f32[256,8,128]{2,1,0:T(8,128)S(1)} all-to-all(f32[256,8,128]{2,1,0:T(8,128)S(1)} %bitcast.3), channel_id=1, replica_groups=mesh['gx'=32,'gy'=8] {'gx','gy'}, dimensions={0} | all-to-all | bytes 2097152 | tf_op jit(solution)/shard_map/all_to_all | solution.py:605
  87.4 2.5 %solve.1 = f32[2,16,4,2048]{3,2,1,0:T(4,128)} custom-call(s32[16]{0:T(128)S(1)} %copy-done.11, f32[3]{0:T(128)S(1)} %copy-done.12, f32[3]{0:T(128)S(1)} %copy-done.13, f32[32,8,8,128]{3,2,1,0:T(8,128)S(1)} %bitcast.4, bf16[256,256]{1,0:T(8,128)(2,1)S(1)} %copy-done.6, bf16[256,256]{1,0:T(8,128)(2,1)S(1)} %copy-done.5, f32[32,128]{1,0:T(8,128)S(1)} %copy-done.7, ...), custom_call_target="tpu_custom_call" | custom-call | flops 1000000 | bytes 3686488 | tf_op jit(solution)/shard_map/solve/pallas_call | solution.py:504
  (27 shorter events, 0.1 us)
Async XLA Ops:
  0.6 6.9 %copy-start.10 = (f32[3]{0:T(128)S(1)}, f32[3]{0:T(128)}, u32[]{:S(2)}) copy-start(f32[3]{0:T(128)} %buoy.3) | copy-start | bytes 40
  0.6 6.9 %copy-start.2 = (s32[16,64,128]{2,1,0:T(8,128)S(1)}, s32[16,64,128]{2,1,0:T(8,128)}, u32[]{:S(2)}) copy-start(s32[16,64,128]{2,1,0:T(8,128)} %material.3) | copy-start | bytes 1572868
  0.7 6.9 %copy-start = (f32[6,16,64,128]{3,2,1,0:T(8,128)S(1)}, f32[6,16,64,128]{3,2,1,0:T(8,128)}, u32[]{:S(2)}) copy-start(f32[6,16,64,128]{3,2,1,0:T(8,128)} %stress.3) | copy-start | bytes 9437188
  0.7 6.9 %copy-start.1 = (f32[3,16,64,128]{3,2,1,0:T(8,128)S(1)}, f32[3,16,64,128]{3,2,1,0:T(8,128)}, u32[]{:S(2)}) copy-start(f32[3,16,64,128]{3,2,1,0:T(8,128)} %veloc_in.1) | copy-start | bytes 4718596
  1.9 9.8 %collective-permute-start = (f32[6,16,128]{2,1,0:T(8,128)S(1)}, f32[6,16,128]{2,1,0:T(8,128)S(1)}, u32[]{:S(2)}, u32[]{:S(2)}) collective-permute-start(f32[6,16,128]{2,1,0:T(8,128)S(1)} %get-tuple-element.18), channel_id=1, source_target_pairs={{8,16},{24,32},{40,48},{56,64},{72,80},{88,96},{104,112},{120,128}... | collective-permute-start | bytes 147464 | tf_op jit(solution)/shard_map/ppermute | solution.py:526
  2.7 8.1 %copy-start.9 = (f32[1,2048]{1,0:T(1,128)S(1)}, f32[1,2048]{1,0:T(1,128)}, u32[]{:S(2)}) copy-start(f32[1,2048]{1,0:T(1,128)} %constant.14.clone.wave_x) | copy-start | bytes 24580
  2.7 8.1 %copy-start.11 = (s32[16]{0:T(128)S(1)}, s32[16]{0:T(128)}, u32[]{:S(2)}) copy-start(s32[16]{0:T(128)} %layer_kind.2) | copy-start | bytes 196
  2.7 8.1 %copy-start.12 = (f32[3]{0:T(128)S(1)}, f32[3]{0:T(128)}, u32[]{:S(2)}) copy-start(f32[3]{0:T(128)} %lateral.3) | copy-start | bytes 40
  2.7 8.1 %copy-start.13 = (f32[3]{0:T(128)S(1)}, f32[3]{0:T(128)}, u32[]{:S(2)}) copy-start(f32[3]{0:T(128)} %normal.3) | copy-start | bytes 40
  2.7 15.4 %copy-start.14 = (f32[3]{0:T(128)S(1)}, f32[3]{0:T(128)}, u32[]{:S(2)}) copy-start(f32[3]{0:T(128)} %lame.1) | copy-start | bytes 40
  2.8 15.4 %copy-start.15 = (f32[3]{0:T(128)S(1)}, f32[3]{0:T(128)}, u32[]{:S(2)}) copy-start(f32[3]{0:T(128)} %shear.1) | copy-start | bytes 40
  2.8 15.4 %copy-start.16 = (f32[3]{0:T(128)S(1)}, f32[3]{0:T(128)}, u32[]{:S(2)}) copy-start(f32[3]{0:T(128)} %piezo.1) | copy-start | bytes 40
  2.8 8.9 %collective-permute-start.1 = (f32[6,16,128]{2,1,0:T(8,128)S(1)}, f32[6,16,128]{2,1,0:T(8,128)S(1)}, u32[]{:S(2)}, u32[]{:S(2)}) collective-permute-start(f32[6,16,128]{2,1,0:T(8,128)S(1)} %get-tuple-element.19), channel_id=1, source_target_pairs={{0,8},{16,24},{32,40},{48,56},{64,72},{80,88},{96,104},{112,120},{... | collective-permute-start | bytes 147464 | tf_op jit(solution)/shard_map/ppermute | solution.py:527
  11.8 6.3 %collective-permute-start.2 = (f32[80,128]{1,0:T(8,128)S(1)}, f32[80,128]{1,0:T(8,128)S(1)}, u32[]{:S(2)}, u32[]{:S(2)}) collective-permute-start(f32[80,128]{1,0:T(8,128)S(1)} %get-tuple-element.25), channel_id=1, source_target_pairs={{1,2},{3,4},{5,6},{2,1},{4,3},{6,5},{9,10},{11,12},{13,14},{10,9},... | collective-permute-start | bytes 122888 | tf_op jit(solution)/shard_map/ppermute | solution.py:526
  16.5 1.7 %collective-permute-start.3 = (f32[80,128]{1,0:T(8,128)S(1)}, f32[80,128]{1,0:T(8,128)S(1)}, u32[]{:S(2)}, u32[]{:S(2)}) collective-permute-start(f32[80,128]{1,0:T(8,128)S(1)} %get-tuple-element.26), channel_id=1, source_target_pairs={{0,1},{2,3},{4,5},{6,7},{1,0},{3,2},{5,4},{7,6},{8,9},{10,11},{12,... | collective-permute-start | bytes 122888 | tf_op jit(solution)/shard_map/ppermute | solution.py:527
  18.2 23.6 %copy-start.3 = (bf16[256,256]{1,0:T(8,128)(2,1)S(1)}, bf16[256,256]{1,0:T(8,128)(2,1)}, u32[]{:S(2)}) copy-start(bf16[256,256]{1,0:T(8,128)(2,1)} %constant.16.clone.w_low) | copy-start | bytes 393220
  18.2 23.6 %copy-start.4 = (bf16[256,256]{1,0:T(8,128)(2,1)S(1)}, bf16[256,256]{1,0:T(8,128)(2,1)}, u32[]{:S(2)}) copy-start(bf16[256,256]{1,0:T(8,128)(2,1)} %constant.15.clone.w_high) | copy-start | bytes 393220
  18.2 23.6 %copy-start.8 = (f32[16,128]{1,0:T(8,128)S(1)}, f32[16,128]{1,0:T(8,128)}, u32[]{:S(2)}) copy-start(f32[16,128]{1,0:T(8,128)} %constant.17.clone.twiddle) | copy-start | bytes 24580
  41.8 45.6 %copy-start.5 = (bf16[256,256]{1,0:T(8,128)(2,1)S(1)}, bf16[256,256]{1,0:T(8,128)(2,1)}, u32[]{:S(2)}) copy-start(bf16[256,256]{1,0:T(8,128)(2,1)} %constant.19.clone.w_low) | copy-start | bytes 393220
  41.8 45.5 %copy-start.6 = (bf16[256,256]{1,0:T(8,128)(2,1)S(1)}, bf16[256,256]{1,0:T(8,128)(2,1)}, u32[]{:S(2)}) copy-start(bf16[256,256]{1,0:T(8,128)(2,1)} %constant.18.clone.w_high) | copy-start | bytes 393220
  41.8 45.5 %copy-start.7 = (f32[32,128]{1,0:T(8,128)S(1)}, f32[32,128]{1,0:T(8,128)}, u32[]{:S(2)}) copy-start(f32[32,128]{1,0:T(8,128)} %constant.20.clone.twiddle) | copy-start | bytes 49156

commit v5 on v4

--- a/solution.py
+++ b/solution.py
@@ -74,6 +74,11 @@
     return jnp.where(codes == 0, first, jnp.where(codes == 1, second, third))
 
 
+def pick_row(codes, rows_ref, table):
+    first, second, third = (rows_ref[4 * table + m : 4 * table + m + 1, :] for m in range(3))
+    return jnp.where(codes == 0, first, jnp.where(codes == 1, second, third))
+
+
 def lanes(values):
     return lax.broadcasted_iota(jnp.int32, values.shape, values.ndim - 1)
 
@@ -129,9 +134,11 @@
 
 
 def edge_rows(
-    buoy_in, stress_in, veloc_in, material_in, second, first, stress, veloc, material, buoy, sems, buoy_sem
+    buoy_in, lame_in, shear_in, piezo_in, stress_in, veloc_in, material_in, second, first, tables,
+    stress, veloc, material, buoy, lame, shear, piezo, sems, table_sems,
 ):
-    moves = [pltpu.make_async_copy(buoy_in, buoy, buoy_sem)]
+    pairs = [(buoy_in, buoy), (lame_in, lame), (shear_in, shear), (piezo_in, piezo)]
+    moves = [pltpu.make_async_copy(*pair, table_sems.at[n]) for n, pair in enumerate(pairs)]
     for n, row in enumerate((0, BX - 1)):
         at = pl.ds(row, 1)
         moves += [
@@ -156,6 +163,10 @@
     for c in range(6):
         first[c] = jnp.where(is_odd, up[c], down[c])
         second[c] = jnp.where(is_odd, down[c], up[c])
+    tables[...] = jnp.zeros_like(tables)
+    for n, (_, table) in enumerate(pairs):
+        for m in range(3):
+            tables[4 * n + m : 4 * n + m + 1, :] = jnp.full((1, BY), table[m])
 
 
 CHUNK = 2
@@ -172,13 +183,13 @@
     return made
 
 
-def advance_velocity(buoy, stress, veloc, material, new, right_ref, left_ref):
+def advance_velocity(tables, stress, veloc, material, new, right_ref, left_ref):
     column = lax.broadcasted_iota(jnp.int32, (BX, BY), 1)
     right = jnp.zeros((BX, BY), jnp.float32)
     left = jnp.zeros((BX, BY), jnp.float32)
     for z in range(NZ):
         sxx, syy, szz, sxy, sxz, syz = (stress[c, z] for c in range(6))
-        b = pick(material[z], buoy)
+        b = pick_row(material[z], tables, 0)
         dz_sxz = sxz - stress[4, z - 1] if z else sxz
         dz_syz = syz - stress[5, z - 1] if z else syz
         dz_szz = stress[2, z + 1] - szz if z < NZ - 1 else -szz
@@ -234,7 +245,7 @@
 
 
 def advance_stress(
-    buoy, lame, shear, piezo, stress, part, material, x_second, x_first,
+    tables, stress, part, material, x_second, x_first,
     own_right, own_left, y_second, y_first, stress_out, veloc_out, charge,
     new_stress, new_veloc, sems,
 ):
@@ -272,7 +283,7 @@
         return jnp.concatenate([values[: BX - 8], tail], axis=0)
 
     def close_edges(z):
-        b = pick(material[z], buoy)
+        b = pick_row(material[z], tables, 0)
         row = slice(z, z + 1)
         head, tail = b[:8], b[BX - 8 :]
         ux = part[0, z] - jnp.where(lane == 0, b * beside(west, 2 * NZ + z), 0.0)
@@ -291,7 +302,7 @@
         sxx, syy, szz, sxy, sxz, syz = (stress[c, z] for c in range(6))
         ux, uy, uz = (new_veloc[c, z] for c in range(3))
         codes = material[z]
-        lam, mu, e = pick(codes, lame), pick(codes, shear), pick(codes, piezo)
+        lam, mu, e = (pick_row(codes, tables, table) for table in (1, 2, 3))
         row = slice(z, z + 1)
         ex = ux - last_row(ux, ux_low[row] + low[1][row] * sxx[0:1])
         ey = uy - jnp.where(lane == 0, beside(uy_west, z), pltpu.roll(uy, 1, 1))
@@ -415,8 +426,11 @@
     return el, g
 
 
-def pivots(layer_kind, lateral, normal, wave_x, inverse):
+def pivots(layer_kind, lateral, normal, wave_x, inverse, couplings):
     el, g = coupling_scalars(layer_kind, lateral, normal)
+    couplings[...] = jnp.zeros_like(couplings)
+    for z in range(NZ + 1):
+        couplings[z : z + 1, :] = jnp.full((1, 256), g[z])
     first = (lax.axis_index("gx") * DY + lax.axis_index("gy")) * 4
     ky = first + rows(jnp.zeros((8, 128), jnp.float32)) % 4
     wave_y = 2.0 * jnp.sin(math.pi * ky.astype(jnp.float32) / NY)
@@ -437,9 +451,7 @@
 SPAN = 512
 
 
-def solve(
-    layer_kind, lateral, normal, lines, w_high, w_low, twiddle, inverse, modes_out, rhs, out, sems
-):
+def solve(lines, w_high, w_low, twiddle, inverse, couplings, modes_out, rhs, out, sems):
     weights = (w_high[...], w_low[...])
     upper = rows(jnp.zeros((8, 128), jnp.float32)) < 4
     for gy in range(DY):
@@ -456,7 +468,7 @@
             at = slice(128 * k2, 128 * k2 + 128)
             rhs[2 * gy, :, at] = jnp.where(upper, re, pltpu.roll(im, 4, 0))
             rhs[2 * gy + 1, :, at] = jnp.where(upper, pltpu.roll(re, 4, 0), im)
-    _, g = coupling_scalars(layer_kind, lateral, normal)
+    g = [couplings[z : z + 1, :] for z in range(NZ + 1)]
     leaving = []
     for k in range(NX // 256):
         at = slice(256 * k, 256 * k + 256)
@@ -530,23 +542,24 @@
 def per_device(
     stress, velocity, material, layer_kind, buoyancy, lame_first, shear_modulus, piezo, permit_lateral, permit_normal
 ):
-    x_edges = call(
+    *x_edges, tables = call(
         edge_rows,
         "edge_rows",
-        [(6, NZ, BY)] * 2,
-        [ANY] * 4,
+        [(6, NZ, BY)] * 2 + [(16, BY)],
+        [ANY] * 7,
         tuple(
-            pltpu.with_memory_space_constraint(v, pltpu.HBM) for v in (buoyancy, stress, velocity, material)
+            pltpu.with_memory_space_constraint(v, pltpu.HBM)
+            for v in (buoyancy, lame_first, shear_modulus, piezo, stress, velocity, material)
         ),
         [
             pltpu.VMEM((2, 6, NZ, 1, BY), jnp.float32),
             pltpu.VMEM((2, 3, NZ, 1, BY), jnp.float32),
             pltpu.VMEM((2, NZ, 1, BY), jnp.int32),
-            pltpu.SMEM((3,), jnp.float32),
+            *[pltpu.SMEM((3,), jnp.float32)] * 4,
             pltpu.SemaphoreType.DMA((2, 3)),
-            pltpu.SemaphoreType.DMA,
+            pltpu.SemaphoreType.DMA((4,)),
         ],
-        keep=(0, 1),
+        keep=(0, 1, 2),
     )
     x_edges = near(*swaps("gx", *x_edges))
     stress, velocity, material = near(stress, velocity, material)
@@ -554,19 +567,18 @@
         advance_velocity,
         "advance_velocity",
         [(3, NZ, BX, BY), (BX, BY), (BX, BY)],
-        [SMEM] + [VMEM] * 3,
-        (buoyancy, stress, velocity, material),
+        [VMEM] * 4,
+        (tables, stress, velocity, material),
         keep=(0, 1, 2),
     )
-    scalars = (layer_kind, permit_lateral, permit_normal)
     own_right, layer_kind = lax.optimization_barrier((own_right, layer_kind))
-    inverse, = call(
+    inverse, couplings = call(
         pivots,
         "pivots",
-        [(NZ, 8, NX)],
+        [(NZ, 8, NX), (24, 256)],
         [SMEM] * 3 + [VMEM],
         (layer_kind, permit_lateral, permit_normal, jnp.asarray(table_wave())),
-        keep=(0,),
+        keep=(0, 1),
     )
     own_right, inverse = lax.optimization_barrier((own_right, inverse))
     own_right, inverse = near(own_right, inverse)
@@ -583,9 +595,9 @@
         advance_stress,
         "advance_stress",
         [(6, NZ, BX, BY), (3, NZ, BX, BY), (NZ, BX, BY)],
-        [SMEM] * 4 + [VMEM] * 9,
+        [VMEM] * 10,
         (
-            buoyancy, lame_first, shear_modulus, piezo, stress, part, material,
+            tables, stress, part, material,
             *x_edges, own_right, own_left, *y_edges,
         ),
         [field(6), field(3), pltpu.SemaphoreType.DMA((NZ // CHUNK, 2))],
@@ -607,8 +619,8 @@
         solve,
         "solve",
         [(2, NZ, 4, NX)],
-        [SMEM] * 3 + [VMEM] * 5,
-        (*scalars, *near(lines.reshape(DX, DY, 8, 128)), *(jnp.asarray(t) for t in tables_x()), inverse),
+        [VMEM] * 6,
+        (*near(lines.reshape(DX, DY, 8, 128)), *(jnp.asarray(t) for t in tables_x()), inverse, couplings),
         [
             pltpu.VMEM((NZ, 8, NX), jnp.float32),
             pltpu.VMEM((2, NZ, 4, NX), jnp.float32),

time: 90.1 us -> 88.9 us (0.987)
  Pallas kernels: 12.5 us -> 10.9 us
    pallas_call x7, Pallas kernels: 12.5 us -> 10.9 us  [call(): pl.pallas_call(body, name=name, out_shape=shapes, in_specs=in_specs, out_...]
  transfers between devices with their start and end apart: 4 -> 4, of which waited for: 1 -> 1; matrix products, arithmetic and copies ran while one was open for 0% -> 0% of each run, Pallas kernels for 5% -> 4%
where the time goes in v5:
time: 88.9 us; the launch traced here: 88.7 us
  blocking collectives  65 us (73%)
  Pallas kernels  10.9 us (12%)
  starting transfers between devices  10.3 us (12%)
  waiting for transfers between devices  1.58 us (2%)
    all_to_all x1, blocking collectives, per_device(): lax.all_to_all(modes.reshape(DX * DY, 8, 128), ('gx', 'gy'), 0, 0, tiled=...  44.8 us
    all_to_all x1, blocking collectives, per_device(): lax.all_to_all(charge, 'gy', 0, 0, tiled=True).reshape(DY, 2, BX, BY)  20.2 us
    pallas_call x7, Pallas kernels, call(): pl.pallas_call(body, name=name, out_shape=shapes, in_specs=in_specs, out_...  10.9 us
    ppermute x2, starting transfers between devices, swaps(): second = lax.ppermute(second, axis, pairs(1))  5.46 us
    ppermute x2, starting transfers between devices, swaps(): return (second, lax.ppermute(first, axis, pairs(0)))  4.85 us
  transfers between devices with their start and end apart: 4, of which 1 were waited for; matrix products, arithmetic and copies ran while one was open for 0% of the time, Pallas kernels for 4%

profile of v5, /device:TPU:1, one launch (start us, length us, event | category | flops | bytes accessed | tf_op | source)
XLA Modules:
  0.0 88.7 jit_solution(2615122519664319666)
XLA Ops:
  0.7 1.2 %edge_rows.1 = (f32[6,16,128]{2,1,0:T(8,128)S(1)}, f32[6,16,128]{2,1,0:T(8,128)S(1)}, f32[16,128]{1,0:T(8,128)S(1)}) custom-call(f32[3]{0:T(128)} %buoy_in.1, f32[3]{0:T(128)} %lame_in.1, f32[3]{0:T(128)} %shear_in.1, f32[3]{0:T(128)} %piezo_in.1, f32[6,16,64,128]{3,2,1,0:T(8,128)} %stress.3, f32[3,16,64,128]{3,2,1,0:T(8,128)} %veloc.1, s32[16,64,128]{2,1,0:T(8,128)} %material.3), custom_call_target="tpu_custom_call" | custom-call | flops 1000000 | bytes 5349424 | tf_op jit(solution)/shard_map/edge_rows/pallas_call | solution.py:516
  1.9 0.8 collective-permute-start
  2.7 4.8 %collective-permute-start.1 = (f32[6,16,128]{2,1,0:T(8,128)S(1)}, f32[6,16,128]{2,1,0:T(8,128)S(1)}, u32[]{:S(2)}, u32[]{:S(2)}) collective-permute-start(f32[6,16,128]{2,1,0:T(8,128)S(1)} %get-tuple-element.23), channel_id=1, source_target_pairs={{0,8},{16,24},{32,40},{48,56},{64,72},{80,88},{96,104},{112,120},{... | collective-permute-start | bytes 147464 | tf_op jit(solution)/shard_map/ppermute | solution.py:539
  7.5 0.0 copy-done.2
  7.5 0.0 copy-start.10
  7.5 0.0 copy-start.11
  7.5 0.0 copy-start.12
  7.5 2.7 %advance_velocity.1 = (f32[3,16,64,128]{3,2,1,0:T(8,128)S(1)}, f32[64,128]{1,0:T(8,128)S(1)}, f32[64,128]{1,0:T(8,128)S(1)}) custom-call(f32[16,128]{1,0:T(8,128)S(1)} %get-tuple-element.20.tables, f32[6,16,64,128]{3,2,1,0:T(8,128)S(1)} %copy-done, f32[3,16,64,128]{3,2,1,0:T(8,128)S(1)} %copy-done.1, s32[16,64,128]{2,1,0:T(8,128)S(1)} %copy-done.2), custom_call_target="tpu_custom_call" | custom-call | flops 1000000 | bytes 6889472 | tf_op jit(solution)/shard_map/advance_velocity/pallas_call | solution.py:516
  10.2 0.9 %pivots.1 = (f32[16,8,2048]{2,1,0:T(8,128)S(1)}, f32[24,256]{1,0:T(8,128)S(1)}) custom-call(s32[16]{0:T(128)S(1)} %copy-done.10, f32[3]{0:T(128)S(1)} %copy-done.11, f32[3]{0:T(128)S(1)} %copy-done.12, f32[1,2048]{1,0:T(1,128)S(1)} %copy-done.9), custom_call_target="tpu_custom_call" | custom-call | flops 1000000 | bytes 1081432 | tf_op jit(solution)/shard_map/pivots/pallas_call | solution.py:516
  11.2 0.0 collective-permute-done.x_second
  11.2 0.0 collective-permute-done.1.x_first
  11.2 0.1 edge_columns.1
  11.3 4.7 %collective-permute-start.2 = (f32[80,128]{1,0:T(8,128)S(1)}, f32[80,128]{1,0:T(8,128)S(1)}, u32[]{:S(2)}, u32[]{:S(2)}) collective-permute-start(f32[80,128]{1,0:T(8,128)S(1)} %get-tuple-element.30), channel_id=1, source_target_pairs={{1,2},{3,4},{5,6},{2,1},{4,3},{6,5},{9,10},{11,12},{13,14},{10,9},... | collective-permute-start | bytes 122888 | tf_op jit(solution)/shard_map/ppermute | solution.py:538
  16.0 0.1 collective-permute-start.3
  16.1 1.6 %collective-permute-done.2.y_second = f32[80,128]{1,0:T(8,128)S(1)} collective-permute-done((f32[80,128]{1,0:T(8,128)S(1)}, f32[80,128]{1,0:T(8,128)S(1)}, u32[]{:S(2)}, u32[]{:S(2)}) %collective-permute-start.2) | collective-permute-done | bytes 40992 | tf_op jit(solution)/shard_map/ppermute | solution.py:538
  17.6 0.0 collective-permute-done.3.y_first
  17.7 2.8 %advance_stress.1 = (f32[6,16,64,128]{3,2,1,0:T(8,128)}, f32[3,16,64,128]{3,2,1,0:T(8,128)}, f32[16,64,128]{2,1,0:T(8,128)S(1)}) custom-call(f32[16,128]{1,0:T(8,128)S(1)} %get-tuple-element.20.tables, f32[6,16,64,128]{3,2,1,0:T(8,128)S(1)} %copy-done, f32[3,16,64,128]{3,2,1,0:T(8,128)S(1)} %get-tuple-element.21.part, s32[16,64,128]{2,1,0:T(8,128)S(1)} %copy-done.2, ...), custom_call_target="tpu_custom_call" | custom-call | flops 1000000 | bytes 10739712 | tf_op jit(solution)/shard_map/advance_stress/pallas_call | solution.py:516
  20.5 20.2 %all_to_all.10 = f32[16,64,128]{2,1,0:T(8,128)S(1)} all-to-all(f32[16,64,128]{2,1,0:T(8,128)S(1)} %get-tuple-element.34), channel_id=1, replica_groups=mesh['gx'=32,'gy'=8] {'gy'}, dimensions={0} | all-to-all | bytes 1048576 | tf_op jit(solution)/shard_map/all_to_all | solution.py:607
  40.7 0.0 copy-start.5
  40.7 0.0 copy-start.6
  40.7 0.0 copy-start.7
  40.8 1.2 %transform_y.1 = f32[2048,128]{1,0:T(8,128)S(1)} custom-call(f32[8,2,64,128]{3,2,1,0:T(8,128)S(1)} %bitcast.5, bf16[256,256]{1,0:T(8,128)(2,1)S(1)} %copy-done.4, bf16[256,256]{1,0:T(8,128)(2,1)S(1)} %copy-done.3, f32[16,128]{1,0:T(8,128)S(1)} %copy-done.8), custom_call_target="tpu_custom_call" | custom-call | flops 1000000 | bytes 2105344 | tf_op jit(solution)/shard_map/transform_y/pallas_call | solution.py:516
  42.0 44.8 %all_to_all.11 = f32[256,8,128]{2,1,0:T(8,128)S(1)} all-to-all(f32[256,8,128]{2,1,0:T(8,128)S(1)} %bitcast.3), channel_id=1, replica_groups=mesh['gx'=32,'gy'=8] {'gx','gy'}, dimensions={0} | all-to-all | bytes 2097152 | tf_op jit(solution)/shard_map/all_to_all | solution.py:617
  86.8 1.9 %solve.1 = f32[2,16,4,2048]{3,2,1,0:T(4,128)} custom-call(f32[32,8,8,128]{3,2,1,0:T(8,128)S(1)} %bitcast.4, bf16[256,256]{1,0:T(8,128)(2,1)S(1)} %copy-done.6, bf16[256,256]{1,0:T(8,128)(2,1)S(1)} %copy-done.5, f32[32,128]{1,0:T(8,128)S(1)} %copy-done.7, f32[16,8,2048]{2,1,0:T(8,128)S(1)} %get-tuple-element.35.inverse, f32[24,256]{1,0:T(8,128)S(1)} %get-tuple-element.36.couplings), custom_call_target="tpu_custom_call" | custom-call | flops 1000000 | bytes 3710976 | tf_op jit(solution)/shard_map/solve/pallas_call | solution.py:516
  (19 shorter events, 0.0 us)
Async XLA Ops:
  0.6 6.8 %copy-start.2 = (s32[16,64,128]{2,1,0:T(8,128)S(1)}, s32[16,64,128]{2,1,0:T(8,128)}, u32[]{:S(2)}) copy-start(s32[16,64,128]{2,1,0:T(8,128)} %material.3) | copy-start | bytes 1572868
  0.6 6.8 %copy-start = (f32[6,16,64,128]{3,2,1,0:T(8,128)S(1)}, f32[6,16,64,128]{3,2,1,0:T(8,128)}, u32[]{:S(2)}) copy-start(f32[6,16,64,128]{3,2,1,0:T(8,128)} %stress.3) | copy-start | bytes 9437188
  0.7 6.8 %copy-start.1 = (f32[3,16,64,128]{3,2,1,0:T(8,128)S(1)}, f32[3,16,64,128]{3,2,1,0:T(8,128)}, u32[]{:S(2)}) copy-start(f32[3,16,64,128]{3,2,1,0:T(8,128)} %veloc.1) | copy-start | bytes 4718596
  1.9 9.3 %collective-permute-start = (f32[6,16,128]{2,1,0:T(8,128)S(1)}, f32[6,16,128]{2,1,0:T(8,128)S(1)}, u32[]{:S(2)}, u32[]{:S(2)}) collective-permute-start(f32[6,16,128]{2,1,0:T(8,128)S(1)} %get-tuple-element.22), channel_id=1, source_target_pairs={{8,16},{24,32},{40,48},{56,64},{72,80},{88,96},{104,112},{120,128}... | collective-permute-start | bytes 147464 | tf_op jit(solution)/shard_map/ppermute | solution.py:538
  2.7 8.5 %collective-permute-start.1 = (f32[6,16,128]{2,1,0:T(8,128)S(1)}, f32[6,16,128]{2,1,0:T(8,128)S(1)}, u32[]{:S(2)}, u32[]{:S(2)}) collective-permute-start(f32[6,16,128]{2,1,0:T(8,128)S(1)} %get-tuple-element.23), channel_id=1, source_target_pairs={{0,8},{16,24},{32,40},{48,56},{64,72},{80,88},{96,104},{112,120},{... | collective-permute-start | bytes 147464 | tf_op jit(solution)/shard_map/ppermute | solution.py:539
  7.5 2.7 %copy-start.9 = (f32[1,2048]{1,0:T(1,128)S(1)}, f32[1,2048]{1,0:T(1,128)}, u32[]{:S(2)}) copy-start(f32[1,2048]{1,0:T(1,128)} %constant.14.clone.wave_x) | copy-start | bytes 24580
  7.5 2.7 %copy-start.10 = (s32[16]{0:T(128)S(1)}, s32[16]{0:T(128)}, u32[]{:S(2)}) copy-start(s32[16]{0:T(128)} %layer_kind) | copy-start | bytes 196
  7.5 2.7 %copy-start.11 = (f32[3]{0:T(128)S(1)}, f32[3]{0:T(128)}, u32[]{:S(2)}) copy-start(f32[3]{0:T(128)} %lateral.1) | copy-start | bytes 40
  7.5 2.7 %copy-start.12 = (f32[3]{0:T(128)S(1)}, f32[3]{0:T(128)}, u32[]{:S(2)}) copy-start(f32[3]{0:T(128)} %normal.1) | copy-start | bytes 40
  11.3 6.3 %collective-permute-start.2 = (f32[80,128]{1,0:T(8,128)S(1)}, f32[80,128]{1,0:T(8,128)S(1)}, u32[]{:S(2)}, u32[]{:S(2)}) collective-permute-start(f32[80,128]{1,0:T(8,128)S(1)} %get-tuple-element.30), channel_id=1, source_target_pairs={{1,2},{3,4},{5,6},{2,1},{4,3},{6,5},{9,10},{11,12},{13,14},{10,9},... | collective-permute-start | bytes 122888 | tf_op jit(solution)/shard_map/ppermute | solution.py:538
  16.0 1.7 %collective-permute-start.3 = (f32[80,128]{1,0:T(8,128)S(1)}, f32[80,128]{1,0:T(8,128)S(1)}, u32[]{:S(2)}, u32[]{:S(2)}) collective-permute-start(f32[80,128]{1,0:T(8,128)S(1)} %get-tuple-element.31), channel_id=1, source_target_pairs={{0,1},{2,3},{4,5},{6,7},{1,0},{3,2},{5,4},{7,6},{8,9},{10,11},{12,... | collective-permute-start | bytes 122888 | tf_op jit(solution)/shard_map/ppermute | solution.py:539
  17.6 23.1 %copy-start.3 = (bf16[256,256]{1,0:T(8,128)(2,1)S(1)}, bf16[256,256]{1,0:T(8,128)(2,1)}, u32[]{:S(2)}) copy-start(bf16[256,256]{1,0:T(8,128)(2,1)} %constant.16.clone.w_low) | copy-start | bytes 393220
  17.6 23.1 %copy-start.4 = (bf16[256,256]{1,0:T(8,128)(2,1)S(1)}, bf16[256,256]{1,0:T(8,128)(2,1)}, u32[]{:S(2)}) copy-start(bf16[256,256]{1,0:T(8,128)(2,1)} %constant.15.clone.w_high) | copy-start | bytes 393220
  17.7 23.1 %copy-start.8 = (f32[16,128]{1,0:T(8,128)S(1)}, f32[16,128]{1,0:T(8,128)}, u32[]{:S(2)}) copy-start(f32[16,128]{1,0:T(8,128)} %constant.17.clone.twiddle) | copy-start | bytes 24580
  40.7 46.1 %copy-start.5 = (bf16[256,256]{1,0:T(8,128)(2,1)S(1)}, bf16[256,256]{1,0:T(8,128)(2,1)}, u32[]{:S(2)}) copy-start(bf16[256,256]{1,0:T(8,128)(2,1)} %constant.19.clone.w_low) | copy-start | bytes 393220
  40.7 46.1 %copy-start.6 = (bf16[256,256]{1,0:T(8,128)(2,1)S(1)}, bf16[256,256]{1,0:T(8,128)(2,1)}, u32[]{:S(2)}) copy-start(bf16[256,256]{1,0:T(8,128)(2,1)} %constant.18.clone.w_high) | copy-start | bytes 393220
  40.7 46.1 %copy-start.7 = (f32[32,128]{1,0:T(8,128)S(1)}, f32[32,128]{1,0:T(8,128)}, u32[]{:S(2)}) copy-start(f32[32,128]{1,0:T(8,128)} %constant.20.clone.twiddle) | copy-start | bytes 49156

commit v6 on v5

--- a/solution.py
+++ b/solution.py
@@ -246,10 +246,9 @@
 
 def advance_stress(
     tables, stress, part, material, x_second, x_first,
-    own_right, own_left, y_second, y_first, stress_out, veloc_out, charge,
-    new_stress, new_veloc, sems,
+    own_right, own_left, y_second, y_first, stress_out, new_veloc, charge, new_stress, sems,
 ):
-    leaving = copies([(new_stress, stress_out), (new_veloc, veloc_out)], sems)
+    leaving = copies([(new_stress, stress_out)], sems)
     lane = lax.broadcasted_iota(jnp.int32, (BX, BY), 1)
     corner_lane = lane[:NZ]
     row8 = lax.broadcasted_iota(jnp.int32, (8, BY), 0)
@@ -352,7 +351,11 @@
     ]
 
 
-def transform_y(charge, w_high, w_low, twiddle, out, real_lines, imag_lines):
+def transform_y(
+    charge, w_high, w_low, twiddle, veloc, out, veloc_out, real_lines, imag_lines, veloc_sem
+):
+    leaving = pltpu.make_async_copy(veloc, veloc_out, veloc_sem)
+    leaving.start()
     for z in range(2):
         for ihi in range(4):
             at = slice(16 * ihi, 16 * ihi + 16)
@@ -377,6 +380,7 @@
             for part in range(2):
                 start = ahi * 8 + part * 4 + ihi
                 out[pl.ds(start, 128, stride=16), :] = modes[part * 128 : (part + 1) * 128]
+    leaving.wait()
 
 
 def butterfly4(x):
@@ -571,7 +575,15 @@
         (tables, stress, velocity, material),
         keep=(0, 1, 2),
     )
-    own_right, layer_kind = lax.optimization_barrier((own_right, layer_kind))
+    y_edges = call(
+        edge_columns,
+        "edge_columns",
+        [(BX + NZ, BY)] * 2,
+        [VMEM] * 4,
+        (own_right, own_left, *x_edges),
+        keep=(0, 1),
+    )
+    to_swap, layer_kind = lax.optimization_barrier((tuple(y_edges), layer_kind))
     inverse, couplings = call(
         pivots,
         "pivots",
@@ -580,18 +592,10 @@
         (layer_kind, permit_lateral, permit_normal, jnp.asarray(table_wave())),
         keep=(0, 1),
     )
+    y_edges = near(*swaps("gy", *near(*to_swap)))
     own_right, inverse = lax.optimization_barrier((own_right, inverse))
     own_right, inverse = near(own_right, inverse)
-    y_edges = call(
-        edge_columns,
-        "edge_columns",
-        [(BX + NZ, BY)] * 2,
-        [VMEM] * 4,
-        (own_right, own_left, *x_edges),
-        keep=(0, 1),
-    )
-    y_edges = near(*swaps("gy", *y_edges))
-    stress_next, velocity_next, charge = call(
+    stress_next, closed, charge = call(
         advance_stress,
         "advance_stress",
         [(6, NZ, BX, BY), (3, NZ, BX, BY), (NZ, BX, BY)],
@@ -600,18 +604,19 @@
             tables, stress, part, material,
             *x_edges, own_right, own_left, *y_edges,
         ),
-        [field(6), field(3), pltpu.SemaphoreType.DMA((NZ // CHUNK, 2))],
-        [ANY, ANY, VMEM],
-        keep=(2,),
+        [field(6), pltpu.SemaphoreType.DMA((NZ // CHUNK, 1))],
+        [ANY, VMEM, VMEM],
+        keep=(1, 2),
     )
     charge = lax.all_to_all(charge, "gy", 0, 0, tiled=True).reshape(DY, 2, BX, BY)
-    modes, = call(
+    modes, velocity_next = call(
         transform_y,
         "transform_y",
-        [(NY * 2, 128)],
-        [VMEM] * 4,
-        (*near(charge), *(jnp.asarray(t) for t in tables_y())),
-        [pltpu.VMEM((1024, 128), jnp.float32)] * 2,
+        [(NY * 2, 128), (3, NZ, BX, BY)],
+        [VMEM] * 5,
+        (*near(charge), *(jnp.asarray(t) for t in tables_y()), closed),
+        [*[pltpu.VMEM((1024, 128), jnp.float32)] * 2, pltpu.SemaphoreType.DMA],
+        [VMEM, ANY],
         keep=(0,),
     )
     lines = lax.all_to_all(modes.reshape(DX * DY, 8, 128), ("gx", "gy"), 0, 0, tiled=True)

time: 88.9 us -> 88.8 us (level)
  blocking collectives: 65 us -> 66 us
  waiting for transfers between devices: 1.58 us -> 0.6 us
    all_to_all x1, blocking collectives: 44.8 us -> 45.8 us  [per_device(): lax.all_to_all(modes.reshape(DX * DY, 8, 128), ('gx', 'gy'), 0, 0, tiled=...]
    ppermute x2, waiting for transfers between devices: 1.57 us -> 0.59 us  [swaps(): second = lax.ppermute(second, axis, pairs(1))]
where the time goes in v6:
time: 88.8 us; the launch traced here: 88.6 us
  blocking collectives  66 us (74%)
  Pallas kernels  10.7 us (12%)
  starting transfers between devices  10.3 us (12%)
    all_to_all x1, blocking collectives, per_device(): lax.all_to_all(modes.reshape(DX * DY, 8, 128), ('gx', 'gy'), 0, 0, tiled=...  45.8 us
    all_to_all x1, blocking collectives, per_device(): lax.all_to_all(charge, 'gy', 0, 0, tiled=True).reshape(DY, 2, BX, BY)  20.2 us
    pallas_call x7, Pallas kernels, call(): pl.pallas_call(body, name=name, out_shape=shapes, in_specs=in_specs, out_...  10.7 us
    ppermute x2, starting transfers between devices, swaps(): second = lax.ppermute(second, axis, pairs(1))  5.46 us
    ppermute x2, starting transfers between devices, swaps(): return (second, lax.ppermute(first, axis, pairs(0)))  4.85 us
  transfers between devices with their start and end apart: 4, of which 1 were waited for; matrix products, arithmetic and copies ran while one was open for 0% of the time, Pallas kernels for 4%

profile of v6, /device:TPU:1, one launch (start us, length us, event | category | flops | bytes accessed | tf_op | source)
XLA Modules:
  0.0 88.6 jit_solution(14862819305432157711)
XLA Ops:
  0.7 1.2 %edge_rows.1 = (f32[6,16,128]{2,1,0:T(8,128)S(1)}, f32[6,16,128]{2,1,0:T(8,128)S(1)}, f32[16,128]{1,0:T(8,128)S(1)}) custom-call(f32[3]{0:T(128)} %buoy_in.1, f32[3]{0:T(128)} %lame_in.1, f32[3]{0:T(128)} %shear_in.1, f32[3]{0:T(128)} %piezo_in.1, f32[6,16,64,128]{3,2,1,0:T(8,128)} %stress.3, f32[3,16,64,128]{3,2,1,0:T(8,128)} %veloc.1, s32[16,64,128]{2,1,0:T(8,128)} %material.3), custom_call_target="tpu_custom_call" | custom-call | flops 1000000 | bytes 5349424 | tf_op jit(solution)/shard_map/edge_rows/pallas_call | solution.py:520
  1.9 0.8 collective-permute-start
  2.7 4.8 %collective-permute-start.1 = (f32[6,16,128]{2,1,0:T(8,128)S(1)}, f32[6,16,128]{2,1,0:T(8,128)S(1)}, u32[]{:S(2)}, u32[]{:S(2)}) collective-permute-start(f32[6,16,128]{2,1,0:T(8,128)S(1)} %get-tuple-element.26), channel_id=1, source_target_pairs={{0,8},{16,24},{32,40},{48,56},{64,72},{80,88},{96,104},{112,120},{... | collective-permute-start | bytes 147464 | tf_op jit(solution)/shard_map/ppermute | solution.py:543
  7.5 0.0 copy-done
  7.5 0.0 copy-start.10
  7.5 0.0 copy-start.11
  7.5 0.0 copy-start.12
  7.5 2.7 %advance_velocity.1 = (f32[3,16,64,128]{3,2,1,0:T(8,128)S(1)}, f32[64,128]{1,0:T(8,128)S(1)}, f32[64,128]{1,0:T(8,128)S(1)}) custom-call(f32[16,128]{1,0:T(8,128)S(1)} %get-tuple-element.23.tables, f32[6,16,64,128]{3,2,1,0:T(8,128)S(1)} %copy-done, f32[3,16,64,128]{3,2,1,0:T(8,128)S(1)} %copy-done.1, s32[16,64,128]{2,1,0:T(8,128)S(1)} %copy-done.2), custom_call_target="tpu_custom_call" | custom-call | flops 1000000 | bytes 6889472 | tf_op jit(solution)/shard_map/advance_velocity/pallas_call | solution.py:520
  10.2 0.0 collective-permute-done.x_second
  10.2 0.0 collective-permute-done.1.x_first
  10.2 0.1 edge_columns.1
  10.3 4.7 %collective-permute-start.2 = (f32[80,128]{1,0:T(8,128)S(1)}, f32[80,128]{1,0:T(8,128)S(1)}, u32[]{:S(2)}, u32[]{:S(2)}) collective-permute-start(f32[80,128]{1,0:T(8,128)S(1)} %get-tuple-element.34), channel_id=1, source_target_pairs={{1,2},{3,4},{5,6},{2,1},{4,3},{6,5},{9,10},{11,12},{13,14},{10,9},... | collective-permute-start | bytes 122888 | tf_op jit(solution)/shard_map/ppermute | solution.py:542
  15.0 0.1 collective-permute-start.3
  15.1 0.9 %pivots.1 = (f32[16,8,2048]{2,1,0:T(8,128)S(1)}, f32[24,256]{1,0:T(8,128)S(1)}) custom-call(s32[16]{0:T(128)S(1)} %copy-done.10, f32[3]{0:T(128)S(1)} %copy-done.11, f32[3]{0:T(128)S(1)} %copy-done.12, f32[1,2048]{1,0:T(1,128)S(1)} %copy-done.9), custom_call_target="tpu_custom_call" | custom-call | flops 1000000 | bytes 1081432 | tf_op jit(solution)/shard_map/pivots/pallas_call | solution.py:520
  16.1 0.6 collective-permute-done.2.y_second
  16.7 0.0 collective-permute-done.3.y_first
  16.7 2.6 %advance_stress.1 = (f32[6,16,64,128]{3,2,1,0:T(8,128)}, f32[3,16,64,128]{3,2,1,0:T(8,128)S(1)}, f32[16,64,128]{2,1,0:T(8,128)S(1)}) custom-call(f32[16,128]{1,0:T(8,128)S(1)} %get-tuple-element.23.tables, f32[6,16,64,128]{3,2,1,0:T(8,128)S(1)} %copy-done, f32[3,16,64,128]{3,2,1,0:T(8,128)S(1)} %get-tuple-element.24.part, s32[16,64,128]{2,1,0:T(8,128)S(1)} %copy-done.2, ...), custom_call_target="tpu_custom_call" | custom-call | flops 1000000 | bytes 10739712 | tf_op jit(solution)/shard_map/advance_stress/pallas_call | solution.py:520
  19.3 20.2 %all_to_all.10 = f32[16,64,128]{2,1,0:T(8,128)S(1)} all-to-all(f32[16,64,128]{2,1,0:T(8,128)S(1)} %get-tuple-element.37), channel_id=1, replica_groups=mesh['gx'=32,'gy'=8] {'gy'}, dimensions={0} | all-to-all | bytes 1048576 | tf_op jit(solution)/shard_map/all_to_all | solution.py:611
  39.6 1.2 %transform_y.1 = (f32[2048,128]{1,0:T(8,128)S(1)}, f32[3,16,64,128]{3,2,1,0:T(8,128)}) custom-call(f32[8,2,64,128]{3,2,1,0:T(8,128)S(1)} %bitcast.4, bf16[256,256]{1,0:T(8,128)(2,1)S(1)} %copy-done.4, bf16[256,256]{1,0:T(8,128)(2,1)S(1)} %copy-done.3, f32[16,128]{1,0:T(8,128)S(1)} %copy-done.8, f32[3,16,64,128]{3,2,1,0:T(8,128)S(1)} %get-tuple-element.38.veloc), custom_call_target="tpu_custom_call" | custom-call | flops 1000000 | bytes 5251072 | tf_op jit(solution)/shard_map/transform_y/pallas_call | solution.py:520
  40.8 0.0 copy-start.5
  40.8 0.0 copy-start.6
  40.8 0.0 copy-start.7
  40.8 45.8 %all_to_all.11 = f32[256,8,128]{2,1,0:T(8,128)S(1)} all-to-all(f32[256,8,128]{2,1,0:T(8,128)S(1)} %bitcast.5), channel_id=1, replica_groups=mesh['gx'=32,'gy'=8] {'gx','gy'}, dimensions={0} | all-to-all | bytes 2097152 | tf_op jit(solution)/shard_map/all_to_all | solution.py:622
  86.6 1.9 %solve.1 = f32[2,16,4,2048]{3,2,1,0:T(4,128)} custom-call(f32[32,8,8,128]{3,2,1,0:T(8,128)S(1)} %bitcast.3, bf16[256,256]{1,0:T(8,128)(2,1)S(1)} %copy-done.6, bf16[256,256]{1,0:T(8,128)(2,1)S(1)} %copy-done.5, f32[32,128]{1,0:T(8,128)S(1)} %copy-done.7, f32[16,8,2048]{2,1,0:T(8,128)S(1)} %get-tuple-element.41.inverse, f32[24,256]{1,0:T(8,128)S(1)} %get-tuple-element.42.couplings), custom_call_target="tpu_custom_call" | custom-call | flops 1000000 | bytes 3710976 | tf_op jit(solution)/shard_map/solve/pallas_call | solution.py:520
  (19 shorter events, 0.0 us)
Async XLA Ops:
  0.6 6.8 %copy-start.2 = (s32[16,64,128]{2,1,0:T(8,128)S(1)}, s32[16,64,128]{2,1,0:T(8,128)}, u32[]{:S(2)}) copy-start(s32[16,64,128]{2,1,0:T(8,128)} %material.3) | copy-start | bytes 1572868
  0.6 6.8 %copy-start = (f32[6,16,64,128]{3,2,1,0:T(8,128)S(1)}, f32[6,16,64,128]{3,2,1,0:T(8,128)}, u32[]{:S(2)}) copy-start(f32[6,16,64,128]{3,2,1,0:T(8,128)} %stress.3) | copy-start | bytes 9437188
  0.7 6.8 %copy-start.1 = (f32[3,16,64,128]{3,2,1,0:T(8,128)S(1)}, f32[3,16,64,128]{3,2,1,0:T(8,128)}, u32[]{:S(2)}) copy-start(f32[3,16,64,128]{3,2,1,0:T(8,128)} %veloc.1) | copy-start | bytes 4718596
  1.9 8.3 %collective-permute-start = (f32[6,16,128]{2,1,0:T(8,128)S(1)}, f32[6,16,128]{2,1,0:T(8,128)S(1)}, u32[]{:S(2)}, u32[]{:S(2)}) collective-permute-start(f32[6,16,128]{2,1,0:T(8,128)S(1)} %get-tuple-element.25), channel_id=1, source_target_pairs={{8,16},{24,32},{40,48},{56,64},{72,80},{88,96},{104,112},{120,128}... | collective-permute-start | bytes 147464 | tf_op jit(solution)/shard_map/ppermute | solution.py:542
  2.7 7.5 %collective-permute-start.1 = (f32[6,16,128]{2,1,0:T(8,128)S(1)}, f32[6,16,128]{2,1,0:T(8,128)S(1)}, u32[]{:S(2)}, u32[]{:S(2)}) collective-permute-start(f32[6,16,128]{2,1,0:T(8,128)S(1)} %get-tuple-element.26), channel_id=1, source_target_pairs={{0,8},{16,24},{32,40},{48,56},{64,72},{80,88},{96,104},{112,120},{... | collective-permute-start | bytes 147464 | tf_op jit(solution)/shard_map/ppermute | solution.py:543
  7.5 7.6 %copy-start.9 = (f32[1,2048]{1,0:T(1,128)S(1)}, f32[1,2048]{1,0:T(1,128)}, u32[]{:S(2)}) copy-start(f32[1,2048]{1,0:T(1,128)} %constant.14.clone.wave_x) | copy-start | bytes 24580
  7.5 7.6 %copy-start.10 = (s32[16]{0:T(128)S(1)}, s32[16]{0:T(128)}, u32[]{:S(2)}) copy-start(s32[16]{0:T(128)} %layer_kind) | copy-start | bytes 196
  7.5 7.6 %copy-start.11 = (f32[3]{0:T(128)S(1)}, f32[3]{0:T(128)}, u32[]{:S(2)}) copy-start(f32[3]{0:T(128)} %lateral.1) | copy-start | bytes 40
  7.5 7.6 %copy-start.12 = (f32[3]{0:T(128)S(1)}, f32[3]{0:T(128)}, u32[]{:S(2)}) copy-start(f32[3]{0:T(128)} %normal.1) | copy-start | bytes 40
  10.3 6.3 %collective-permute-start.2 = (f32[80,128]{1,0:T(8,128)S(1)}, f32[80,128]{1,0:T(8,128)S(1)}, u32[]{:S(2)}, u32[]{:S(2)}) collective-permute-start(f32[80,128]{1,0:T(8,128)S(1)} %get-tuple-element.34), channel_id=1, source_target_pairs={{1,2},{3,4},{5,6},{2,1},{4,3},{6,5},{9,10},{11,12},{13,14},{10,9},... | collective-permute-start | bytes 122888 | tf_op jit(solution)/shard_map/ppermute | solution.py:542
  15.0 1.7 %collective-permute-start.3 = (f32[80,128]{1,0:T(8,128)S(1)}, f32[80,128]{1,0:T(8,128)S(1)}, u32[]{:S(2)}, u32[]{:S(2)}) collective-permute-start(f32[80,128]{1,0:T(8,128)S(1)} %get-tuple-element.35), channel_id=1, source_target_pairs={{0,1},{2,3},{4,5},{6,7},{1,0},{3,2},{5,4},{7,6},{8,9},{10,11},{12,... | collective-permute-start | bytes 122888 | tf_op jit(solution)/shard_map/ppermute | solution.py:543
  16.7 22.9 %copy-start.3 = (bf16[256,256]{1,0:T(8,128)(2,1)S(1)}, bf16[256,256]{1,0:T(8,128)(2,1)}, u32[]{:S(2)}) copy-start(bf16[256,256]{1,0:T(8,128)(2,1)} %constant.16.clone.w_low) | copy-start | bytes 393220
  16.7 22.9 %copy-start.4 = (bf16[256,256]{1,0:T(8,128)(2,1)S(1)}, bf16[256,256]{1,0:T(8,128)(2,1)}, u32[]{:S(2)}) copy-start(bf16[256,256]{1,0:T(8,128)(2,1)} %constant.15.clone.w_high) | copy-start | bytes 393220
  16.7 22.9 %copy-start.8 = (f32[16,128]{1,0:T(8,128)S(1)}, f32[16,128]{1,0:T(8,128)}, u32[]{:S(2)}) copy-start(f32[16,128]{1,0:T(8,128)} %constant.17.clone.twiddle) | copy-start | bytes 24580
  40.8 45.8 %copy-start.5 = (bf16[256,256]{1,0:T(8,128)(2,1)S(1)}, bf16[256,256]{1,0:T(8,128)(2,1)}, u32[]{:S(2)}) copy-start(bf16[256,256]{1,0:T(8,128)(2,1)} %constant.19.clone.w_low) | copy-start | bytes 393220
  40.8 45.8 %copy-start.6 = (bf16[256,256]{1,0:T(8,128)(2,1)S(1)}, bf16[256,256]{1,0:T(8,128)(2,1)}, u32[]{:S(2)}) copy-start(bf16[256,256]{1,0:T(8,128)(2,1)} %constant.18.clone.w_high) | copy-start | bytes 393220
  40.8 45.8 %copy-start.7 = (f32[32,128]{1,0:T(8,128)S(1)}, f32[32,128]{1,0:T(8,128)}, u32[]{:S(2)}) copy-start(f32[32,128]{1,0:T(8,128)} %constant.20.clone.twiddle) | copy-start | bytes 49156
